TPU v7x, 1024 devices: a whole 4x4x32 slice. The times are simulated.
1024 devices in a mesh: layer: 64 (over z_lo, y), blk: 16 (over z_hi, x, core).
Axes of the slice: x: 4, y: 4, z: 32 (z_hi: 2, z_lo: 16; z = z_hi * 16 + z_lo), core: 2. Of those that a mesh axis runs over, the one named last changes fastest.
Arguments:
- train_in: float32 [64, 32, 64, 512], P('layer', 'blk'), may hold values from -6 to 6
- train_out: float32 [64, 32, 64, 512], P('layer', 'blk'), may hold values from -6 to 6
- query_in: bfloat16 [64, 16, 256, 512], P('layer', 'blk'), may hold values from -6 to 6
- query_out: bfloat16 [64, 16, 256, 512], P('layer', 'blk'), may hold values from -6 to 6
- basis_in: bfloat16 [64, 512, 512], P('layer'), may hold values from -0.25 to 0.25
- basis_out: bfloat16 [64, 512, 512], P('layer'), may hold values from -0.25 to 0.25
- eigen_values: float32 [64, 512, 512], P('layer'), may hold values from 0.05 to 5
- train_ids: int32 [32], P('blk'), may hold values from 0 to 31, each once
- query_ids: int32 [16], P('blk'), may hold values from 0 to 31
Outputs:
- scores: float32 [16, 32], P('blk')
Inputs may be any that keep to these rules, and one draw needn't show every extreme that they name: `train_ids`: every training sequence index appears exactly once.
All inputs are finite; a program needn't handle non-finite values.
Results may differ from a plain program's by a relative error of at most 0.006.
Values may be sent and summed in bfloat16 or wider, within the bound.
No kernel may reach another device: no remote copies, remote signals or barrier semaphores. Data moves between devices by JAX's collectives and lax.ppermute only.
A program may use at most 32 MiB of HBM per device.

v0:
```python
import math

import jax
import jax.numpy as jnp
from jax import lax
from jax.sharding import PartitionSpec as P

damping = 0.1


def project(token_rows, eigen_basis):
    return jnp.einsum(
        "stk,ki->sti", token_rows, eigen_basis, preferred_element_type=jnp.float32
    ).astype(jnp.bfloat16)


def token_scores(out_side, in_side, weights):
    weighted = jnp.einsum("sto,qoi->qsti", out_side, weights, preferred_element_type=jnp.float32)
    return jnp.sum(weighted * in_side[None], axis=(2, 3))


def local(
    train_in,
    train_out,
    query_in,
    query_out,
    basis_in,
    basis_out,
    eigen_values,
    train_ids,
    query_ids,
):
    in_basis = basis_in[0]
    out_basis = basis_out[0]
    query_side_in = project(query_in[0], in_basis)
    query_side_out = project(query_out[0], out_basis)
    moment = jnp.einsum(
        "qto,qti->qoi", query_side_out, query_side_in, preferred_element_type=jnp.float32
    )
    query_len = query_in.shape[2]
    precond = (moment / (query_len * (eigen_values[0] + damping))).astype(jnp.bfloat16)
    local_in = train_in[0].astype(jnp.bfloat16)
    local_out = train_out[0].astype(jnp.bfloat16)
    seq_total = train_ids.shape[0] * lax.axis_size("blk")
    columns = jnp.arange(seq_total, dtype=jnp.int32)
    arrived_in = project(lax.all_gather(local_in, "blk", axis=0, tiled=True), in_basis)
    arrived_out = project(lax.all_gather(local_out, "blk", axis=0, tiled=True), out_basis)
    one_hot = (
        lax.all_gather(train_ids, "blk", axis=0, tiled=True)[:, None] == columns[None, :]
    ).astype(jnp.float32)
    partial_value = jnp.dot(
        token_scores(arrived_out, arrived_in, precond),
        one_hot,
        precision=lax.Precision.HIGHEST,
        preferred_element_type=jnp.float32,
    )
    summed = lax.psum(partial_value, "layer")
    factor = 1.0 / math.sqrt(lax.axis_size("layer") * in_basis.shape[0] * out_basis.shape[0])
    scores = summed * factor
    return jnp.where(query_ids[:, None] == columns[None, :], 0.0, scores)


def solution(mesh):
    placed = (
        P("layer", "blk", None, None),
        P("layer", "blk", None, None),
        P("layer", "blk", None, None),
        P("layer", "blk", None, None),
        P("layer", None, None),
        P("layer", None, None),
        P("layer", None, None),
        P("blk"),
        P("blk"),
    )
    return jax.shard_map(
        local, mesh=mesh, in_specs=placed, out_specs=P("blk", None), check_vma=False
    )
```

profile of v0, /device:TPU:2, one launch (start us, length us, event | category | flops | bytes accessed | tf_op | source)
XLA Modules:
  0.0 697.8 jit_solution(9300830256777405586)
XLA Ops:
  6.5 0.0 copy-start
  6.5 0.0 copy-start.3
  6.5 0.0 copy-start.2
  6.5 0.0 copy-start.1
  6.5 0.0 all-gather.7.cloned.1.call-start
  6.6 1.8 bitcast_convert_fusion
  8.3 0.0 all-gather.7.cloned.1.call-update
  8.4 0.0 all-gather.5.cloned.1.call-start
  8.4 1.6 bitcast_convert_fusion.1
  10.0 0.0 all-gather.5.cloned.1.call-update
  10.7 1.3 dynamic-slice
  12.7 0.9 dynamic-update-slice
  13.5 36.6 %all-reduce = s32[32]{0:T(128)S(1)} all-reduce(s32[32]{0:T(128)S(1)} %dynamic-update-slice), channel_id=1, replica_groups=mesh['layer'=64,'blk'=16] {'blk'}, use_global_device_ids=true, to_apply=%add | all-reduce | flops 32 | bytes 256
  50.2 0.0 copy-done
  50.2 1.2 convolution_convert_fusion
  51.4 0.0 copy-done.3
  51.4 0.0 copy-done.2
  51.4 0.0 copy-done.1
  51.4 0.6 fusion.11
  52.1 117.8 %all-gather.7.cloned.1.call-done = bf16[1,32,64,512]{3,2,0,1:T(8,128)(2,1)} async-done(((bf16[1,2,64,512]{3,2,0,1:T(8,128)(2,1)}), bf16[1,32,64,512]{3,2,0,1:T(8,128)(2,1)}) %all-gather.7.cloned.1.call-update) | async-done | bytes 2097168 | tf_op jit(solution)/shard_map/all_gather | solution.py:46
  169.8 4.2 fusion.1
  174.0 131.8 %all-gather.5.cloned.1.call-done = bf16[1,32,64,512]{3,2,0,1:T(8,128)(2,1)} async-done(((bf16[1,2,64,512]{3,2,0,1:T(8,128)(2,1)}), bf16[1,32,64,512]{3,2,0,1:T(8,128)(2,1)}) %all-gather.5.cloned.1.call-update) | async-done | bytes 2097168 | tf_op jit(solution)/shard_map/all_gather | solution.py:47
  305.8 4.7 fusion
  310.5 0.2 fusion.21
  310.7 379.8 %psum.7 = f32[1,32]{1,0:T(1,128)S(1)} all-reduce(f32[1,32]{1,0:T(1,128)S(1)} %fusion.21), channel_id=1, replica_groups=mesh['layer'=64,'blk'=16] {'layer'}, use_global_device_ids=true, to_apply=%region_1.0 | all-reduce | flops 32 | bytes 256 | tf_op jit(solution)/shard_map/psum | solution.py:57
  690.5 0.5 compare_select_fusion
  (1 shorter events, 0.0 us)
Async XLA Ops:
  6.5 43.6 %copy-start = (bf16[1,512,512]{2,1,0:T(8,128)(2,1)S(1)}, bf16[1,512,512]{2,1,0:T(8,128)(2,1)}, u32[]{:S(2)}) copy-start(bf16[1,512,512]{2,1,0:T(8,128)(2,1)} %param.13) | copy-start | bytes 1572868
  6.5 44.9 %copy-start.3 = (bf16[1,1,256,512]{3,2,1,0:T(8,128)(2,1)S(1)}, bf16[1,1,256,512]{3,2,1,0:T(8,128)(2,1)}, u32[]{:S(2)}) copy-start(bf16[1,1,256,512]{3,2,1,0:T(8,128)(2,1)} %param.12) | copy-start | bytes 786436
  6.5 44.9 %copy-start.2 = (bf16[1,512,512]{2,1,0:T(8,128)(2,1)S(1)}, bf16[1,512,512]{2,1,0:T(8,128)(2,1)}, u32[]{:S(2)}) copy-start(bf16[1,512,512]{2,1,0:T(8,128)(2,1)} %param.14) | copy-start | bytes 1572868
  6.5 44.9 %copy-start.1 = (f32[1,512,512]{2,1,0:T(8,128)S(1)}, f32[1,512,512]{2,1,0:T(8,128)}, u32[]{:S(2)}) copy-start(f32[1,512,512]{2,1,0:T(8,128)} %param.15) | copy-start | bytes 3145732
  6.5 163.3 %all-gather.7.cloned.1.call-start = ((), (), s32[]{:S(2)}) async-start(), calls=%async_computation.1 | async-start | bytes 2228224 | tf_op jit(solution)/shard_map/all_gather | solution.py:46
  8.4 297.4 %all-gather.5.cloned.1.call-start = ((), (), s32[]{:S(2)}) async-start(), calls=%async_computation | async-start | bytes 2228224 | tf_op jit(solution)/shard_map/all_gather | solution.py:47
Sparse Core Ops, SparseCore 0:
  11.9 157.9 all-gather.6
  174.3 131.4 all-gather.4
where the time goes:
time: 698 us
  blocking collectives  416 us (60%)
  waiting for transfers between devices  250 us (36%)
  between operations  14.8 us (2%)
  matrix products  10.9 us (2%)
    psum x1, blocking collectives, local(): summed = lax.psum(partial_value, 'layer')  380 us
    all_gather x1, waiting for transfers between devices, local(): lax.all_gather(local_out, 'blk', axis=0, tiled=True)  132 us
    all_gather x1, waiting for transfers between devices, local(): lax.all_gather(local_in, 'blk', axis=0, tiled=True)  118 us
    unnamed x1, blocking collectives  36.6 us
  transfers between devices with their start and end apart: 2, of which 2 were waited for; matrix products, arithmetic and copies ran while one was open for 1% of the time, Pallas kernels for 0%

commit v1 on v0

v1 whole, which is shorter than its diff:
```python
import math

import jax
import jax.numpy as jnp
from jax import lax
from jax.experimental import pallas as pl
from jax.experimental.pallas import tpu as pltpu
from jax.sharding import Mesh
from jax.sharding import PartitionSpec as P

damping = 0.1

ZLO, Y, ZHI, X, CORE = 16, 4, 2, 4, 2
NAMES = ("zlo", "y", "zhi", "x", "core")


def project(rows, basis):
    return jnp.dot(rows, basis, preferred_element_type=jnp.float32).astype(jnp.bfloat16)


def side_sums(tokens_ref, precond_refs, seqs, length):
    inside = tokens_ref[0].astype(jnp.float32)
    outside = tokens_ref[1]
    rows = []
    for ref in precond_refs:
        weighted = jnp.dot(outside, ref[...], preferred_element_type=jnp.float32)
        prod = weighted * inside
        rows.append(
            jnp.concatenate(
                [
                    jnp.sum(
                        jnp.sum(prod[s * length : (s + 1) * length], axis=0, keepdims=True),
                        axis=1,
                        keepdims=True,
                    )
                    for s in range(seqs)
                ],
                axis=1,
            )
        )
    return jnp.concatenate(rows, axis=0)


def place(sums, hot):
    total = sums[:, 0:1] * hot[0:1, :]
    for s in range(1, hot.shape[0]):
        total = total + sums[:, s : s + 1] * hot[s : s + 1, :]
    return total


def score_kernel(tokens_ref, hot_ref, *refs, length):
    out_ref = refs[-1]
    hot = hot_ref[...]
    out_ref[...] = place(side_sums(tokens_ref, refs[:-1], hot.shape[0], length), hot)


def scores_of(tokens, hot, preconds, length):
    vmem = pl.BlockSpec(memory_space=pltpu.VMEM)
    return pl.pallas_call(
        lambda *refs: score_kernel(*refs, length=length),
        out_shape=jax.ShapeDtypeStruct((len(preconds), hot.shape[1]), jnp.float32),
        in_specs=[vmem] * (2 + len(preconds)),
        out_specs=vmem,
        compiler_params=pltpu.CompilerParams(vmem_limit_bytes=40 << 20),
    )(tokens, hot, *preconds)


def gather_preconds(
    query_in, query_out, in_basis, out_basis, eigen_values, mine, hot, train_ids, length
):
    their_ids = lax.ppermute(train_ids, "zhi", [(0, 1), (1, 0)])
    side_in = project(query_in, in_basis)
    side_out = project(query_out, out_basis)
    moment = lax.dot_general(
        side_out, side_in, (((0,), (0,)), ((), ())), preferred_element_type=jnp.float32
    )
    scale = query_in.shape[0] * (eigen_values + damping)
    precond = (moment / scale).astype(jnp.bfloat16)
    along = [precond]
    for step in range(1, X):
        along.append(lax.ppermute(precond, "x", [(i, i ^ step) for i in range(X)]))
    beside = [lax.ppermute(p, "core", [(0, 1), (1, 0)]) for p in along]
    preconds = along + beside
    return preconds, scores_of(mine, hot, preconds, length), their_ids


def local(
    train_in,
    train_out,
    query_in,
    query_out,
    basis_in,
    basis_out,
    eigen_values,
    train_ids,
    query_ids,
):
    in_basis = basis_in[0]
    out_basis = basis_out[0]
    seqs, length, width = train_in.shape[1:]
    across = [(0, 1), (1, 0)]

    mine = jnp.stack(
        [
            project(train_in[0].astype(jnp.bfloat16).reshape(seqs * length, width), in_basis),
            project(train_out[0].astype(jnp.bfloat16).reshape(seqs * length, width), out_basis),
        ]
    )
    theirs = lax.ppermute(mine, "zhi", across)
    columns = jnp.arange(seqs * ZHI * X * CORE, dtype=jnp.int32)
    hot_mine = (train_ids[:, None] == columns[None, :]).astype(jnp.float32)
    preconds, partial_mine, their_ids = lax.cond(
        lax.axis_index("x") < X,
        lambda *ops: gather_preconds(*ops, length),
        lambda *ops: (
            [jnp.zeros((width, width), jnp.bfloat16)] * (X * CORE),
            jnp.zeros((X * CORE, columns.shape[0]), jnp.float32),
            train_ids,
        ),
        query_in[0, 0], query_out[0, 0], in_basis, out_basis, eigen_values[0], mine, hot_mine,
        train_ids,
    )
    hot_theirs = (their_ids[:, None] == columns[None, :]).astype(jnp.float32)
    partial_theirs = scores_of(theirs, hot_theirs, preconds, length)
    partial_value = partial_mine + partial_theirs

    k = jnp.arange(X * CORE, dtype=jnp.int32)
    owner = (lax.axis_index("x") ^ (k % X)) * CORE + (lax.axis_index("core") ^ (k // X))
    order = owner[None, :] == k[:, None]
    ordered = jnp.sum(
        jnp.where(order[:, :, None], partial_value[None, :, :], 0.0), axis=1
    )
    spread = jnp.broadcast_to(ordered[None], (Y,) + ordered.shape).reshape(Y * X * CORE, -1)
    near = jnp.sum(lax.all_to_all(spread, ("y", "x", "core"), 0, 0), axis=0)
    far = jnp.broadcast_to(near[None], (ZLO,) + near.shape)
    summed = jnp.sum(lax.all_to_all(far, "zlo", 0, 0), axis=0)
    factor = 1.0 / math.sqrt(ZLO * Y * in_basis.shape[0] * out_basis.shape[0])
    scores = (summed * factor)[None, :]
    return jnp.where(query_ids[:, None] == columns[None, :], 0.0, scores)


def solution(mesh):
    split = Mesh(mesh.devices.reshape(ZLO, Y, ZHI, X, CORE), NAMES)
    layer, blk = ("zlo", "y"), ("zhi", "x", "core")
    placed = (
        P(layer, blk, None, None),
        P(layer, blk, None, None),
        P(layer, blk, None, None),
        P(layer, blk, None, None),
        P(layer, None, None),
        P(layer, None, None),
        P(layer, None, None),
        P(blk),
        P(blk),
    )
    return jax.shard_map(
        local, mesh=split, in_specs=placed, out_specs=P(blk, None), check_vma=False
    )
```

time: 698 us -> 195 us (0.28)
  the two profiles are of different devices: /device:TPU:2 before, /device:TPU:1 now
where the time goes in v1:
time: 195 us
  starting transfers between devices  142 us (73%)
  waiting for transfers between devices  24.8 us (13%)
  blocking collectives  13.4 us (7%)
  Pallas kernels  6.01 us (3%)
  local copies, waits for them, and re-layouts  3.1 us (2%)
  matrix products  2.17 us (1%)
    all_to_all x1, starting transfers between devices, local(): summed = jnp.sum(lax.all_to_all(far, 'zlo', 0, 0), axis=0)  52.9 us
    ppermute x4, starting transfers between devices, gather_preconds(): beside = [lax.ppermute(p, 'core', [(0, 1), (1, 0)]) for p in along]  28.9 us
    ppermute x1, starting transfers between devices, gather_preconds(): their_ids = lax.ppermute(train_ids, 'zhi', [(0, 1), (1, 0)])  28.7 us
    ppermute x1, starting transfers between devices, local(): theirs = lax.ppermute(mine, 'zhi', across)  21.7 us
    all_to_all x1, waiting for transfers between devices, local(): summed = jnp.sum(lax.all_to_all(far, 'zlo', 0, 0), axis=0)  18.1 us
    all_to_all x1, blocking collectives, local(): near = jnp.sum(lax.all_to_all(spread, ('y', 'x', 'core'), 0, 0), axis=0)  13.4 us
    ppermute x3, starting transfers between devices, gather_preconds(): along.append(lax.ppermute(precond, 'x', [(i, i ^ step) for i in range(X)]))  10.2 us
    pallas_call x2, Pallas kernels, scores_of(): pl.pallas_call(lambda *refs: score_kernel(*refs, length=length), out_shap...  6.01 us
  transfers between devices with their start and end apart: 10, of which 3 were waited for; matrix products, arithmetic and copies ran while one was open for 0% of the time, Pallas kernels for 0%

profile of v1, /device:TPU:1, one launch (start us, length us, event | category | flops | bytes accessed | tf_op | source)
XLA Modules:
  0.0 194.8 jit_solution(1422170075504740792)
XLA Ops:
  0.0 0.0 copy-start.2
  0.0 0.0 copy-start
  0.0 0.7 copy.36
  0.7 0.1 compare_convert_fusion.1
  0.8 1.0 convert_element_type.39
  1.8 0.0 copy-done.2
  1.8 0.0 copy-start.1
  1.8 0.0 copy-done
  1.8 0.0 copy-start.4
  1.9 0.2 fusion.4
  2.1 0.7 copy-done.1
  2.8 0.2 fusion.5
  3.1 0.0 copy-start.3
  3.1 0.0 copy-start.5
  3.1 0.1 copy-done.4
  3.2 0.9 copy-done.3
  4.1 0.1 copy-done.5
  4.1 73.6 %conditional.1 = (bf16[512,512]{1,0:T(8,128)(2,1)}, bf16[512,512]{1,0:T(8,128)(2,1)}, bf16[512,512]{1,0:T(8,128)(2,1)}, bf16[512,512]{1,0:T(8,128)(2,1)}, bf16[5...) conditional(s32[]{:T(128)} %convert_element_type.38, ...), branch_computations={%region_0.0_spmd, %region_1.0_spmd} | conditional | flops 403963904 | bytes 18350528 | solution.py:112
  4.1 0.3 convolution_convert_fusion
  4.4 1.4 fusion.refs_2_
  5.9 3.9 %collective-permute-start = (bf16[512,512]{1,0:T(8,128)(2,1)}, bf16[512,512]{1,0:T(8,128)(2,1)}, u32[]{:S(2)}, u32[]{:S(2)}) collective-permute-start(bf16[512,512]{1,0:T(8,128)(2,1)} %fusion.refs_2_), channel_id=1, source_target_pairs={{0,2},{2,0},{4,6},{6,4},{1,3},{3,1},{5,7},{7,5},{8,10},{10,8},{12,... | collective-permute-start | bytes 1572872 | tf_op jit(solution)/shard_map/cond/branch_1_fun/ppermute | solution.py:81
  9.8 4.4 %collective-permute-start.1 = (bf16[512,512]{1,0:T(8,128)(2,1)}, bf16[512,512]{1,0:T(8,128)(2,1)}, u32[]{:S(2)}, u32[]{:S(2)}) collective-permute-start(bf16[512,512]{1,0:T(8,128)(2,1)} %fusion.refs_2_), channel_id=1, source_target_pairs={{0,4},{2,6},{4,0},{6,2},{1,5},{3,7},{5,1},{7,3},{8,12},{10,14},{12... | collective-permute-start | bytes 1572872 | tf_op jit(solution)/shard_map/cond/branch_1_fun/ppermute | solution.py:81
  14.2 1.9 collective-permute-start.2
  16.1 16.3 %collective-permute-start.3 = (bf16[512,512]{1,0:T(8,128)(2,1)}, bf16[512,512]{1,0:T(8,128)(2,1)}, u32[]{:S(2)}, u32[]{:S(2)}) collective-permute-start(bf16[512,512]{1,0:T(8,128)(2,1)} %fusion.refs_2_), channel_id=1, source_target_pairs={{0,1},{1,0},{2,3},{3,2},{4,5},{5,4},{6,7},{7,6},{8,9},{9,8},{10,11... | collective-permute-start | bytes 1572872 | tf_op jit(solution)/shard_map/cond/branch_1_fun/ppermute | solution.py:82
  32.4 0.0 collective-permute-done.refs_3_
  32.4 1.9 collective-permute-start.4
  34.3 0.0 collective-permute-done.1.refs_4_
  34.3 4.3 %collective-permute-start.5 = (bf16[512,512]{1,0:T(8,128)(2,1)}, bf16[512,512]{1,0:T(8,128)(2,1)}, u32[]{:S(2)}, u32[]{:S(2)}) collective-permute-start(bf16[512,512]{1,0:T(8,128)(2,1)} %collective-permute-done.1.refs_4_), channel_id=1, source_target_pairs={{0,1},{1,0},{2,3},{3,2},{4,5},{5,4},{6,7},{7,6},{8,9},{9,8},{10,11... | collective-permute-start | bytes 1572872 | tf_op jit(solution)/shard_map/cond/branch_1_fun/ppermute | solution.py:82
  38.7 0.0 collective-permute-done.2.refs_5_
  38.7 6.4 %collective-permute-start.6 = (bf16[512,512]{1,0:T(8,128)(2,1)}, bf16[512,512]{1,0:T(8,128)(2,1)}, u32[]{:S(2)}, u32[]{:S(2)}) collective-permute-start(bf16[512,512]{1,0:T(8,128)(2,1)} %collective-permute-done.2.refs_5_), channel_id=1, source_target_pairs={{0,1},{1,0},{2,3},{3,2},{4,5},{5,4},{6,7},{7,6},{8,9},{9,8},{10,11... | collective-permute-start | bytes 1572872 | tf_op jit(solution)/shard_map/cond/branch_1_fun/ppermute | solution.py:82
  45.1 28.7 %collective-permute-start.7 = (s32[2]{0:T(128)S(1)}, s32[2]{0:T(128)S(1)}, u32[]{:S(2)}, u32[]{:S(2)}) collective-permute-start(s32[2]{0:T(128)S(1)} %get-tuple-element.29), channel_id=1, source_target_pairs={{0,8},{8,0},{1,9},{9,1},{2,10},{10,2},{3,11},{11,3},{4,12},{12,4},... | collective-permute-start | bytes 32 | tf_op jit(solution)/shard_map/cond/branch_1_fun/ppermute | solution.py:71
  73.8 0.9 collective-permute-done.7
  74.7 0.0 collective-permute-done.3.refs_6_
  74.7 0.0 collective-permute-done.4.refs_7_
  74.7 0.0 collective-permute-done.5.refs_8_
  74.7 0.0 collective-permute-done.6.refs_9_
  74.7 3.0 %branch_1_fun.1 = f32[8,32]{1,0:T(8,128)S(1)} custom-call(bf16[2,128,512]{2,1,0:T(8,128)(2,1)S(1)} %get-tuple-element.27.refs_0_, f32[2,32]{1,0:T(2,128)S(1)} %get-tuple-element.28.refs_1_, bf16[512,512]{1,0:T(8,128)(2,1)} %fusion.refs_2_, bf16[512,512]{1,0:T(8,128)(2,1)} %collective-permute-done.refs_3_, bf16[512,512]{1,0:T(8,128)(2,1)} %collective-permute-done.1.refs_4_, ...), custom_call_target="tpu_custom_call" | custom-call | tf_op jit(solution)/shard_map/cond/branch_1_fun/pallas_call | solution.py:59
  77.7 21.7 %collective-permute-start.8 = (bf16[2,128,512]{2,1,0:T(8,128)(2,1)S(1)}, bf16[2,128,512]{2,1,0:T(8,128)(2,1)S(1)}, u32[]{:S(2)}, u32[]{:S(2)}) collective-permute-start(bf16[2,128,512]{2,1,0:T(8,128)(2,1)S(1)} %pad_maximum_fusion), channel_id=1, source_target_pairs={{0,8},{8,0},{1,9},{9,1},{2,10},{10,2},{3,11},{11,3},{4,12},{12,4},... | collective-permute-start | bytes 786440 | tf_op jit(solution)/shard_map/ppermute | solution.py:109
  99.5 0.1 compare_convert_fusion.refs_1_
  99.5 5.8 %collective-permute-done.8.refs_0_ = bf16[2,128,512]{2,1,0:T(8,128)(2,1)S(1)} collective-permute-done((bf16[2,128,512]{2,1,0:T(8,128)(2,1)S(1)}, bf16[2,128,512]{2,1,0:T(8,128)(2,1)S(1)}, u32[]{:S(2)}, u32[]{:S(2)}) %collective-permute-start.8) | collective-permute-done | bytes 262176 | tf_op jit(solution)/shard_map/ppermute | solution.py:109
  105.3 3.0 %shard_map.97 = f32[8,32]{1,0:T(8,128)S(1)} custom-call(bf16[2,128,512]{2,1,0:T(8,128)(2,1)S(1)} %collective-permute-done.8.refs_0_, f32[2,32]{1,0:T(2,128)S(1)} %compare_convert_fusion.refs_1_, bf16[512,512]{1,0:T(8,128)(2,1)} %get-tuple-element.42.refs_2_, bf16[512,512]{1,0:T(8,128)(2,1)} %get-tuple-element.43.refs_3_, ...), custom_call_target="tpu_custom_call" | custom-call | tf_op jit(solution)/shard_map/pallas_call | solution.py:59
  108.3 0.1 select_reduce_fusion
  108.5 13.4 %all_to_all.15 = f32[32,1,32]{2,1,0:T(1,128)S(1)} all-to-all(f32[32,1,32]{2,1,0:T(1,128)S(1)} %bitcast.36), channel_id=1, replica_groups=mesh['zlo'=16,'y'=4,'zhi'=2,'x'=4,'core'=2] {'y','x','core'}, dimensions={0} | all-to-all | bytes 8192 | tf_op jit(solution)/shard_map/all_to_all | solution.py:134
  121.9 0.1 reduce_sum.28
  121.9 0.6 broadcast_in_dim.32
  122.5 52.9 %all-to-all-start.1 = ((f32[16,1,32]{2,1,0:T(1,128)}), f32[16,1,32]{2,1,0:T(1,128)S(1)}, u32[]{:S(2)}, u32[]{:S(2)}) async-start(f32[16,1,32]{2,1,0:T(1,128)} %broadcast_in_dim.32), calls=%async_computation.1 | async-start | bytes 16384 | tf_op jit(solution)/shard_map/all_to_all | solution.py:136
  176.1 18.1 %all-to-all-done.1 = f32[16,1,32]{2,1,0:T(1,128)S(1)} async-done(((f32[16,1,32]{2,1,0:T(1,128)}), f32[16,1,32]{2,1,0:T(1,128)S(1)}, u32[]{:S(2)}, u32[]{:S(2)}) %all-to-all-start.1) | async-done | bytes 2080 | tf_op jit(solution)/shard_map/all_to_all | solution.py:136
  194.3 0.5 compare_select_fusion
  (8 shorter events, 0.1 us)
Async XLA Ops:
  0.0 1.8 copy-start.2
  0.0 1.8 copy-start
  1.8 1.0 copy-start.1
  1.8 1.4 copy-start.4
  3.1 1.0 copy-start.3
  3.1 1.0 copy-start.5
  5.9 26.5 %collective-permute-start = (bf16[512,512]{1,0:T(8,128)(2,1)}, bf16[512,512]{1,0:T(8,128)(2,1)}, u32[]{:S(2)}, u32[]{:S(2)}) collective-permute-start(bf16[512,512]{1,0:T(8,128)(2,1)} %fusion.refs_2_), channel_id=1, source_target_pairs={{0,2},{2,0},{4,6},{6,4},{1,3},{3,1},{5,7},{7,5},{8,10},{10,8},{12,... | collective-permute-start | bytes 1572872 | tf_op jit(solution)/shard_map/cond/branch_1_fun/ppermute | solution.py:81
  9.8 24.5 %collective-permute-start.1 = (bf16[512,512]{1,0:T(8,128)(2,1)}, bf16[512,512]{1,0:T(8,128)(2,1)}, u32[]{:S(2)}, u32[]{:S(2)}) collective-permute-start(bf16[512,512]{1,0:T(8,128)(2,1)} %fusion.refs_2_), channel_id=1, source_target_pairs={{0,4},{2,6},{4,0},{6,2},{1,5},{3,7},{5,1},{7,3},{8,12},{10,14},{12... | collective-permute-start | bytes 1572872 | tf_op jit(solution)/shard_map/cond/branch_1_fun/ppermute | solution.py:81
  14.2 24.5 %collective-permute-start.2 = (bf16[512,512]{1,0:T(8,128)(2,1)}, bf16[512,512]{1,0:T(8,128)(2,1)}, u32[]{:S(2)}, u32[]{:S(2)}) collective-permute-start(bf16[512,512]{1,0:T(8,128)(2,1)} %fusion.refs_2_), channel_id=1, source_target_pairs={{0,6},{2,4},{4,2},{6,0},{1,7},{3,5},{5,3},{7,1},{8,14},{10,12},{12... | collective-permute-start | bytes 1572872 | tf_op jit(solution)/shard_map/cond/branch_1_fun/ppermute | solution.py:81
  16.1 58.6 %collective-permute-start.3 = (bf16[512,512]{1,0:T(8,128)(2,1)}, bf16[512,512]{1,0:T(8,128)(2,1)}, u32[]{:S(2)}, u32[]{:S(2)}) collective-permute-start(bf16[512,512]{1,0:T(8,128)(2,1)} %fusion.refs_2_), channel_id=1, source_target_pairs={{0,1},{1,0},{2,3},{3,2},{4,5},{5,4},{6,7},{7,6},{8,9},{9,8},{10,11... | collective-permute-start | bytes 1572872 | tf_op jit(solution)/shard_map/cond/branch_1_fun/ppermute | solution.py:82
  32.4 42.3 %collective-permute-start.4 = (bf16[512,512]{1,0:T(8,128)(2,1)}, bf16[512,512]{1,0:T(8,128)(2,1)}, u32[]{:S(2)}, u32[]{:S(2)}) collective-permute-start(bf16[512,512]{1,0:T(8,128)(2,1)} %collective-permute-done.refs_3_), channel_id=1, source_target_pairs={{0,1},{1,0},{2,3},{3,2},{4,5},{5,4},{6,7},{7,6},{8,9},{9,8},{10,11... | collective-permute-start | bytes 1572872 | tf_op jit(solution)/shard_map/cond/branch_1_fun/ppermute | solution.py:82
  34.3 40.4 %collective-permute-start.5 = (bf16[512,512]{1,0:T(8,128)(2,1)}, bf16[512,512]{1,0:T(8,128)(2,1)}, u32[]{:S(2)}, u32[]{:S(2)}) collective-permute-start(bf16[512,512]{1,0:T(8,128)(2,1)} %collective-permute-done.1.refs_4_), channel_id=1, source_target_pairs={{0,1},{1,0},{2,3},{3,2},{4,5},{5,4},{6,7},{7,6},{8,9},{9,8},{10,11... | collective-permute-start | bytes 1572872 | tf_op jit(solution)/shard_map/cond/branch_1_fun/ppermute | solution.py:82
  38.7 36.0 %collective-permute-start.6 = (bf16[512,512]{1,0:T(8,128)(2,1)}, bf16[512,512]{1,0:T(8,128)(2,1)}, u32[]{:S(2)}, u32[]{:S(2)}) collective-permute-start(bf16[512,512]{1,0:T(8,128)(2,1)} %collective-permute-done.2.refs_5_), channel_id=1, source_target_pairs={{0,1},{1,0},{2,3},{3,2},{4,5},{5,4},{6,7},{7,6},{8,9},{9,8},{10,11... | collective-permute-start | bytes 1572872 | tf_op jit(solution)/shard_map/cond/branch_1_fun/ppermute | solution.py:82
  45.1 29.6 %collective-permute-start.7 = (s32[2]{0:T(128)S(1)}, s32[2]{0:T(128)S(1)}, u32[]{:S(2)}, u32[]{:S(2)}) collective-permute-start(s32[2]{0:T(128)S(1)} %get-tuple-element.29), channel_id=1, source_target_pairs={{0,8},{8,0},{1,9},{9,1},{2,10},{10,2},{3,11},{11,3},{4,12},{12,4},... | collective-permute-start | bytes 32 | tf_op jit(solution)/shard_map/cond/branch_1_fun/ppermute | solution.py:71
  77.7 27.6 %collective-permute-start.8 = (bf16[2,128,512]{2,1,0:T(8,128)(2,1)S(1)}, bf16[2,128,512]{2,1,0:T(8,128)(2,1)S(1)}, u32[]{:S(2)}, u32[]{:S(2)}) collective-permute-start(bf16[2,128,512]{2,1,0:T(8,128)(2,1)S(1)} %pad_maximum_fusion), channel_id=1, source_target_pairs={{0,8},{8,0},{1,9},{9,1},{2,10},{10,2},{3,11},{11,3},{4,12},{12,4},... | collective-permute-start | bytes 786440 | tf_op jit(solution)/shard_map/ppermute | solution.py:109
  122.5 71.7 %all-to-all-start.1 = ((f32[16,1,32]{2,1,0:T(1,128)}), f32[16,1,32]{2,1,0:T(1,128)S(1)}, u32[]{:S(2)}, u32[]{:S(2)}) async-start(f32[16,1,32]{2,1,0:T(1,128)} %broadcast_in_dim.32), calls=%async_computation.1 | async-start | bytes 16384 | tf_op jit(solution)/shard_map/all_to_all | solution.py:136

commit v2 on v1

v2 whole, which is shorter than its diff:
```python
import math

import jax
import jax.numpy as jnp
from jax import lax
from jax.experimental import pallas as pl
from jax.experimental.pallas import tpu as pltpu
from jax.sharding import Mesh
from jax.sharding import PartitionSpec as P

damping = 0.1

ZLO, Y, ZHI, X, CORE = 16, 4, 2, 4, 2
NAMES = ("zlo", "y", "zhi", "x", "core")
SWAP = [(0, 1), (1, 0)]
EXTRA = 8

VMEM = pl.BlockSpec(memory_space=pltpu.VMEM)
SMEM = pl.BlockSpec(memory_space=pltpu.SMEM)


def project(rows, basis):
    return jnp.dot(rows, basis, preferred_element_type=jnp.float32).astype(jnp.bfloat16)


def train_kernel(ids_ref, in_ref, out_ref, in_basis_ref, out_basis_ref, packed_ref):
    tokens = in_ref.shape[0]
    packed_ref[:tokens] = project(in_ref[...].astype(jnp.bfloat16), in_basis_ref[...])
    packed_ref[tokens : 2 * tokens] = project(out_ref[...].astype(jnp.bfloat16), out_basis_ref[...])
    row = lax.broadcasted_iota(jnp.int32, (EXTRA, in_ref.shape[1]), 0)
    lane = lax.broadcasted_iota(jnp.int32, (EXTRA, in_ref.shape[1]), 1)
    hit = (row == 0) & (lane == ids_ref[0])
    for s in range(1, ids_ref.shape[0]):
        hit = hit | ((row == s) & (lane == ids_ref[s]))
    packed_ref[2 * tokens :] = jnp.where(hit, 1.0, 0.0).astype(jnp.bfloat16)


def pack_train(train_ids, train_in, train_out, in_basis, out_basis):
    tokens, width = train_in.shape
    return pl.pallas_call(
        train_kernel,
        out_shape=jax.ShapeDtypeStruct((2 * tokens + EXTRA, width), jnp.bfloat16),
        in_specs=[SMEM] + [VMEM] * 4,
        out_specs=VMEM,
    )(train_ids, train_in, train_out, in_basis, out_basis)


def score_kernel(packed_ref, *refs, length, columns):
    out_ref = refs[-1]
    tokens = (packed_ref.shape[0] - EXTRA) // 2
    seqs = tokens // length
    inside = packed_ref[:tokens].astype(jnp.float32)
    outside = packed_ref[tokens : 2 * tokens]
    hot = packed_ref[2 * tokens :].astype(jnp.float32)
    rows = [[] for _ in range(seqs)]
    for ref in refs[:-1]:
        weighted = jnp.dot(outside, ref[...], preferred_element_type=jnp.float32)
        prod = weighted * inside
        for s in range(seqs):
            rows[s].append(jnp.sum(prod[s * length : (s + 1) * length], axis=0, keepdims=True))
    total = None
    for s in range(seqs):
        sums = jnp.sum(jnp.concatenate(rows[s], axis=0), axis=1, keepdims=True)
        placed = sums * hot[s : s + 1, :columns]
        total = placed if total is None else total + placed
    out_ref[...] = total


def scores_of(packed, preconds, length, columns):
    return pl.pallas_call(
        lambda *refs: score_kernel(*refs, length=length, columns=columns),
        out_shape=jax.ShapeDtypeStruct((len(preconds), columns), jnp.float32),
        in_specs=[VMEM] * (1 + len(preconds)),
        out_specs=VMEM,
        compiler_params=pltpu.CompilerParams(vmem_limit_bytes=40 << 20),
    )(packed, *preconds)


def gather_preconds(query_in, query_out, in_basis, out_basis, eigen_values, mine, length, columns):
    side_in = project(query_in, in_basis)
    side_out = project(query_out, out_basis)
    moment = lax.dot_general(
        side_out, side_in, (((0,), (0,)), ((), ())), preferred_element_type=jnp.float32
    )
    scale = query_in.shape[0] * (eigen_values + damping)
    precond = (moment / scale).astype(jnp.bfloat16)
    along = [precond]
    for step in range(1, X):
        along.append(lax.ppermute(precond, "x", [(i, i ^ step) for i in range(X)]))
    beside = [lax.ppermute(p, "core", SWAP) for p in along]
    preconds = along + beside
    return preconds, scores_of(mine, preconds, length, columns)


def local(
    train_in,
    train_out,
    query_in,
    query_out,
    basis_in,
    basis_out,
    eigen_values,
    train_ids,
    query_ids,
):
    in_basis = basis_in[0]
    out_basis = basis_out[0]
    seqs, length, width = train_in.shape[1:]
    columns = seqs * ZHI * X * CORE
    tokens = (seqs * length, width)

    mine = pack_train(
        train_ids, train_in[0].reshape(tokens), train_out[0].reshape(tokens), in_basis, out_basis
    )
    theirs = lax.ppermute(mine, "zhi", SWAP)
    preconds, partial_mine = lax.cond(
        lax.axis_index("x") < X,
        lambda *ops: gather_preconds(*ops, length, columns),
        lambda *ops: (
            [jnp.zeros((width, width), jnp.bfloat16)] * (X * CORE),
            jnp.zeros((X * CORE, columns), jnp.float32),
        ),
        query_in[0, 0], query_out[0, 0], in_basis, out_basis, eigen_values[0], mine,
    )
    partial_theirs = scores_of(theirs, preconds, length, columns)
    partial_value = partial_mine + partial_theirs

    k = jnp.arange(X * CORE, dtype=jnp.int32)
    owner = (lax.axis_index("x") ^ (k % X)) * CORE + (lax.axis_index("core") ^ (k // X))
    order = owner[None, :] == k[:, None]
    ordered = jnp.sum(
        jnp.where(order[:, :, None], partial_value[None, :, :], 0.0), axis=1
    )
    spread = jnp.broadcast_to(ordered[None], (Y,) + ordered.shape).reshape(Y * X * CORE, -1)
    near = jnp.sum(lax.all_to_all(spread, ("y", "x", "core"), 0, 0), axis=0)
    far = jnp.broadcast_to(near[None], (ZLO,) + near.shape)
    summed = jnp.sum(lax.all_to_all(far, "zlo", 0, 0), axis=0)
    factor = 1.0 / math.sqrt(ZLO * Y * in_basis.shape[0] * out_basis.shape[0])
    scores = (summed * factor)[None, :]
    seat = jnp.arange(columns, dtype=jnp.int32)
    return jnp.where(query_ids[:, None] == seat[None, :], 0.0, scores)


def solution(mesh):
    split = Mesh(mesh.devices.reshape(ZLO, Y, ZHI, X, CORE), NAMES)
    layer, blk = ("zlo", "y"), ("zhi", "x", "core")
    placed = (
        P(layer, blk, None, None),
        P(layer, blk, None, None),
        P(layer, blk, None, None),
        P(layer, blk, None, None),
        P(layer, None, None),
        P(layer, None, None),
        P(layer, None, None),
        P(blk),
        P(blk),
    )
    return jax.shard_map(
        local, mesh=split, in_specs=placed, out_specs=P(blk, None), check_vma=False
    )
```

time: 195 us -> 132 us (0.68)
  starting transfers between devices: 142 us -> 74.8 us
  waiting for transfers between devices: 24.8 us -> 31.6 us
  Pallas kernels: 6.01 us -> 8.49 us
    all_to_all x1, starting transfers between devices: 52.9 us -> 18.5 us  [local(): summed = jnp.sum(lax.all_to_all(far, 'zlo', 0, 0), axis=0)]
    ppermute x6 -> x5, starting transfers between devices: 79.3 us -> 46.6 us  [the longest x1 29.5 us: local(): theirs = lax.ppermute(mine, 'zhi', SWAP)]
    ppermute x3, waiting for transfers between devices: 0.01 us -> 11.6 us  [gather_preconds(): along.append(lax.ppermute(precond, 'x', [(i, i ^ step) for i in range(X)]))]
    ppermute x6 -> x5, waiting for transfers between devices: 6.7 us -> 1.84 us  [the longest x4 1.83 us: gather_preconds(): beside = [lax.ppermute(p, 'core', SWAP) for p in along]]
    pallas_call x2 -> x3, Pallas kernels: 6.01 us -> 8.49 us  [the longest x2 5.99 us: scores_of(): pl.pallas_call(lambda *refs: score_kernel(*refs, length=length, columns=c...]
    unnamed x13 -> x8, local copies, waits for them, and re-layouts: 2.49 us -> 0.02 us
  transfers between devices with their start and end apart: 10 -> 9, of which waited for: 3 -> 5; matrix products, arithmetic and copies ran while one was open for 0% -> 1% of each run, Pallas kernels for 0% -> 2%
where the time goes in v2:
time: 132 us; the launch traced here: 131 us
  starting transfers between devices  74.8 us (57%)
  waiting for transfers between devices  31.6 us (24%)
  blocking collectives  11.7 us (9%)
  Pallas kernels  8.49 us (6%)
  matrix products  1.73 us (1%)
  local copies, waits for them, and re-layouts  1.54 us (1%)
    ppermute x1, starting transfers between devices, local(): theirs = lax.ppermute(mine, 'zhi', SWAP)  29.5 us
    all_to_all x1, starting transfers between devices, local(): summed = jnp.sum(lax.all_to_all(far, 'zlo', 0, 0), axis=0)  18.5 us
    all_to_all x1, waiting for transfers between devices, local(): summed = jnp.sum(lax.all_to_all(far, 'zlo', 0, 0), axis=0)  18.1 us
    ppermute x4, starting transfers between devices, gather_preconds(): beside = [lax.ppermute(p, 'core', SWAP) for p in along]  17.1 us
    all_to_all x1, blocking collectives, local(): near = jnp.sum(lax.all_to_all(spread, ('y', 'x', 'core'), 0, 0), axis=0)  11.7 us
    ppermute x3, waiting for transfers between devices, gather_preconds(): along.append(lax.ppermute(precond, 'x', [(i, i ^ step) for i in range(X)]))  11.6 us
    ppermute x3, starting transfers between devices, gather_preconds(): along.append(lax.ppermute(precond, 'x', [(i, i ^ step) for i in range(X)]))  9.57 us
    pallas_call x2, Pallas kernels, scores_of(): pl.pallas_call(lambda *refs: score_kernel(*refs, length=length, columns=c...  5.99 us
  transfers between devices with their start and end apart: 9, of which 5 were waited for; matrix products, arithmetic and copies ran while one was open for 1% of the time, Pallas kernels for 2%

profile of v2, /device:TPU:1, one launch (start us, length us, event | category | flops | bytes accessed | tf_op | source)
XLA Modules:
  0.0 131.4 jit_solution(1700392965060351403)
XLA Ops:
  0.0 0.0 copy-start
  0.0 0.0 copy-start.1
  0.0 0.0 copy-start.2
  0.0 0.0 copy-start.4
  0.0 2.5 %shard_map.94 = bf16[264,512]{1,0:T(8,128)(2,1)} custom-call(s32[2]{0:T(128)} %ids_ref.1, f32[128,512]{1,0:T(8,128)} %bitcast.26, f32[128,512]{1,0:T(8,128)} %bitcast.27, bf16[512,512]{1,0:T(8,128)(2,1)} %bitcast.22, bf16[512,512]{1,0:T(8,128)(2,1)} %bitcast.24), custom_call_target="tpu_custom_call" | custom-call | tf_op jit(solution)/shard_map/pallas_call | solution.py:40
  2.5 29.5 %collective-permute-start.7 = (bf16[264,512]{1,0:T(8,128)(2,1)}, bf16[264,512]{1,0:T(8,128)(2,1)S(1)}, u32[]{:S(2)}, u32[]{:S(2)}) collective-permute-start(bf16[264,512]{1,0:T(8,128)(2,1)} %shard_map.94), channel_id=1, source_target_pairs={{0,8},{8,0},{1,9},{9,1},{2,10},{10,2},{3,11},{11,3},{4,12},{12,4},... | collective-permute-start | bytes 811016 | tf_op jit(solution)/shard_map/ppermute | solution.py:115
  32.1 0.0 copy-done
  32.1 0.0 copy-done.1
  32.1 0.0 copy-done.2
  32.1 0.0 copy-done.4
  32.1 46.0 %conditional.1 = (bf16[512,512]{1,0:T(8,128)(2,1)}, bf16[512,512]{1,0:T(8,128)(2,1)}, bf16[512,512]{1,0:T(8,128)(2,1)}, bf16[512,512]{1,0:T(8,128)(2,1)}, bf16[5...) conditional(s32[]{:T(128)} %convert_element_type.12, () %tuple.13, ...), branch_computations={%region_0.0_spmd, %region_1.0_spmd} | conditional | flops 403963904 | bytes 22544764 | solution.py:116
  32.1 0.0 copy-start.3
  32.1 0.3 convolution_convert_fusion
  32.4 0.9 copy-done.3
  33.3 1.4 %fusion.refs_1_ = bf16[512,512]{1,0:T(8,128)(2,1)} fusion(bf16[256,512]{1,0:T(8,128)(2,1)S(1)} %convolution_convert_fusion, bf16[512,512]{1,0:T(8,128)(2,1)S(1)} %get-tuple-element.21, f32[1,512,512]{2,1,0:T(8,128)S(1)} %copy-done.3, bf16[1,1,256,512]{3,2,1,0:T(8,128)(2,1)S(1)} %get-tuple-element.47), kind=kOutput, calls=%fused_computation.1 | convolution fusion | flops 269615104 | bytes 2621440 | tf_op jit(solution)/shard_map/cond/branch_1_fun/dot_general | solution.py:82
  34.8 3.1 %collective-permute-start = (bf16[512,512]{1,0:T(8,128)(2,1)}, bf16[512,512]{1,0:T(8,128)(2,1)}, u32[]{:S(2)}, u32[]{:S(2)}) collective-permute-start(bf16[512,512]{1,0:T(8,128)(2,1)} %fusion.refs_1_), channel_id=1, source_target_pairs={{0,2},{2,0},{4,6},{6,4},{1,3},{3,1},{5,7},{7,5},{8,10},{10,8},{12,... | collective-permute-start | bytes 1572872 | tf_op jit(solution)/shard_map/cond/branch_1_fun/ppermute | solution.py:89
  37.9 4.4 %collective-permute-start.1 = (bf16[512,512]{1,0:T(8,128)(2,1)}, bf16[512,512]{1,0:T(8,128)(2,1)}, u32[]{:S(2)}, u32[]{:S(2)}) collective-permute-start(bf16[512,512]{1,0:T(8,128)(2,1)} %fusion.refs_1_), channel_id=1, source_target_pairs={{0,4},{2,6},{4,0},{6,2},{1,5},{3,7},{5,1},{7,3},{8,12},{10,14},{12... | collective-permute-start | bytes 1572872 | tf_op jit(solution)/shard_map/cond/branch_1_fun/ppermute | solution.py:89
  42.2 2.1 %collective-permute-start.2 = (bf16[512,512]{1,0:T(8,128)(2,1)}, bf16[512,512]{1,0:T(8,128)(2,1)}, u32[]{:S(2)}, u32[]{:S(2)}) collective-permute-start(bf16[512,512]{1,0:T(8,128)(2,1)} %fusion.refs_1_), channel_id=1, source_target_pairs={{0,6},{2,4},{4,2},{6,0},{1,7},{3,5},{5,3},{7,1},{8,14},{10,12},{12... | collective-permute-start | bytes 1572872 | tf_op jit(solution)/shard_map/cond/branch_1_fun/ppermute | solution.py:89
  44.4 3.7 %collective-permute-start.3 = (bf16[512,512]{1,0:T(8,128)(2,1)}, bf16[512,512]{1,0:T(8,128)(2,1)}, u32[]{:S(2)}, u32[]{:S(2)}) collective-permute-start(bf16[512,512]{1,0:T(8,128)(2,1)} %fusion.refs_1_), channel_id=1, source_target_pairs={{0,1},{1,0},{2,3},{3,2},{4,5},{5,4},{6,7},{7,6},{8,9},{9,8},{10,11... | collective-permute-start | bytes 1572872 | tf_op jit(solution)/shard_map/cond/branch_1_fun/ppermute | solution.py:90
  48.1 1.4 %collective-permute-done.refs_2_ = bf16[512,512]{1,0:T(8,128)(2,1)} collective-permute-done((bf16[512,512]{1,0:T(8,128)(2,1)}, bf16[512,512]{1,0:T(8,128)(2,1)}, u32[]{:S(2)}, u32[]{:S(2)}) %collective-permute-start) | collective-permute-done | bytes 524320 | tf_op jit(solution)/shard_map/cond/branch_1_fun/ppermute | solution.py:89
  49.4 5.2 %collective-permute-start.4 = (bf16[512,512]{1,0:T(8,128)(2,1)}, bf16[512,512]{1,0:T(8,128)(2,1)}, u32[]{:S(2)}, u32[]{:S(2)}) collective-permute-start(bf16[512,512]{1,0:T(8,128)(2,1)} %collective-permute-done.refs_2_), channel_id=1, source_target_pairs={{0,1},{1,0},{2,3},{3,2},{4,5},{5,4},{6,7},{7,6},{8,9},{9,8},{10,11... | collective-permute-start | bytes 1572872 | tf_op jit(solution)/shard_map/cond/branch_1_fun/ppermute | solution.py:90
  54.7 8.2 %collective-permute-done.1.refs_3_ = bf16[512,512]{1,0:T(8,128)(2,1)} collective-permute-done((bf16[512,512]{1,0:T(8,128)(2,1)}, bf16[512,512]{1,0:T(8,128)(2,1)}, u32[]{:S(2)}, u32[]{:S(2)}) %collective-permute-start.1) | collective-permute-done | bytes 524320 | tf_op jit(solution)/shard_map/cond/branch_1_fun/ppermute | solution.py:89
  62.9 3.8 %collective-permute-start.5 = (bf16[512,512]{1,0:T(8,128)(2,1)}, bf16[512,512]{1,0:T(8,128)(2,1)}, u32[]{:S(2)}, u32[]{:S(2)}) collective-permute-start(bf16[512,512]{1,0:T(8,128)(2,1)} %collective-permute-done.1.refs_3_), channel_id=1, source_target_pairs={{0,1},{1,0},{2,3},{3,2},{4,5},{5,4},{6,7},{7,6},{8,9},{9,8},{10,11... | collective-permute-start | bytes 1572872 | tf_op jit(solution)/shard_map/cond/branch_1_fun/ppermute | solution.py:90
  66.7 2.0 %collective-permute-done.2.refs_4_ = bf16[512,512]{1,0:T(8,128)(2,1)} collective-permute-done((bf16[512,512]{1,0:T(8,128)(2,1)}, bf16[512,512]{1,0:T(8,128)(2,1)}, u32[]{:S(2)}, u32[]{:S(2)}) %collective-permute-start.2) | collective-permute-done | bytes 524320 | tf_op jit(solution)/shard_map/cond/branch_1_fun/ppermute | solution.py:89
  68.8 4.3 %collective-permute-start.6 = (bf16[512,512]{1,0:T(8,128)(2,1)}, bf16[512,512]{1,0:T(8,128)(2,1)}, u32[]{:S(2)}, u32[]{:S(2)}) collective-permute-start(bf16[512,512]{1,0:T(8,128)(2,1)} %collective-permute-done.2.refs_4_), channel_id=1, source_target_pairs={{0,1},{1,0},{2,3},{3,2},{4,5},{5,4},{6,7},{7,6},{8,9},{9,8},{10,11... | collective-permute-start | bytes 1572872 | tf_op jit(solution)/shard_map/cond/branch_1_fun/ppermute | solution.py:90
  73.1 0.0 collective-permute-done.3.refs_5_
  73.2 0.0 collective-permute-done.4.refs_6_
  73.2 0.0 collective-permute-done.5.refs_7_
  73.2 1.8 %collective-permute-done.6.refs_8_ = bf16[512,512]{1,0:T(8,128)(2,1)} collective-permute-done((bf16[512,512]{1,0:T(8,128)(2,1)}, bf16[512,512]{1,0:T(8,128)(2,1)}, u32[]{:S(2)}, u32[]{:S(2)}) %collective-permute-start.6) | collective-permute-done | bytes 524320 | tf_op jit(solution)/shard_map/cond/branch_1_fun/ppermute | solution.py:90
  75.0 3.0 %branch_1_fun.1 = f32[8,32]{1,0:T(8,128)S(1)} custom-call(bf16[264,512]{1,0:T(8,128)(2,1)} %get-tuple-element.25.refs_0_, bf16[512,512]{1,0:T(8,128)(2,1)} %fusion.refs_1_, bf16[512,512]{1,0:T(8,128)(2,1)} %collective-permute-done.refs_2_, bf16[512,512]{1,0:T(8,128)(2,1)} %collective-permute-done.1.refs_3_, bf16[512,512]{1,0:T(8,128)(2,1)} %collective-permute-done.2.refs_4_, ...), custom_call_target="tpu_custom_call" | custom-call | tf_op jit(solution)/shard_map/cond/branch_1_fun/pallas_call | solution.py:70
  78.1 0.0 collective-permute-done.7.refs_0_
  78.1 3.0 %shard_map.95 = f32[8,32]{1,0:T(8,128)S(1)} custom-call(bf16[264,512]{1,0:T(8,128)(2,1)S(1)} %collective-permute-done.7.refs_0_, bf16[512,512]{1,0:T(8,128)(2,1)} %get-tuple-element.36.refs_1_, bf16[512,512]{1,0:T(8,128)(2,1)} %get-tuple-element.37.refs_2_, bf16[512,512]{1,0:T(8,128)(2,1)} %get-tuple-element.38.refs_3_, ...), custom_call_target="tpu_custom_call" | custom-call | tf_op jit(solution)/shard_map/pallas_call | solution.py:70
  81.0 0.1 select_reduce_fusion
  81.1 11.7 %all_to_all.15 = f32[32,1,32]{2,1,0:T(1,128)S(1)} all-to-all(f32[32,1,32]{2,1,0:T(1,128)S(1)} %bitcast.28), channel_id=1, replica_groups=mesh['zlo'=16,'y'=4,'zhi'=2,'x'=4,'core'=2] {'y','x','core'}, dimensions={0} | all-to-all | bytes 8192 | tf_op jit(solution)/shard_map/all_to_all | solution.py:135
  92.9 0.1 reduce_sum.28
  92.9 0.6 broadcast_in_dim.48
  93.5 18.5 %all-to-all-start.1 = ((f32[16,1,32]{2,1,0:T(1,128)}), f32[16,1,32]{2,1,0:T(1,128)S(1)}, u32[]{:S(2)}, u32[]{:S(2)}) async-start(f32[16,1,32]{2,1,0:T(1,128)} %broadcast_in_dim.48), calls=%async_computation.1 | async-start | bytes 16384 | tf_op jit(solution)/shard_map/all_to_all | solution.py:137
  112.7 18.1 %all-to-all-done.1 = f32[16,1,32]{2,1,0:T(1,128)S(1)} async-done(((f32[16,1,32]{2,1,0:T(1,128)}), f32[16,1,32]{2,1,0:T(1,128)S(1)}, u32[]{:S(2)}, u32[]{:S(2)}) %all-to-all-start.1) | async-done | bytes 2080 | tf_op jit(solution)/shard_map/all_to_all | solution.py:137
  130.9 0.5 compare_select_fusion
  (5 shorter events, 0.0 us)
Async XLA Ops:
  0.0 32.1 %copy-start = (bf16[1,512,512]{2,1,0:T(8,128)(2,1)S(1)}, bf16[1,512,512]{2,1,0:T(8,128)(2,1)}, u32[]{:S(2)}) copy-start(bf16[1,512,512]{2,1,0:T(8,128)(2,1)} %param.15) | copy-start | bytes 1572868
  0.0 32.1 %copy-start.1 = (bf16[1,512,512]{2,1,0:T(8,128)(2,1)S(1)}, bf16[1,512,512]{2,1,0:T(8,128)(2,1)}, u32[]{:S(2)}) copy-start(bf16[1,512,512]{2,1,0:T(8,128)(2,1)} %param.16) | copy-start | bytes 1572868
  0.0 32.1 %copy-start.2 = (bf16[1,1,256,512]{3,2,1,0:T(8,128)(2,1)S(1)}, bf16[1,1,256,512]{3,2,1,0:T(8,128)(2,1)}, u32[]{:S(2)}) copy-start(bf16[1,1,256,512]{3,2,1,0:T(8,128)(2,1)} %param.13) | copy-start | bytes 786436
  0.0 32.1 %copy-start.4 = (bf16[1,1,256,512]{3,2,1,0:T(8,128)(2,1)S(1)}, bf16[1,1,256,512]{3,2,1,0:T(8,128)(2,1)}, u32[]{:S(2)}) copy-start(bf16[1,1,256,512]{3,2,1,0:T(8,128)(2,1)} %param.14) | copy-start | bytes 786436
  2.5 75.5 %collective-permute-start.7 = (bf16[264,512]{1,0:T(8,128)(2,1)}, bf16[264,512]{1,0:T(8,128)(2,1)S(1)}, u32[]{:S(2)}, u32[]{:S(2)}) collective-permute-start(bf16[264,512]{1,0:T(8,128)(2,1)} %shard_map.94), channel_id=1, source_target_pairs={{0,8},{8,0},{1,9},{9,1},{2,10},{10,2},{3,11},{11,3},{4,12},{12,4},... | collective-permute-start | bytes 811016 | tf_op jit(solution)/shard_map/ppermute | solution.py:115
  32.1 1.2 copy-start.3
  34.8 14.7 %collective-permute-start = (bf16[512,512]{1,0:T(8,128)(2,1)}, bf16[512,512]{1,0:T(8,128)(2,1)}, u32[]{:S(2)}, u32[]{:S(2)}) collective-permute-start(bf16[512,512]{1,0:T(8,128)(2,1)} %fusion.refs_1_), channel_id=1, source_target_pairs={{0,2},{2,0},{4,6},{6,4},{1,3},{3,1},{5,7},{7,5},{8,10},{10,8},{12,... | collective-permute-start | bytes 1572872 | tf_op jit(solution)/shard_map/cond/branch_1_fun/ppermute | solution.py:89
  37.9 25.0 %collective-permute-start.1 = (bf16[512,512]{1,0:T(8,128)(2,1)}, bf16[512,512]{1,0:T(8,128)(2,1)}, u32[]{:S(2)}, u32[]{:S(2)}) collective-permute-start(bf16[512,512]{1,0:T(8,128)(2,1)} %fusion.refs_1_), channel_id=1, source_target_pairs={{0,4},{2,6},{4,0},{6,2},{1,5},{3,7},{5,1},{7,3},{8,12},{10,14},{12... | collective-permute-start | bytes 1572872 | tf_op jit(solution)/shard_map/cond/branch_1_fun/ppermute | solution.py:89
  42.2 26.5 %collective-permute-start.2 = (bf16[512,512]{1,0:T(8,128)(2,1)}, bf16[512,512]{1,0:T(8,128)(2,1)}, u32[]{:S(2)}, u32[]{:S(2)}) collective-permute-start(bf16[512,512]{1,0:T(8,128)(2,1)} %fusion.refs_1_), channel_id=1, source_target_pairs={{0,6},{2,4},{4,2},{6,0},{1,7},{3,5},{5,3},{7,1},{8,14},{10,12},{12... | collective-permute-start | bytes 1572872 | tf_op jit(solution)/shard_map/cond/branch_1_fun/ppermute | solution.py:89
  44.4 28.8 %collective-permute-start.3 = (bf16[512,512]{1,0:T(8,128)(2,1)}, bf16[512,512]{1,0:T(8,128)(2,1)}, u32[]{:S(2)}, u32[]{:S(2)}) collective-permute-start(bf16[512,512]{1,0:T(8,128)(2,1)} %fusion.refs_1_), channel_id=1, source_target_pairs={{0,1},{1,0},{2,3},{3,2},{4,5},{5,4},{6,7},{7,6},{8,9},{9,8},{10,11... | collective-permute-start | bytes 1572872 | tf_op jit(solution)/shard_map/cond/branch_1_fun/ppermute | solution.py:90
  49.4 23.7 %collective-permute-start.4 = (bf16[512,512]{1,0:T(8,128)(2,1)}, bf16[512,512]{1,0:T(8,128)(2,1)}, u32[]{:S(2)}, u32[]{:S(2)}) collective-permute-start(bf16[512,512]{1,0:T(8,128)(2,1)} %collective-permute-done.refs_2_), channel_id=1, source_target_pairs={{0,1},{1,0},{2,3},{3,2},{4,5},{5,4},{6,7},{7,6},{8,9},{9,8},{10,11... | collective-permute-start | bytes 1572872 | tf_op jit(solution)/shard_map/cond/branch_1_fun/ppermute | solution.py:90
  62.9 10.3 %collective-permute-start.5 = (bf16[512,512]{1,0:T(8,128)(2,1)}, bf16[512,512]{1,0:T(8,128)(2,1)}, u32[]{:S(2)}, u32[]{:S(2)}) collective-permute-start(bf16[512,512]{1,0:T(8,128)(2,1)} %collective-permute-done.1.refs_3_), channel_id=1, source_target_pairs={{0,1},{1,0},{2,3},{3,2},{4,5},{5,4},{6,7},{7,6},{8,9},{9,8},{10,11... | collective-permute-start | bytes 1572872 | tf_op jit(solution)/shard_map/cond/branch_1_fun/ppermute | solution.py:90
  68.8 6.2 %collective-permute-start.6 = (bf16[512,512]{1,0:T(8,128)(2,1)}, bf16[512,512]{1,0:T(8,128)(2,1)}, u32[]{:S(2)}, u32[]{:S(2)}) collective-permute-start(bf16[512,512]{1,0:T(8,128)(2,1)} %collective-permute-done.2.refs_4_), channel_id=1, source_target_pairs={{0,1},{1,0},{2,3},{3,2},{4,5},{5,4},{6,7},{7,6},{8,9},{9,8},{10,11... | collective-permute-start | bytes 1572872 | tf_op jit(solution)/shard_map/cond/branch_1_fun/ppermute | solution.py:90
  93.5 37.3 %all-to-all-start.1 = ((f32[16,1,32]{2,1,0:T(1,128)}), f32[16,1,32]{2,1,0:T(1,128)S(1)}, u32[]{:S(2)}, u32[]{:S(2)}) async-start(f32[16,1,32]{2,1,0:T(1,128)} %broadcast_in_dim.48), calls=%async_computation.1 | async-start | bytes 16384 | tf_op jit(solution)/shard_map/all_to_all | solution.py:137

commit v3 on v2

--- a/solution.py
+++ b/solution.py
@@ -45,38 +45,45 @@
     )(train_ids, train_in, train_out, in_basis, out_basis)
 
 
-def score_kernel(packed_ref, *refs, length, columns):
-    out_ref = refs[-1]
-    tokens = (packed_ref.shape[0] - EXTRA) // 2
+def score_kernel(mine_ref, theirs_ref, here_ref, there_ref, out_ref, sums_ref, *, length, columns):
+    step, steps = pl.program_id(0), pl.num_programs(0)
+    tokens = (mine_ref.shape[0] - EXTRA) // 2
     seqs = tokens // length
-    inside = packed_ref[:tokens].astype(jnp.float32)
-    outside = packed_ref[tokens : 2 * tokens]
-    hot = packed_ref[2 * tokens :].astype(jnp.float32)
-    rows = [[] for _ in range(seqs)]
-    for ref in refs[:-1]:
-        weighted = jnp.dot(outside, ref[...], preferred_element_type=jnp.float32)
-        prod = weighted * inside
-        for s in range(seqs):
-            rows[s].append(jnp.sum(prod[s * length : (s + 1) * length], axis=0, keepdims=True))
-    total = None
-    for s in range(seqs):
-        sums = jnp.sum(jnp.concatenate(rows[s], axis=0), axis=1, keepdims=True)
-        placed = sums * hot[s : s + 1, :columns]
-        total = placed if total is None else total + placed
-    out_ref[...] = total
+    for p, packed_ref in enumerate((mine_ref, theirs_ref)):
+        inside = packed_ref[:tokens].astype(jnp.float32)
+        outside = packed_ref[tokens : 2 * tokens]
+        for c, ref in enumerate((here_ref, there_ref)):
+            prod = inside * jnp.dot(outside, ref[0], preferred_element_type=jnp.float32)
+            for s in range(seqs):
+                part = jnp.sum(prod[s * length : (s + 1) * length], axis=0, keepdims=True)
+                sums_ref[p * seqs + s, pl.ds(c * X + step, 1), :] = part
+
+    @pl.when(step == steps - 1)
+    def _():
+        total = jnp.zeros(out_ref.shape, jnp.float32)
+        for p, packed_ref in enumerate((mine_ref, theirs_ref)):
+            hot = packed_ref[2 * tokens :].astype(jnp.float32)
+            for s in range(seqs):
+                sums = jnp.sum(sums_ref[p * seqs + s], axis=1, keepdims=True)
+                total = total + sums * hot[s : s + 1, :columns]
+        out_ref[...] = total
 
 
-def scores_of(packed, preconds, length, columns):
+def scores_of(mine, theirs, here, there, length, columns):
+    queries, rows, width = here.shape
+    seqs = (mine.shape[0] - EXTRA) // 2 // length
+    each = pl.BlockSpec((1, rows, width), lambda i: (i, 0, 0))
     return pl.pallas_call(
         lambda *refs: score_kernel(*refs, length=length, columns=columns),
-        out_shape=jax.ShapeDtypeStruct((len(preconds), columns), jnp.float32),
-        in_specs=[VMEM] * (1 + len(preconds)),
-        out_specs=VMEM,
-        compiler_params=pltpu.CompilerParams(vmem_limit_bytes=40 << 20),
-    )(packed, *preconds)
+        out_shape=jax.ShapeDtypeStruct((CORE * queries, columns), jnp.float32),
+        grid=(queries,),
+        in_specs=[VMEM, VMEM, each, each],
+        out_specs=pl.BlockSpec((CORE * queries, columns), lambda i: (0, 0)),
+        scratch_shapes=[pltpu.VMEM((2 * seqs, CORE * queries, width), jnp.float32)],
+    )(mine, theirs, here, there)
 
 
-def gather_preconds(query_in, query_out, in_basis, out_basis, eigen_values, mine, length, columns):
+def gather_preconds(query_in, query_out, in_basis, out_basis, eigen_values):
     side_in = project(query_in, in_basis)
     side_out = project(query_out, out_basis)
     moment = lax.dot_general(
@@ -87,9 +94,8 @@
     along = [precond]
     for step in range(1, X):
         along.append(lax.ppermute(precond, "x", [(i, i ^ step) for i in range(X)]))
-    beside = [lax.ppermute(p, "core", SWAP) for p in along]
-    preconds = along + beside
-    return preconds, scores_of(mine, preconds, length, columns)
+    here = jnp.stack(along)
+    return [here, lax.ppermute(here, "core", SWAP)]
 
 
 def local(
@@ -113,17 +119,13 @@
         train_ids, train_in[0].reshape(tokens), train_out[0].reshape(tokens), in_basis, out_basis
     )
     theirs = lax.ppermute(mine, "zhi", SWAP)
-    preconds, partial_mine = lax.cond(
+    here, there = lax.cond(
         lax.axis_index("x") < X,
-        lambda *ops: gather_preconds(*ops, length, columns),
-        lambda *ops: (
-            [jnp.zeros((width, width), jnp.bfloat16)] * (X * CORE),
-            jnp.zeros((X * CORE, columns), jnp.float32),
-        ),
-        query_in[0, 0], query_out[0, 0], in_basis, out_basis, eigen_values[0], mine,
+        gather_preconds,
+        lambda *ops: [jnp.zeros((X, width, width), jnp.bfloat16)] * CORE,
+        query_in[0, 0], query_out[0, 0], in_basis, out_basis, eigen_values[0],
     )
-    partial_theirs = scores_of(theirs, preconds, length, columns)
-    partial_value = partial_mine + partial_theirs
+    partial_value = scores_of(mine, theirs, here, there, length, columns)
 
     k = jnp.arange(X * CORE, dtype=jnp.int32)
     owner = (lax.axis_index("x") ^ (k % X)) * CORE + (lax.axis_index("core") ^ (k // X))

time: 132 us -> 135 us (1.023)
  waiting for transfers between devices: 31.6 us -> 46.3 us
  starting transfers between devices: 74.8 us -> 60.7 us
  other arithmetic: 0.69 us -> 2.96 us
  matrix products: 1.73 us -> 3.52 us
  Pallas kernels: 8.49 us -> 7.09 us
    ppermute x4 -> x1, starting transfers between devices: 17.1 us -> 4.33 us  [gather_preconds(): return [here, lax.ppermute(here, 'core', SWAP)]]
    ppermute x3, waiting for transfers between devices: 11.6 us -> 24.1 us  [gather_preconds(): along.append(lax.ppermute(precond, 'x', [(i, i ^ step) for i in range(X)]))]
    ppermute x4 -> x1, waiting for transfers between devices: 1.83 us -> 4.11 us  [gather_preconds(): return [here, lax.ppermute(here, 'core', SWAP)]]
    another operation x0 -> x1, other arithmetic: none -> 1.6 us  [gather_preconds(): here = jnp.stack(along)]
    pallas_call x2 -> x1, Pallas kernels: 5.99 us -> 4.71 us  [scores_of(): pl.pallas_call(lambda *refs: score_kernel(*refs, length=length, columns=c...]
  transfers between devices with their start and end apart: 9 -> 6, of which waited for: 5 -> 5; matrix products, arithmetic and copies ran while one was open for 1% -> 4% of each run, Pallas kernels for 2% -> 0%
where the time goes in v3:
time: 135 us; the launch traced here: 134 us
  starting transfers between devices  60.7 us (45%)
  waiting for transfers between devices  46.3 us (34%)
  blocking collectives  11.7 us (9%)
  Pallas kernels  7.09 us (5%)
  matrix products  3.52 us (3%)
  other arithmetic  2.96 us (2%)
    ppermute x1, starting transfers between devices, local(): theirs = lax.ppermute(mine, 'zhi', SWAP)  29.5 us
    ppermute x3, waiting for transfers between devices, gather_preconds(): along.append(lax.ppermute(precond, 'x', [(i, i ^ step) for i in range(X)]))  24.1 us
    all_to_all x1, waiting for transfers between devices, local(): summed = jnp.sum(lax.all_to_all(far, 'zlo', 0, 0), axis=0)  18.1 us
    all_to_all x1, starting transfers between devices, local(): summed = jnp.sum(lax.all_to_all(far, 'zlo', 0, 0), axis=0)  17.2 us
    all_to_all x1, blocking collectives, local(): near = jnp.sum(lax.all_to_all(spread, ('y', 'x', 'core'), 0, 0), axis=0)  11.7 us
    ppermute x3, starting transfers between devices, gather_preconds(): along.append(lax.ppermute(precond, 'x', [(i, i ^ step) for i in range(X)]))  9.58 us
    pallas_call x1, Pallas kernels, scores_of(): pl.pallas_call(lambda *refs: score_kernel(*refs, length=length, columns=c...  4.71 us
    ppermute x1, starting transfers between devices, gather_preconds(): return [here, lax.ppermute(here, 'core', SWAP)]  4.33 us
  transfers between devices with their start and end apart: 6, of which 5 were waited for; matrix products, arithmetic and copies ran while one was open for 4% of the time, Pallas kernels for 0%

profile of v3, /device:TPU:1, one launch (start us, length us, event | category | flops | bytes accessed | tf_op | source)
XLA Modules:
  0.0 134.4 jit_solution(14845023347646693959)
XLA Ops:
  0.0 2.4 %shard_map.94.refs_0_ = bf16[264,512]{1,0:T(8,128)(2,1)} custom-call(s32[2]{0:T(128)} %ids_ref.1, f32[128,512]{1,0:T(8,128)} %bitcast.34, f32[128,512]{1,0:T(8,128)} %bitcast.35, bf16[512,512]{1,0:T(8,128)(2,1)} %bitcast.26, bf16[512,512]{1,0:T(8,128)(2,1)} %bitcast.28), custom_call_target="tpu_custom_call" | custom-call | tf_op jit(solution)/shard_map/pallas_call | solution.py:40
  2.4 29.5 %collective-permute-start.4 = (bf16[264,512]{1,0:T(8,128)(2,1)}, bf16[264,512]{1,0:T(8,128)(2,1)S(1)}, u32[]{:S(2)}, u32[]{:S(2)}) collective-permute-start(bf16[264,512]{1,0:T(8,128)(2,1)} %shard_map.94.refs_0_), channel_id=1, source_target_pairs={{0,8},{8,0},{1,9},{9,1},{2,10},{10,2},{3,11},{11,3},{4,12},{12,4},... | collective-permute-start | bytes 811016 | tf_op jit(solution)/shard_map/ppermute | solution.py:121
  31.9 47.3 %conditional.1 = (bf16[4,512,512]{2,1,0:T(8,128)(2,1)}, bf16[4,512,512]{2,1,0:T(8,128)(2,1)}) conditional(s32[]{:T(128)} %convert_element_type.12, () %tuple.13, (bf16[1,1,256,512]{3,2,1,0:T(8,128)(2,1)}, bf16[512,512]{1,0:T(8,128)(2,1)}, bf16[1,1,256,512]{3,2,1,0:T(8,128)(2,1)}, bf16[512,512]{1,0:T(8,128)(2,1)}, f32[1,512,512]{2,1,0:T(8,128)}) %tuple.18), branch_computations={%region_0.0_spmd, %region_1.0_spmd} | conditional | flops 407109632 | bytes 22544560 | solution.py:122
  31.9 1.4 %convolution_convert_fusion = bf16[256,512]{1,0:T(8,128)(2,1)S(1)} fusion(bf16[512,512]{1,0:T(8,128)(2,1)} %get-tuple-element.21, bf16[1,1,256,512]{3,2,1,0:T(8,128)(2,1)} %get-tuple-element.31), kind=kOutput, calls=%fused_computation.3 | convolution fusion | flops 134348800 | bytes 1048576 | tf_op jit(solution)/shard_map/cond/branch_1_fun/dot_general | solution.py:23
  33.4 2.1 %fusion = bf16[512,512]{1,0:T(8,128)(2,1)S(1)} fusion(bf16[256,512]{1,0:T(8,128)(2,1)S(1)} %convolution_convert_fusion, bf16[512,512]{1,0:T(8,128)(2,1)} %get-tuple-element.19, f32[1,512,512]{2,1,0:T(8,128)} %get-tuple-element.32, bf16[1,1,256,512]{3,2,1,0:T(8,128)(2,1)} %get-tuple-element.30), kind=kOutput, calls=%fused_computation.2 | convolution fusion | flops 269615104 | bytes 2621440 | tf_op jit(solution)/shard_map/cond/branch_1_fun/dot_general | solution.py:89
  35.5 3.1 %collective-permute-start = (bf16[512,512]{1,0:T(8,128)(2,1)S(1)}, bf16[512,512]{1,0:T(8,128)(2,1)S(1)}, u32[]{:S(2)}, u32[]{:S(2)}) collective-permute-start(bf16[512,512]{1,0:T(8,128)(2,1)S(1)} %fusion), channel_id=1, source_target_pairs={{0,2},{2,0},{4,6},{6,4},{1,3},{3,1},{5,7},{7,5},{8,10},{10,8},{12,... | collective-permute-start | bytes 1572872 | tf_op jit(solution)/shard_map/cond/branch_1_fun/ppermute | solution.py:96
  38.6 4.4 %collective-permute-start.1 = (bf16[512,512]{1,0:T(8,128)(2,1)S(1)}, bf16[512,512]{1,0:T(8,128)(2,1)S(1)}, u32[]{:S(2)}, u32[]{:S(2)}) collective-permute-start(bf16[512,512]{1,0:T(8,128)(2,1)S(1)} %fusion), channel_id=1, source_target_pairs={{0,4},{2,6},{4,0},{6,2},{1,5},{3,7},{5,1},{7,3},{8,12},{10,14},{12... | collective-permute-start | bytes 1572872 | tf_op jit(solution)/shard_map/cond/branch_1_fun/ppermute | solution.py:96
  42.9 2.1 %collective-permute-start.2 = (bf16[512,512]{1,0:T(8,128)(2,1)S(1)}, bf16[512,512]{1,0:T(8,128)(2,1)S(1)}, u32[]{:S(2)}, u32[]{:S(2)}) collective-permute-start(bf16[512,512]{1,0:T(8,128)(2,1)S(1)} %fusion), channel_id=1, source_target_pairs={{0,6},{2,4},{4,2},{6,0},{1,7},{3,5},{5,3},{7,1},{8,14},{10,12},{12... | collective-permute-start | bytes 1572872 | tf_op jit(solution)/shard_map/cond/branch_1_fun/ppermute | solution.py:96
  45.1 4.8 %collective-permute-done = bf16[512,512]{1,0:T(8,128)(2,1)S(1)} collective-permute-done((bf16[512,512]{1,0:T(8,128)(2,1)S(1)}, bf16[512,512]{1,0:T(8,128)(2,1)S(1)}, u32[]{:S(2)}, u32[]{:S(2)}) %collective-permute-start) | collective-permute-done | bytes 524320 | tf_op jit(solution)/shard_map/cond/branch_1_fun/ppermute | solution.py:96
  49.8 13.5 %collective-permute-done.1 = bf16[512,512]{1,0:T(8,128)(2,1)S(1)} collective-permute-done((bf16[512,512]{1,0:T(8,128)(2,1)S(1)}, bf16[512,512]{1,0:T(8,128)(2,1)S(1)}, u32[]{:S(2)}, u32[]{:S(2)}) %collective-permute-start.1) | collective-permute-done | bytes 524320 | tf_op jit(solution)/shard_map/cond/branch_1_fun/ppermute | solution.py:96
  63.3 5.9 %collective-permute-done.2 = bf16[512,512]{1,0:T(8,128)(2,1)S(1)} collective-permute-done((bf16[512,512]{1,0:T(8,128)(2,1)S(1)}, bf16[512,512]{1,0:T(8,128)(2,1)S(1)}, u32[]{:S(2)}, u32[]{:S(2)}) %collective-permute-start.2) | collective-permute-done | bytes 524320 | tf_op jit(solution)/shard_map/cond/branch_1_fun/ppermute | solution.py:96
  69.2 1.6 %pad_maximum_fusion = bf16[4,512,512]{2,1,0:T(8,128)(2,1)} fusion(bf16[1,512,512]{2,1,0:T(8,128)(2,1)S(1)} %bitcast.33, bf16[1,512,512]{2,1,0:T(8,128)(2,1)S(1)} %bitcast.32, bf16[1,512,512]{2,1,0:T(8,128)(2,1)S(1)} %bitcast.31, bf16[1,512,512]{2,1,0:T(8,128)(2,1)S(1)} %bitcast.30), kind=kLoop, calls=%fused_computation | loop fusion | flops 3145728 | bytes 4194304 | tf_op jit(solution)/shard_map/cond/branch_1_fun/stack | solution.py:97
  70.8 4.3 %collective-permute-start.3 = (bf16[4,512,512]{2,1,0:T(8,128)(2,1)}, bf16[4,512,512]{2,1,0:T(8,128)(2,1)}, u32[]{:S(2)}, u32[]{:S(2)}) collective-permute-start(bf16[4,512,512]{2,1,0:T(8,128)(2,1)} %pad_maximum_fusion), channel_id=1, source_target_pairs={{0,1},{1,0},{2,3},{3,2},{4,5},{5,4},{6,7},{7,6},{8,9},{9,8},{10,11... | collective-permute-start | bytes 6291464 | tf_op jit(solution)/shard_map/cond/branch_1_fun/ppermute | solution.py:98
  75.1 4.1 %collective-permute-done.3 = bf16[4,512,512]{2,1,0:T(8,128)(2,1)} collective-permute-done((bf16[4,512,512]{2,1,0:T(8,128)(2,1)}, bf16[4,512,512]{2,1,0:T(8,128)(2,1)}, u32[]{:S(2)}, u32[]{:S(2)}) %collective-permute-start.3) | collective-permute-done | bytes 2097184 | tf_op jit(solution)/shard_map/cond/branch_1_fun/ppermute | solution.py:98
  79.2 0.0 collective-permute-done.4.refs_1_
  79.3 0.0 copy-start
  79.3 0.7 copy-done
  80.0 4.7 %shard_map.95 = f32[8,32]{1,0:T(8,128)} custom-call(bf16[264,512]{1,0:T(8,128)(2,1)} %shard_map.94.refs_0_, bf16[264,512]{1,0:T(8,128)(2,1)} %copy-done, bf16[4,512,512]{2,1,0:T(8,128)(2,1)} %get-tuple-element.25.refs_2_, bf16[4,512,512]{2,1,0:T(8,128)(2,1)} %get-tuple-element.26.refs_3_), custom_call_target="tpu_custom_call" | custom-call | tf_op jit(solution)/shard_map/pallas_call | solution.py:76
  84.7 0.8 select_reduce_fusion
  85.4 11.7 %all_to_all.15 = f32[32,1,32]{2,1,0:T(1,128)S(1)} all-to-all(f32[32,1,32]{2,1,0:T(1,128)S(1)} %bitcast.36), channel_id=1, replica_groups=mesh['zlo'=16,'y'=4,'zhi'=2,'x'=4,'core'=2] {'y','x','core'}, dimensions={0} | all-to-all | bytes 8192 | tf_op jit(solution)/shard_map/all_to_all | solution.py:137
  97.2 0.1 reduce_sum.28
  97.2 0.6 broadcast_in_dim.48
  97.8 17.2 %all-to-all-start.1 = ((f32[16,1,32]{2,1,0:T(1,128)}), f32[16,1,32]{2,1,0:T(1,128)S(1)}, u32[]{:S(2)}, u32[]{:S(2)}) async-start(f32[16,1,32]{2,1,0:T(1,128)} %broadcast_in_dim.48), calls=%async_computation.1 | async-start | bytes 16384 | tf_op jit(solution)/shard_map/all_to_all | solution.py:139
  115.7 18.1 %all-to-all-done.1 = f32[16,1,32]{2,1,0:T(1,128)S(1)} async-done(((f32[16,1,32]{2,1,0:T(1,128)}), f32[16,1,32]{2,1,0:T(1,128)S(1)}, u32[]{:S(2)}, u32[]{:S(2)}) %all-to-all-start.1) | async-done | bytes 2080 | tf_op jit(solution)/shard_map/all_to_all | solution.py:139
  133.8 0.5 compare_select_fusion
  (4 shorter events, 0.0 us)
Async XLA Ops:
  2.4 76.9 %collective-permute-start.4 = (bf16[264,512]{1,0:T(8,128)(2,1)}, bf16[264,512]{1,0:T(8,128)(2,1)S(1)}, u32[]{:S(2)}, u32[]{:S(2)}) collective-permute-start(bf16[264,512]{1,0:T(8,128)(2,1)} %shard_map.94.refs_0_), channel_id=1, source_target_pairs={{0,8},{8,0},{1,9},{9,1},{2,10},{10,2},{3,11},{11,3},{4,12},{12,4},... | collective-permute-start | bytes 811016 | tf_op jit(solution)/shard_map/ppermute | solution.py:121
  35.5 14.4 %collective-permute-start = (bf16[512,512]{1,0:T(8,128)(2,1)S(1)}, bf16[512,512]{1,0:T(8,128)(2,1)S(1)}, u32[]{:S(2)}, u32[]{:S(2)}) collective-permute-start(bf16[512,512]{1,0:T(8,128)(2,1)S(1)} %fusion), channel_id=1, source_target_pairs={{0,2},{2,0},{4,6},{6,4},{1,3},{3,1},{5,7},{7,5},{8,10},{10,8},{12,... | collective-permute-start | bytes 1572872 | tf_op jit(solution)/shard_map/cond/branch_1_fun/ppermute | solution.py:96
  38.6 24.7 %collective-permute-start.1 = (bf16[512,512]{1,0:T(8,128)(2,1)S(1)}, bf16[512,512]{1,0:T(8,128)(2,1)S(1)}, u32[]{:S(2)}, u32[]{:S(2)}) collective-permute-start(bf16[512,512]{1,0:T(8,128)(2,1)S(1)} %fusion), channel_id=1, source_target_pairs={{0,4},{2,6},{4,0},{6,2},{1,5},{3,7},{5,1},{7,3},{8,12},{10,14},{12... | collective-permute-start | bytes 1572872 | tf_op jit(solution)/shard_map/cond/branch_1_fun/ppermute | solution.py:96
  42.9 26.2 %collective-permute-start.2 = (bf16[512,512]{1,0:T(8,128)(2,1)S(1)}, bf16[512,512]{1,0:T(8,128)(2,1)S(1)}, u32[]{:S(2)}, u32[]{:S(2)}) collective-permute-start(bf16[512,512]{1,0:T(8,128)(2,1)S(1)} %fusion), channel_id=1, source_target_pairs={{0,6},{2,4},{4,2},{6,0},{1,7},{3,5},{5,3},{7,1},{8,14},{10,12},{12... | collective-permute-start | bytes 1572872 | tf_op jit(solution)/shard_map/cond/branch_1_fun/ppermute | solution.py:96
  70.8 8.4 %collective-permute-start.3 = (bf16[4,512,512]{2,1,0:T(8,128)(2,1)}, bf16[4,512,512]{2,1,0:T(8,128)(2,1)}, u32[]{:S(2)}, u32[]{:S(2)}) collective-permute-start(bf16[4,512,512]{2,1,0:T(8,128)(2,1)} %pad_maximum_fusion), channel_id=1, source_target_pairs={{0,1},{1,0},{2,3},{3,2},{4,5},{5,4},{6,7},{7,6},{8,9},{9,8},{10,11... | collective-permute-start | bytes 6291464 | tf_op jit(solution)/shard_map/cond/branch_1_fun/ppermute | solution.py:98
  79.3 0.7 copy-start
  97.8 36.0 %all-to-all-start.1 = ((f32[16,1,32]{2,1,0:T(1,128)}), f32[16,1,32]{2,1,0:T(1,128)S(1)}, u32[]{:S(2)}, u32[]{:S(2)}) async-start(f32[16,1,32]{2,1,0:T(1,128)} %broadcast_in_dim.48), calls=%async_computation.1 | async-start | bytes 16384 | tf_op jit(solution)/shard_map/all_to_all | solution.py:139

commit v4 on v2

--- a/solution.py
+++ b/solution.py
@@ -45,24 +45,25 @@
     )(train_ids, train_in, train_out, in_basis, out_basis)
 
 
-def score_kernel(packed_ref, *refs, length, columns):
-    out_ref = refs[-1]
-    tokens = (packed_ref.shape[0] - EXTRA) // 2
+def score_kernel(*refs, length, columns):
+    packed_refs, precond_refs, out_ref = refs[:4], refs[4:-1], refs[-1]
+    tokens = (packed_refs[0].shape[0] - EXTRA) // 2
     seqs = tokens // length
-    inside = packed_ref[:tokens].astype(jnp.float32)
-    outside = packed_ref[tokens : 2 * tokens]
-    hot = packed_ref[2 * tokens :].astype(jnp.float32)
-    rows = [[] for _ in range(seqs)]
-    for ref in refs[:-1]:
-        weighted = jnp.dot(outside, ref[...], preferred_element_type=jnp.float32)
-        prod = weighted * inside
+    total = None
+    for packed_ref in packed_refs:
+        inside = packed_ref[:tokens].astype(jnp.float32)
+        outside = packed_ref[tokens : 2 * tokens]
+        hot = packed_ref[2 * tokens :].astype(jnp.float32)
+        rows = [[] for _ in range(seqs)]
+        for ref in precond_refs:
+            prod = inside * jnp.dot(outside, ref[...], preferred_element_type=jnp.float32)
+            for s in range(seqs):
+                part = prod[s * length : (s + 1) * length]
+                rows[s].append(jnp.sum(part, axis=0, keepdims=True))
         for s in range(seqs):
-            rows[s].append(jnp.sum(prod[s * length : (s + 1) * length], axis=0, keepdims=True))
-    total = None
-    for s in range(seqs):
-        sums = jnp.sum(jnp.concatenate(rows[s], axis=0), axis=1, keepdims=True)
-        placed = sums * hot[s : s + 1, :columns]
-        total = placed if total is None else total + placed
+            sums = jnp.sum(jnp.concatenate(rows[s], axis=0), axis=1, keepdims=True)
+            placed = sums * hot[s : s + 1, :columns]
+            total = placed if total is None else total + placed
     out_ref[...] = total
 
 
@@ -70,26 +71,20 @@
     return pl.pallas_call(
         lambda *refs: score_kernel(*refs, length=length, columns=columns),
         out_shape=jax.ShapeDtypeStruct((len(preconds), columns), jnp.float32),
-        in_specs=[VMEM] * (1 + len(preconds)),
+        in_specs=[VMEM] * (len(packed) + len(preconds)),
         out_specs=VMEM,
         compiler_params=pltpu.CompilerParams(vmem_limit_bytes=40 << 20),
-    )(packed, *preconds)
+    )(*packed, *preconds)
 
 
-def gather_preconds(query_in, query_out, in_basis, out_basis, eigen_values, mine, length, columns):
+def precondition(query_in, query_out, in_basis, out_basis, eigen_values):
     side_in = project(query_in, in_basis)
     side_out = project(query_out, out_basis)
     moment = lax.dot_general(
         side_out, side_in, (((0,), (0,)), ((), ())), preferred_element_type=jnp.float32
     )
     scale = query_in.shape[0] * (eigen_values + damping)
-    precond = (moment / scale).astype(jnp.bfloat16)
-    along = [precond]
-    for step in range(1, X):
-        along.append(lax.ppermute(precond, "x", [(i, i ^ step) for i in range(X)]))
-    beside = [lax.ppermute(p, "core", SWAP) for p in along]
-    preconds = along + beside
-    return preconds, scores_of(mine, preconds, length, columns)
+    return (moment / scale).astype(jnp.bfloat16)
 
 
 def local(
@@ -113,26 +108,20 @@
         train_ids, train_in[0].reshape(tokens), train_out[0].reshape(tokens), in_basis, out_basis
     )
     theirs = lax.ppermute(mine, "zhi", SWAP)
-    preconds, partial_mine = lax.cond(
-        lax.axis_index("x") < X,
-        lambda *ops: gather_preconds(*ops, length, columns),
-        lambda *ops: (
-            [jnp.zeros((width, width), jnp.bfloat16)] * (X * CORE),
-            jnp.zeros((X * CORE, columns), jnp.float32),
-        ),
-        query_in[0, 0], query_out[0, 0], in_basis, out_basis, eigen_values[0], mine,
-    )
-    partial_theirs = scores_of(theirs, preconds, length, columns)
-    partial_value = partial_mine + partial_theirs
+    packed = [mine, lax.ppermute(mine, "core", SWAP), theirs, lax.ppermute(theirs, "core", SWAP)]
+    precond = precondition(query_in[0, 0], query_out[0, 0], in_basis, out_basis, eigen_values[0])
+    preconds = [precond]
+    for step in range(1, X):
+        preconds.append(lax.ppermute(precond, "x", [(i, i ^ step) for i in range(X)]))
+    partial_value = scores_of(packed, preconds, length, columns)
 
-    k = jnp.arange(X * CORE, dtype=jnp.int32)
-    owner = (lax.axis_index("x") ^ (k % X)) * CORE + (lax.axis_index("core") ^ (k // X))
-    order = owner[None, :] == k[:, None]
+    k = jnp.arange(X, dtype=jnp.int32)
+    order = (lax.axis_index("x") ^ k)[None, :] == k[:, None]
     ordered = jnp.sum(
         jnp.where(order[:, :, None], partial_value[None, :, :], 0.0), axis=1
     )
-    spread = jnp.broadcast_to(ordered[None], (Y,) + ordered.shape).reshape(Y * X * CORE, -1)
-    near = jnp.sum(lax.all_to_all(spread, ("y", "x", "core"), 0, 0), axis=0)
+    spread = jnp.broadcast_to(ordered[None], (Y,) + ordered.shape).reshape(Y * X, -1)
+    near = jnp.sum(lax.all_to_all(spread, ("y", "x"), 0, 0), axis=0)
     far = jnp.broadcast_to(near[None], (ZLO,) + near.shape)
     summed = jnp.sum(lax.all_to_all(far, "zlo", 0, 0), axis=0)
     factor = 1.0 / math.sqrt(ZLO * Y * in_basis.shape[0] * out_basis.shape[0])

time: 132 us -> 133 us (level)
  waiting for transfers between devices: 31.6 us -> 36.5 us
  Pallas kernels: 8.49 us -> 3.88 us
  starting transfers between devices: 74.8 us -> 78.2 us
    all_to_all x1, starting transfers between devices: 18.5 us -> 33.3 us  [local(): summed = jnp.sum(lax.all_to_all(far, 'zlo', 0, 0), axis=0)]
    ppermute x7 -> x5, starting transfers between devices: 26.7 us -> 15.2 us  [the longest x3 9.58 us: local(): lax.ppermute(precond, 'x', [(i, i ^ step) for i in range(X)])]
    ppermute x7 -> x5, waiting for transfers between devices: 13.5 us -> 18.4 us  [the longest x3 18.4 us: local(): lax.ppermute(precond, 'x', [(i, i ^ step) for i in range(X)])]
    pallas_call x2 -> x1, Pallas kernels: 5.99 us -> 1.36 us  [scores_of(): pl.pallas_call(lambda *refs: score_kernel(*refs, length=length, columns=c...]
  transfers between devices with their start and end apart: 9 -> 7, of which waited for: 5 -> 3; matrix products, arithmetic and copies ran while one was open for 1% -> 1% of each run, Pallas kernels for 2% -> 0%
where the time goes in v4:
time: 133 us; the launch traced here: 132 us
  starting transfers between devices  78.2 us (59%)
  waiting for transfers between devices  36.5 us (27%)
  blocking collectives  10.5 us (8%)
  Pallas kernels  3.88 us (3%)
    all_to_all x1, starting transfers between devices, local(): summed = jnp.sum(lax.all_to_all(far, 'zlo', 0, 0), axis=0)  33.3 us
    ppermute x1, starting transfers between devices, local(): theirs = lax.ppermute(mine, 'zhi', SWAP)  29.6 us
    ppermute x3, waiting for transfers between devices, local(): lax.ppermute(precond, 'x', [(i, i ^ step) for i in range(X)])  18.4 us
    all_to_all x1, waiting for transfers between devices, local(): summed = jnp.sum(lax.all_to_all(far, 'zlo', 0, 0), axis=0)  18.1 us
    all_to_all x1, blocking collectives, local(): near = jnp.sum(lax.all_to_all(spread, ('y', 'x'), 0, 0), axis=0)  10.5 us
    ppermute x3, starting transfers between devices, local(): lax.ppermute(precond, 'x', [(i, i ^ step) for i in range(X)])  9.58 us
    ppermute x1, starting transfers between devices, local(): lax.ppermute(mine, 'core', SWAP)  3.7 us
  transfers between devices with their start and end apart: 7, of which 3 were waited for; matrix products, arithmetic and copies ran while one was open for 1% of the time, Pallas kernels for 0%

profile of v4, /device:TPU:1, one launch (start us, length us, event | category | flops | bytes accessed | tf_op | source)
XLA Modules:
  0.0 132.1 jit_solution(1442301377483415263)
XLA Ops:
  0.0 0.0 copy-start
  0.0 0.0 copy-start.2
  0.0 0.0 copy-start.4
  0.0 0.0 copy-start.5
  0.0 2.5 %shard_map.91.refs_0_ = bf16[264,512]{1,0:T(8,128)(2,1)} custom-call(s32[2]{0:T(128)} %ids_ref.1, f32[128,512]{1,0:T(8,128)} %bitcast.27, f32[128,512]{1,0:T(8,128)} %bitcast.28, bf16[512,512]{1,0:T(8,128)(2,1)} %bitcast.25, bf16[512,512]{1,0:T(8,128)(2,1)} %bitcast.26), custom_call_target="tpu_custom_call" | custom-call | tf_op jit(solution)/shard_map/pallas_call | solution.py:40
  2.5 0.0 copy-start.3
  2.5 29.6 %collective-permute-start.1 = (bf16[264,512]{1,0:T(8,128)(2,1)}, bf16[264,512]{1,0:T(8,128)(2,1)S(1)}, u32[]{:S(2)}, u32[]{:S(2)}) collective-permute-start(bf16[264,512]{1,0:T(8,128)(2,1)} %shard_map.91.refs_0_), channel_id=1, source_target_pairs={{0,8},{8,0},{1,9},{9,1},{2,10},{10,2},{3,11},{11,3},{4,12},{12,4},... | collective-permute-start | bytes 811016 | tf_op jit(solution)/shard_map/ppermute | solution.py:110
  32.2 0.0 copy-done.2
  32.2 0.0 copy-done.4
  32.2 0.3 convolution_convert_fusion
  32.5 0.0 copy-done
  32.5 0.0 copy-done.5
  32.5 0.0 copy-done.3
  32.6 0.0 copy-start.1
  32.6 0.6 fusion.refs_4_
  33.2 3.1 %collective-permute-start.3 = (bf16[512,512]{1,0:T(8,128)(2,1)S(1)}, bf16[512,512]{1,0:T(8,128)(2,1)S(1)}, u32[]{:S(2)}, u32[]{:S(2)}) collective-permute-start(bf16[512,512]{1,0:T(8,128)(2,1)S(1)} %fusion.refs_4_), channel_id=1, source_target_pairs={{0,2},{2,0},{4,6},{6,4},{1,3},{3,1},{5,7},{7,5},{8,10},{10,8},{12,... | collective-permute-start | bytes 1572872 | tf_op jit(solution)/shard_map/ppermute | solution.py:115
  36.3 4.4 %collective-permute-start.4 = (bf16[512,512]{1,0:T(8,128)(2,1)S(1)}, bf16[512,512]{1,0:T(8,128)(2,1)S(1)}, u32[]{:S(2)}, u32[]{:S(2)}) collective-permute-start(bf16[512,512]{1,0:T(8,128)(2,1)S(1)} %fusion.refs_4_), channel_id=1, source_target_pairs={{0,4},{2,6},{4,0},{6,2},{1,5},{3,7},{5,1},{7,3},{8,12},{10,14},{12... | collective-permute-start | bytes 1572872 | tf_op jit(solution)/shard_map/ppermute | solution.py:115
  40.7 2.1 %collective-permute-start.5 = (bf16[512,512]{1,0:T(8,128)(2,1)S(1)}, bf16[512,512]{1,0:T(8,128)(2,1)S(1)}, u32[]{:S(2)}, u32[]{:S(2)}) collective-permute-start(bf16[512,512]{1,0:T(8,128)(2,1)S(1)} %fusion.refs_4_), channel_id=1, source_target_pairs={{0,6},{2,4},{4,2},{6,0},{1,7},{3,5},{5,3},{7,1},{8,14},{10,12},{12... | collective-permute-start | bytes 1572872 | tf_op jit(solution)/shard_map/ppermute | solution.py:115
  42.8 0.0 copy-done.1
  42.8 3.7 %collective-permute-start = (bf16[264,512]{1,0:T(8,128)(2,1)S(1)}, bf16[264,512]{1,0:T(8,128)(2,1)S(1)}, u32[]{:S(2)}, u32[]{:S(2)}) collective-permute-start(bf16[264,512]{1,0:T(8,128)(2,1)S(1)} %copy-done.1), channel_id=1, source_target_pairs={{0,1},{1,0},{2,3},{3,2},{4,5},{5,4},{6,7},{7,6},{8,9},{9,8},{10,11... | collective-permute-start | bytes 811016 | tf_op jit(solution)/shard_map/ppermute | solution.py:111
  46.5 0.0 collective-permute-done.1.refs_2_
  46.5 1.9 %collective-permute-start.2 = (bf16[264,512]{1,0:T(8,128)(2,1)S(1)}, bf16[264,512]{1,0:T(8,128)(2,1)S(1)}, u32[]{:S(2)}, u32[]{:S(2)}) collective-permute-start(bf16[264,512]{1,0:T(8,128)(2,1)S(1)} %collective-permute-done.1.refs_2_), channel_id=1, source_target_pairs={{0,1},{1,0},{2,3},{3,2},{4,5},{5,4},{6,7},{7,6},{8,9},{9,8},{10,11... | collective-permute-start | bytes 811016 | tf_op jit(solution)/shard_map/ppermute | solution.py:111
  48.5 0.0 collective-permute-done.refs_1_
  48.5 0.0 collective-permute-done.3.refs_5_
  48.5 12.5 %collective-permute-done.4.refs_6_ = bf16[512,512]{1,0:T(8,128)(2,1)S(1)} collective-permute-done((bf16[512,512]{1,0:T(8,128)(2,1)S(1)}, bf16[512,512]{1,0:T(8,128)(2,1)S(1)}, u32[]{:S(2)}, u32[]{:S(2)}) %collective-permute-start.4) | collective-permute-done | bytes 524320 | tf_op jit(solution)/shard_map/ppermute | solution.py:115
  61.0 5.9 %collective-permute-done.5.refs_7_ = bf16[512,512]{1,0:T(8,128)(2,1)S(1)} collective-permute-done((bf16[512,512]{1,0:T(8,128)(2,1)S(1)}, bf16[512,512]{1,0:T(8,128)(2,1)S(1)}, u32[]{:S(2)}, u32[]{:S(2)}) %collective-permute-start.5) | collective-permute-done | bytes 524320 | tf_op jit(solution)/shard_map/ppermute | solution.py:115
  66.9 0.0 collective-permute-done.2.refs_3_
  66.9 1.4 %shard_map.92 = f32[4,32]{1,0:T(4,128)S(1)} custom-call(bf16[264,512]{1,0:T(8,128)(2,1)S(1)} %copy-done.1, bf16[264,512]{1,0:T(8,128)(2,1)S(1)} %collective-permute-done.refs_1_, bf16[264,512]{1,0:T(8,128)(2,1)S(1)} %collective-permute-done.1.refs_2_, bf16[264,512]{1,0:T(8,128)(2,1)S(1)} %collective-permute-done.2.refs_3_, ...), custom_call_target="tpu_custom_call" | custom-call | tf_op jit(solution)/shard_map/pallas_call | solution.py:71
  68.3 0.1 select_reduce_fusion
  68.4 10.5 %all_to_all.15 = f32[16,1,32]{2,1,0:T(1,128)S(1)} all-to-all(f32[16,1,32]{2,1,0:T(1,128)S(1)} %bitcast.29), channel_id=1, replica_groups=mesh['zlo'=16,'y'=4,'zhi'=2,'x'=4,'core'=2] {'y','x'}, dimensions={0} | all-to-all | bytes 4096 | tf_op jit(solution)/shard_map/all_to_all | solution.py:124
  78.9 0.6 broadcast_in_dim.48
  79.5 33.3 %all-to-all-start.1 = ((f32[16,1,32]{2,1,0:T(1,128)}), f32[16,1,32]{2,1,0:T(1,128)S(1)}, u32[]{:S(2)}, u32[]{:S(2)}) async-start(f32[16,1,32]{2,1,0:T(1,128)} %broadcast_in_dim.48), calls=%async_computation.1 | async-start | bytes 16384 | tf_op jit(solution)/shard_map/all_to_all | solution.py:126
  113.5 18.1 %all-to-all-done.1 = f32[16,1,32]{2,1,0:T(1,128)S(1)} async-done(((f32[16,1,32]{2,1,0:T(1,128)}), f32[16,1,32]{2,1,0:T(1,128)S(1)}, u32[]{:S(2)}, u32[]{:S(2)}) %all-to-all-start.1) | async-done | bytes 2080 | tf_op jit(solution)/shard_map/all_to_all | solution.py:126
  131.6 0.5 compare_select_fusion
  (5 shorter events, 0.1 us)
Async XLA Ops:
  0.0 32.5 %copy-start = (bf16[1,1,256,512]{3,2,1,0:T(8,128)(2,1)S(1)}, bf16[1,1,256,512]{3,2,1,0:T(8,128)(2,1)}, u32[]{:S(2)}) copy-start(bf16[1,1,256,512]{3,2,1,0:T(8,128)(2,1)} %param.12) | copy-start | bytes 786436
  0.0 32.2 %copy-start.2 = (bf16[1,512,512]{2,1,0:T(8,128)(2,1)S(1)}, bf16[1,512,512]{2,1,0:T(8,128)(2,1)}, u32[]{:S(2)}) copy-start(bf16[1,512,512]{2,1,0:T(8,128)(2,1)} %param.13) | copy-start | bytes 1572868
  0.0 32.2 %copy-start.4 = (bf16[1,1,256,512]{3,2,1,0:T(8,128)(2,1)S(1)}, bf16[1,1,256,512]{3,2,1,0:T(8,128)(2,1)}, u32[]{:S(2)}) copy-start(bf16[1,1,256,512]{3,2,1,0:T(8,128)(2,1)} %param.11) | copy-start | bytes 786436
  0.0 32.5 %copy-start.5 = (f32[1,512,512]{2,1,0:T(8,128)S(1)}, f32[1,512,512]{2,1,0:T(8,128)}, u32[]{:S(2)}) copy-start(f32[1,512,512]{2,1,0:T(8,128)} %param.15) | copy-start | bytes 3145732
  2.5 30.0 %copy-start.3 = (bf16[1,512,512]{2,1,0:T(8,128)(2,1)S(1)}, bf16[1,512,512]{2,1,0:T(8,128)(2,1)}, u32[]{:S(2)}) copy-start(bf16[1,512,512]{2,1,0:T(8,128)(2,1)} %param.14) | copy-start | bytes 1572868
  2.5 44.0 %collective-permute-start.1 = (bf16[264,512]{1,0:T(8,128)(2,1)}, bf16[264,512]{1,0:T(8,128)(2,1)S(1)}, u32[]{:S(2)}, u32[]{:S(2)}) collective-permute-start(bf16[264,512]{1,0:T(8,128)(2,1)} %shard_map.91.refs_0_), channel_id=1, source_target_pairs={{0,8},{8,0},{1,9},{9,1},{2,10},{10,2},{3,11},{11,3},{4,12},{12,4},... | collective-permute-start | bytes 811016 | tf_op jit(solution)/shard_map/ppermute | solution.py:110
  32.6 10.2 %copy-start.1 = (bf16[264,512]{1,0:T(8,128)(2,1)S(1)}, bf16[264,512]{1,0:T(8,128)(2,1)}, u32[]{:S(2)}) copy-start(bf16[264,512]{1,0:T(8,128)(2,1)} %shard_map.91.refs_0_) | copy-start | bytes 811012
  33.2 15.3 %collective-permute-start.3 = (bf16[512,512]{1,0:T(8,128)(2,1)S(1)}, bf16[512,512]{1,0:T(8,128)(2,1)S(1)}, u32[]{:S(2)}, u32[]{:S(2)}) collective-permute-start(bf16[512,512]{1,0:T(8,128)(2,1)S(1)} %fusion.refs_4_), channel_id=1, source_target_pairs={{0,2},{2,0},{4,6},{6,4},{1,3},{3,1},{5,7},{7,5},{8,10},{10,8},{12,... | collective-permute-start | bytes 1572872 | tf_op jit(solution)/shard_map/ppermute | solution.py:115
  36.3 24.7 %collective-permute-start.4 = (bf16[512,512]{1,0:T(8,128)(2,1)S(1)}, bf16[512,512]{1,0:T(8,128)(2,1)S(1)}, u32[]{:S(2)}, u32[]{:S(2)}) collective-permute-start(bf16[512,512]{1,0:T(8,128)(2,1)S(1)} %fusion.refs_4_), channel_id=1, source_target_pairs={{0,4},{2,6},{4,0},{6,2},{1,5},{3,7},{5,1},{7,3},{8,12},{10,14},{12... | collective-permute-start | bytes 1572872 | tf_op jit(solution)/shard_map/ppermute | solution.py:115
  40.7 26.2 %collective-permute-start.5 = (bf16[512,512]{1,0:T(8,128)(2,1)S(1)}, bf16[512,512]{1,0:T(8,128)(2,1)S(1)}, u32[]{:S(2)}, u32[]{:S(2)}) collective-permute-start(bf16[512,512]{1,0:T(8,128)(2,1)S(1)} %fusion.refs_4_), channel_id=1, source_target_pairs={{0,6},{2,4},{4,2},{6,0},{1,7},{3,5},{5,3},{7,1},{8,14},{10,12},{12... | collective-permute-start | bytes 1572872 | tf_op jit(solution)/shard_map/ppermute | solution.py:115
  42.8 5.7 %collective-permute-start = (bf16[264,512]{1,0:T(8,128)(2,1)S(1)}, bf16[264,512]{1,0:T(8,128)(2,1)S(1)}, u32[]{:S(2)}, u32[]{:S(2)}) collective-permute-start(bf16[264,512]{1,0:T(8,128)(2,1)S(1)} %copy-done.1), channel_id=1, source_target_pairs={{0,1},{1,0},{2,3},{3,2},{4,5},{5,4},{6,7},{7,6},{8,9},{9,8},{10,11... | collective-permute-start | bytes 811016 | tf_op jit(solution)/shard_map/ppermute | solution.py:111
  46.5 20.4 %collective-permute-start.2 = (bf16[264,512]{1,0:T(8,128)(2,1)S(1)}, bf16[264,512]{1,0:T(8,128)(2,1)S(1)}, u32[]{:S(2)}, u32[]{:S(2)}) collective-permute-start(bf16[264,512]{1,0:T(8,128)(2,1)S(1)} %collective-permute-done.1.refs_2_), channel_id=1, source_target_pairs={{0,1},{1,0},{2,3},{3,2},{4,5},{5,4},{6,7},{7,6},{8,9},{9,8},{10,11... | collective-permute-start | bytes 811016 | tf_op jit(solution)/shard_map/ppermute | solution.py:111
  79.5 52.0 %all-to-all-start.1 = ((f32[16,1,32]{2,1,0:T(1,128)}), f32[16,1,32]{2,1,0:T(1,128)S(1)}, u32[]{:S(2)}, u32[]{:S(2)}) async-start(f32[16,1,32]{2,1,0:T(1,128)} %broadcast_in_dim.48), calls=%async_computation.1 | async-start | bytes 16384 | tf_op jit(solution)/shard_map/all_to_all | solution.py:126

commit v5 on v2

--- a/solution.py
+++ b/solution.py
@@ -13,6 +13,7 @@
 ZLO, Y, ZHI, X, CORE = 16, 4, 2, 4, 2
 NAMES = ("zlo", "y", "zhi", "x", "core")
 SWAP = [(0, 1), (1, 0)]
+LANES = 128
 EXTRA = 8
 
 VMEM = pl.BlockSpec(memory_space=pltpu.VMEM)
@@ -24,38 +25,41 @@
 
 
 def train_kernel(ids_ref, in_ref, out_ref, in_basis_ref, out_basis_ref, packed_ref):
-    tokens = in_ref.shape[0]
-    packed_ref[:tokens] = project(in_ref[...].astype(jnp.bfloat16), in_basis_ref[...])
-    packed_ref[tokens : 2 * tokens] = project(out_ref[...].astype(jnp.bfloat16), out_basis_ref[...])
-    row = lax.broadcasted_iota(jnp.int32, (EXTRA, in_ref.shape[1]), 0)
-    lane = lax.broadcasted_iota(jnp.int32, (EXTRA, in_ref.shape[1]), 1)
+    tokens, width = in_ref.shape
+    inside = project(in_ref[...].astype(jnp.bfloat16), in_basis_ref[...])
+    outside = project(out_ref[...].astype(jnp.bfloat16), out_basis_ref[...])
+    for at, side in ((0, inside), (width // LANES, outside)):
+        for c in range(width // LANES):
+            packed_ref[(at + c) * tokens : (at + c + 1) * tokens] = side[:, c * LANES : (c + 1) * LANES]
+    row = lax.broadcasted_iota(jnp.int32, (EXTRA, LANES), 0)
+    lane = lax.broadcasted_iota(jnp.int32, (EXTRA, LANES), 1)
     hit = (row == 0) & (lane == ids_ref[0])
     for s in range(1, ids_ref.shape[0]):
         hit = hit | ((row == s) & (lane == ids_ref[s]))
-    packed_ref[2 * tokens :] = jnp.where(hit, 1.0, 0.0).astype(jnp.bfloat16)
+    packed_ref[packed_ref.shape[0] - EXTRA :] = jnp.where(hit, 1.0, 0.0).astype(jnp.bfloat16)
 
 
 def pack_train(train_ids, train_in, train_out, in_basis, out_basis):
     tokens, width = train_in.shape
     return pl.pallas_call(
         train_kernel,
-        out_shape=jax.ShapeDtypeStruct((2 * tokens + EXTRA, width), jnp.bfloat16),
+        out_shape=jax.ShapeDtypeStruct((2 * tokens * width // LANES + EXTRA, LANES), jnp.bfloat16),
         in_specs=[SMEM] + [VMEM] * 4,
         out_specs=VMEM,
     )(train_ids, train_in, train_out, in_basis, out_basis)
 
 
-def score_kernel(packed_ref, *refs, length, columns):
-    out_ref = refs[-1]
-    tokens = (packed_ref.shape[0] - EXTRA) // 2
+def packed_scores(packed_ref, preconds, length, columns):
+    end = packed_ref.shape[0] - EXTRA
+    tokens = end * LANES // (2 * preconds[0].shape[0])
     seqs = tokens // length
-    inside = packed_ref[:tokens].astype(jnp.float32)
-    outside = packed_ref[tokens : 2 * tokens]
-    hot = packed_ref[2 * tokens :].astype(jnp.float32)
+    blocks = [packed_ref[at : at + tokens] for at in range(0, end, tokens)]
+    inside = jnp.concatenate(blocks[: len(blocks) // 2], axis=1).astype(jnp.float32)
+    outside = jnp.concatenate(blocks[len(blocks) // 2 :], axis=1)
+    hot = packed_ref[end:].astype(jnp.float32)
     rows = [[] for _ in range(seqs)]
-    for ref in refs[:-1]:
-        weighted = jnp.dot(outside, ref[...], preferred_element_type=jnp.float32)
-        prod = weighted * inside
+    for precond in preconds:
+        prod = inside * jnp.dot(outside, precond[...], preferred_element_type=jnp.float32)
         for s in range(seqs):
             rows[s].append(jnp.sum(prod[s * length : (s + 1) * length], axis=0, keepdims=True))
     total = None
@@ -63,20 +67,45 @@
         sums = jnp.sum(jnp.concatenate(rows[s], axis=0), axis=1, keepdims=True)
         placed = sums * hot[s : s + 1, :columns]
         total = placed if total is None else total + placed
-    out_ref[...] = total
+    return total
 
 
-def scores_of(packed, preconds, length, columns):
+def first_scores(packed, preconds, length, columns):
+    count = len(preconds)
+
+    def kernel(packed_ref, *refs):
+        stack_ref, out_ref = refs[-2:]
+        out_ref[...] = packed_scores(packed_ref, refs[:count], length, columns)
+        for q in range(count):
+            stack_ref[q] = refs[q][...]
+
     return pl.pallas_call(
-        lambda *refs: score_kernel(*refs, length=length, columns=columns),
-        out_shape=jax.ShapeDtypeStruct((len(preconds), columns), jnp.float32),
-        in_specs=[VMEM] * (1 + len(preconds)),
-        out_specs=VMEM,
+        kernel,
+        out_shape=[
+            jax.ShapeDtypeStruct((count,) + preconds[0].shape, jnp.bfloat16),
+            jax.ShapeDtypeStruct((count, columns), jnp.float32),
+        ],
+        in_specs=[VMEM] * (1 + count),
+        out_specs=[VMEM] * 2,
         compiler_params=pltpu.CompilerParams(vmem_limit_bytes=40 << 20),
     )(packed, *preconds)
 
 
-def gather_preconds(query_in, query_out, in_basis, out_basis, eigen_values, mine, length, columns):
+def last_scores(packed, stack, before, length, columns):
+    def kernel(packed_ref, stack_ref, before_ref, out_ref):
+        preconds = [stack_ref.at[q] for q in range(stack_ref.shape[0])]
+        out_ref[...] = before_ref[...] + packed_scores(packed_ref, preconds, length, columns)
+
+    return pl.pallas_call(
+        kernel,
+        out_shape=jax.ShapeDtypeStruct(before.shape, jnp.float32),
+        in_specs=[VMEM] * 3,
+        out_specs=VMEM,
+        compiler_params=pltpu.CompilerParams(vmem_limit_bytes=40 << 20),
+    )(packed, stack, before)
+
+
+def gather_preconds(query_in, query_out, in_basis, out_basis, eigen_values):
     side_in = project(query_in, in_basis)
     side_out = project(query_out, out_basis)
     moment = lax.dot_general(
@@ -88,8 +117,7 @@
     for step in range(1, X):
         along.append(lax.ppermute(precond, "x", [(i, i ^ step) for i in range(X)]))
     beside = [lax.ppermute(p, "core", SWAP) for p in along]
-    preconds = along + beside
-    return preconds, scores_of(mine, preconds, length, columns)
+    return along + beside
 
 
 def local(
@@ -113,17 +141,14 @@
         train_ids, train_in[0].reshape(tokens), train_out[0].reshape(tokens), in_basis, out_basis
     )
     theirs = lax.ppermute(mine, "zhi", SWAP)
-    preconds, partial_mine = lax.cond(
+    preconds = lax.cond(
         lax.axis_index("x") < X,
-        lambda *ops: gather_preconds(*ops, length, columns),
-        lambda *ops: (
-            [jnp.zeros((width, width), jnp.bfloat16)] * (X * CORE),
-            jnp.zeros((X * CORE, columns), jnp.float32),
-        ),
-        query_in[0, 0], query_out[0, 0], in_basis, out_basis, eigen_values[0], mine,
+        gather_preconds,
+        lambda *ops: [jnp.zeros((width, width), jnp.bfloat16)] * (X * CORE),
+        query_in[0, 0], query_out[0, 0], in_basis, out_basis, eigen_values[0],
     )
-    partial_theirs = scores_of(theirs, preconds, length, columns)
-    partial_value = partial_mine + partial_theirs
+    stack, partial_mine = first_scores(mine, preconds, length, columns)
+    partial_value = last_scores(theirs, stack, partial_mine, length, columns)
 
     k = jnp.arange(X * CORE, dtype=jnp.int32)
     owner = (lax.axis_index("x") ^ (k % X)) * CORE + (lax.axis_index("core") ^ (k // X))

time: 132 us -> 129 us (0.977)
  starting transfers between devices: 74.8 us -> 71.8 us
  matrix products: 1.73 us -> 4.34 us
  Pallas kernels: 8.49 us -> 6.46 us
    all_to_all x1, starting transfers between devices: 18.5 us -> 15.7 us  [local(): summed = jnp.sum(lax.all_to_all(far, 'zlo', 0, 0), axis=0)]
    pallas_call x3, Pallas kernels: 8.49 us -> 6.46 us  [the longest x1 3.22 us: first_scores(): pl.pallas_call(kernel, out_shape=[jax.ShapeDtypeStruct((count,) + precond...]
    dot_general x1, matrix products: 1.44 us -> 2.88 us  [gather_preconds(): lax.dot_general(side_out, side_in, (((0,), (0,)), ((), ())), preferred_el...]
  transfers between devices with their start and end apart: 9 -> 9, of which waited for: 5 -> 5; matrix products, arithmetic and copies ran while one was open for 1% -> 3% of each run, Pallas kernels for 2% -> 3%
where the time goes in v5:
time: 129 us; the launch traced here: 128 us
  starting transfers between devices  71.8 us (56%)
  waiting for transfers between devices  31.6 us (24%)
  blocking collectives  11.8 us (9%)
  Pallas kernels  6.46 us (5%)
  matrix products  4.34 us (3%)
    ppermute x1, starting transfers between devices, local(): theirs = lax.ppermute(mine, 'zhi', SWAP)  29.5 us
    all_to_all x1, waiting for transfers between devices, local(): summed = jnp.sum(lax.all_to_all(far, 'zlo', 0, 0), axis=0)  18.1 us
    ppermute x4, starting transfers between devices, gather_preconds(): beside = [lax.ppermute(p, 'core', SWAP) for p in along]  17.1 us
    all_to_all x1, starting transfers between devices, local(): summed = jnp.sum(lax.all_to_all(far, 'zlo', 0, 0), axis=0)  15.7 us
    all_to_all x1, blocking collectives, local(): near = jnp.sum(lax.all_to_all(spread, ('y', 'x', 'core'), 0, 0), axis=0)  11.8 us
    ppermute x3, waiting for transfers between devices, gather_preconds(): along.append(lax.ppermute(precond, 'x', [(i, i ^ step) for i in range(X)]))  11.7 us
    ppermute x3, starting transfers between devices, gather_preconds(): along.append(lax.ppermute(precond, 'x', [(i, i ^ step) for i in range(X)]))  9.57 us
    pallas_call x1, Pallas kernels, first_scores(): pl.pallas_call(kernel, out_shape=[jax.ShapeDtypeStruct((count,) + precond...  3.22 us
  transfers between devices with their start and end apart: 9, of which 5 were waited for; matrix products, arithmetic and copies ran while one was open for 3% of the time, Pallas kernels for 3%

profile of v5, /device:TPU:1, one launch (start us, length us, event | category | flops | bytes accessed | tf_op | source)
XLA Modules:
  0.0 128.1 jit_solution(4588223996112968934)
XLA Ops:
  0.0 2.4 %shard_map.94.packed_ref = bf16[1032,128]{1,0:T(8,128)(2,1)} custom-call(s32[2]{0:T(128)} %ids_ref.1, f32[128,512]{1,0:T(8,128)} %bitcast.26, f32[128,512]{1,0:T(8,128)} %bitcast.27, bf16[512,512]{1,0:T(8,128)(2,1)} %bitcast.22, bf16[512,512]{1,0:T(8,128)(2,1)} %bitcast.24), custom_call_target="tpu_custom_call" | custom-call | tf_op jit(solution)/shard_map/pallas_call | solution.py:44
  2.4 29.5 %collective-permute-start.7 = (bf16[1032,128]{1,0:T(8,128)(2,1)}, bf16[1032,128]{1,0:T(8,128)(2,1)S(1)}, u32[]{:S(2)}, u32[]{:S(2)}) collective-permute-start(bf16[1032,128]{1,0:T(8,128)(2,1)} %shard_map.94.packed_ref), channel_id=1, source_target_pairs={{0,8},{8,0},{1,9},{9,1},{2,10},{10,2},{3,11},{11,3},{4,12},{12,4},... | collective-permute-start | bytes 792584 | tf_op jit(solution)/shard_map/ppermute | solution.py:143
  31.9 0.0 copy-start
  31.9 44.6 %conditional.1 = (bf16[512,512]{1,0:T(8,128)(2,1)}, bf16[512,512]{1,0:T(8,128)(2,1)}, bf16[512,512]{1,0:T(8,128)(2,1)}, bf16[512,512]{1,0:T(8,128)(2,1)}, bf16[5...) conditional(s32[]{:T(128)} %convert_element_type.12, () %tuple.13, ...), branch_computations={%region_0.0_spmd, %region_1.0_spmd} | conditional | flops 403963904 | bytes 18350424 | solution.py:144
  31.9 1.5 %convolution_convert_fusion = bf16[256,512]{1,0:T(8,128)(2,1)S(1)} fusion(bf16[512,512]{1,0:T(8,128)(2,1)} %get-tuple-element.21, bf16[1,1,256,512]{3,2,1,0:T(8,128)(2,1)} %get-tuple-element.47), kind=kOutput, calls=%fused_computation.2 | convolution fusion | flops 134348800 | bytes 1048576 | tf_op jit(solution)/shard_map/cond/branch_1_fun/dot_general | solution.py:24
  33.4 2.9 %fusion = bf16[512,512]{1,0:T(8,128)(2,1)} fusion(bf16[256,512]{1,0:T(8,128)(2,1)S(1)} %convolution_convert_fusion, bf16[512,512]{1,0:T(8,128)(2,1)} %get-tuple-element.19, f32[1,512,512]{2,1,0:T(8,128)} %get-tuple-element.48, bf16[1,1,256,512]{3,2,1,0:T(8,128)(2,1)} %get-tuple-element.46), kind=kOutput, calls=%fused_computation.1 | convolution fusion | flops 269615104 | bytes 2621440 | tf_op jit(solution)/shard_map/cond/branch_1_fun/dot_general | solution.py:111
  36.3 3.1 %collective-permute-start = (bf16[512,512]{1,0:T(8,128)(2,1)}, bf16[512,512]{1,0:T(8,128)(2,1)}, u32[]{:S(2)}, u32[]{:S(2)}) collective-permute-start(bf16[512,512]{1,0:T(8,128)(2,1)} %fusion), channel_id=1, source_target_pairs={{0,2},{2,0},{4,6},{6,4},{1,3},{3,1},{5,7},{7,5},{8,10},{10,8},{12,... | collective-permute-start | bytes 1572872 | tf_op jit(solution)/shard_map/cond/branch_1_fun/ppermute | solution.py:118
  39.4 4.4 %collective-permute-start.1 = (bf16[512,512]{1,0:T(8,128)(2,1)}, bf16[512,512]{1,0:T(8,128)(2,1)}, u32[]{:S(2)}, u32[]{:S(2)}) collective-permute-start(bf16[512,512]{1,0:T(8,128)(2,1)} %fusion), channel_id=1, source_target_pairs={{0,4},{2,6},{4,0},{6,2},{1,5},{3,7},{5,1},{7,3},{8,12},{10,14},{12... | collective-permute-start | bytes 1572872 | tf_op jit(solution)/shard_map/cond/branch_1_fun/ppermute | solution.py:118
  43.8 2.1 %collective-permute-start.2 = (bf16[512,512]{1,0:T(8,128)(2,1)}, bf16[512,512]{1,0:T(8,128)(2,1)}, u32[]{:S(2)}, u32[]{:S(2)}) collective-permute-start(bf16[512,512]{1,0:T(8,128)(2,1)} %fusion), channel_id=1, source_target_pairs={{0,6},{2,4},{4,2},{6,0},{1,7},{3,5},{5,3},{7,1},{8,14},{10,12},{12... | collective-permute-start | bytes 1572872 | tf_op jit(solution)/shard_map/cond/branch_1_fun/ppermute | solution.py:118
  45.9 3.7 %collective-permute-start.3 = (bf16[512,512]{1,0:T(8,128)(2,1)}, bf16[512,512]{1,0:T(8,128)(2,1)}, u32[]{:S(2)}, u32[]{:S(2)}) collective-permute-start(bf16[512,512]{1,0:T(8,128)(2,1)} %fusion), channel_id=1, source_target_pairs={{0,1},{1,0},{2,3},{3,2},{4,5},{5,4},{6,7},{7,6},{8,9},{9,8},{10,11... | collective-permute-start | bytes 1572872 | tf_op jit(solution)/shard_map/cond/branch_1_fun/ppermute | solution.py:119
  49.6 1.4 %collective-permute-done = bf16[512,512]{1,0:T(8,128)(2,1)} collective-permute-done((bf16[512,512]{1,0:T(8,128)(2,1)}, bf16[512,512]{1,0:T(8,128)(2,1)}, u32[]{:S(2)}, u32[]{:S(2)}) %collective-permute-start) | collective-permute-done | bytes 524320 | tf_op jit(solution)/shard_map/cond/branch_1_fun/ppermute | solution.py:118
  51.0 5.2 %collective-permute-start.4 = (bf16[512,512]{1,0:T(8,128)(2,1)}, bf16[512,512]{1,0:T(8,128)(2,1)}, u32[]{:S(2)}, u32[]{:S(2)}) collective-permute-start(bf16[512,512]{1,0:T(8,128)(2,1)} %collective-permute-done), channel_id=1, source_target_pairs={{0,1},{1,0},{2,3},{3,2},{4,5},{5,4},{6,7},{7,6},{8,9},{9,8},{10,11... | collective-permute-start | bytes 1572872 | tf_op jit(solution)/shard_map/cond/branch_1_fun/ppermute | solution.py:119
  56.2 8.3 %collective-permute-done.1 = bf16[512,512]{1,0:T(8,128)(2,1)} collective-permute-done((bf16[512,512]{1,0:T(8,128)(2,1)}, bf16[512,512]{1,0:T(8,128)(2,1)}, u32[]{:S(2)}, u32[]{:S(2)}) %collective-permute-start.1) | collective-permute-done | bytes 524320 | tf_op jit(solution)/shard_map/cond/branch_1_fun/ppermute | solution.py:118
  64.4 3.8 %collective-permute-start.5 = (bf16[512,512]{1,0:T(8,128)(2,1)}, bf16[512,512]{1,0:T(8,128)(2,1)}, u32[]{:S(2)}, u32[]{:S(2)}) collective-permute-start(bf16[512,512]{1,0:T(8,128)(2,1)} %collective-permute-done.1), channel_id=1, source_target_pairs={{0,1},{1,0},{2,3},{3,2},{4,5},{5,4},{6,7},{7,6},{8,9},{9,8},{10,11... | collective-permute-start | bytes 1572872 | tf_op jit(solution)/shard_map/cond/branch_1_fun/ppermute | solution.py:119
  68.3 2.1 %collective-permute-done.2 = bf16[512,512]{1,0:T(8,128)(2,1)} collective-permute-done((bf16[512,512]{1,0:T(8,128)(2,1)}, bf16[512,512]{1,0:T(8,128)(2,1)}, u32[]{:S(2)}, u32[]{:S(2)}) %collective-permute-start.2) | collective-permute-done | bytes 524320 | tf_op jit(solution)/shard_map/cond/branch_1_fun/ppermute | solution.py:118
  70.3 4.3 %collective-permute-start.6 = (bf16[512,512]{1,0:T(8,128)(2,1)}, bf16[512,512]{1,0:T(8,128)(2,1)}, u32[]{:S(2)}, u32[]{:S(2)}) collective-permute-start(bf16[512,512]{1,0:T(8,128)(2,1)} %collective-permute-done.2), channel_id=1, source_target_pairs={{0,1},{1,0},{2,3},{3,2},{4,5},{5,4},{6,7},{7,6},{8,9},{9,8},{10,11... | collective-permute-start | bytes 1572872 | tf_op jit(solution)/shard_map/cond/branch_1_fun/ppermute | solution.py:119
  74.7 0.0 collective-permute-done.3
  74.7 0.0 collective-permute-done.4
  74.7 0.0 collective-permute-done.5
  74.7 1.8 %collective-permute-done.6 = bf16[512,512]{1,0:T(8,128)(2,1)} collective-permute-done((bf16[512,512]{1,0:T(8,128)(2,1)}, bf16[512,512]{1,0:T(8,128)(2,1)}, u32[]{:S(2)}, u32[]{:S(2)}) %collective-permute-start.6) | collective-permute-done | bytes 524320 | tf_op jit(solution)/shard_map/cond/branch_1_fun/ppermute | solution.py:119
  76.5 0.0 copy-done
  76.5 3.2 %shard_map.95 = (bf16[8,512,512]{2,1,0:T(8,128)(2,1)S(1)}, f32[8,32]{1,0:T(8,128)S(1)}) custom-call(bf16[1032,128]{1,0:T(8,128)(2,1)S(1)} %copy-done, bf16[512,512]{1,0:T(8,128)(2,1)} %get-tuple-element.33.refs_0_, bf16[512,512]{1,0:T(8,128)(2,1)} %get-tuple-element.34.refs_1_, bf16[512,512]{1,0:T(8,128)(2,1)} %get-tuple-element.35.refs_2_, ...), custom_call_target="tpu_custom_call" | custom-call | tf_op jit(solution)/shard_map/pallas_call | solution.py:82
  79.8 0.0 collective-permute-done.7.packed_ref
  79.8 0.9 shard_map.96
  80.6 0.1 select_reduce_fusion
  80.7 11.8 %all_to_all.15 = f32[32,1,32]{2,1,0:T(1,128)S(1)} all-to-all(f32[32,1,32]{2,1,0:T(1,128)S(1)} %bitcast.28), channel_id=1, replica_groups=mesh['zlo'=16,'y'=4,'zhi'=2,'x'=4,'core'=2] {'y','x','core'}, dimensions={0} | all-to-all | bytes 8192 | tf_op jit(solution)/shard_map/all_to_all | solution.py:160
  92.5 0.1 reduce_sum.28
  92.5 0.6 broadcast_in_dim.48
  93.1 15.7 %all-to-all-start.1 = ((f32[16,1,32]{2,1,0:T(1,128)}), f32[16,1,32]{2,1,0:T(1,128)S(1)}, u32[]{:S(2)}, u32[]{:S(2)}) async-start(f32[16,1,32]{2,1,0:T(1,128)} %broadcast_in_dim.48), calls=%async_computation.1 | async-start | bytes 16384 | tf_op jit(solution)/shard_map/all_to_all | solution.py:162
  109.5 18.1 %all-to-all-done.1 = f32[16,1,32]{2,1,0:T(1,128)S(1)} async-done(((f32[16,1,32]{2,1,0:T(1,128)}), f32[16,1,32]{2,1,0:T(1,128)S(1)}, u32[]{:S(2)}, u32[]{:S(2)}) %all-to-all-start.1) | async-done | bytes 2080 | tf_op jit(solution)/shard_map/all_to_all | solution.py:162
  127.6 0.5 compare_select_fusion
  (4 shorter events, 0.0 us)
Async XLA Ops:
  2.4 77.4 %collective-permute-start.7 = (bf16[1032,128]{1,0:T(8,128)(2,1)}, bf16[1032,128]{1,0:T(8,128)(2,1)S(1)}, u32[]{:S(2)}, u32[]{:S(2)}) collective-permute-start(bf16[1032,128]{1,0:T(8,128)(2,1)} %shard_map.94.packed_ref), channel_id=1, source_target_pairs={{0,8},{8,0},{1,9},{9,1},{2,10},{10,2},{3,11},{11,3},{4,12},{12,4},... | collective-permute-start | bytes 792584 | tf_op jit(solution)/shard_map/ppermute | solution.py:143
  31.9 44.6 %copy-start = (bf16[1032,128]{1,0:T(8,128)(2,1)S(1)}, bf16[1032,128]{1,0:T(8,128)(2,1)}, u32[]{:S(2)}) copy-start(bf16[1032,128]{1,0:T(8,128)(2,1)} %shard_map.94.packed_ref) | copy-start | bytes 792580
  36.3 14.7 %collective-permute-start = (bf16[512,512]{1,0:T(8,128)(2,1)}, bf16[512,512]{1,0:T(8,128)(2,1)}, u32[]{:S(2)}, u32[]{:S(2)}) collective-permute-start(bf16[512,512]{1,0:T(8,128)(2,1)} %fusion), channel_id=1, source_target_pairs={{0,2},{2,0},{4,6},{6,4},{1,3},{3,1},{5,7},{7,5},{8,10},{10,8},{12,... | collective-permute-start | bytes 1572872 | tf_op jit(solution)/shard_map/cond/branch_1_fun/ppermute | solution.py:118
  39.4 25.0 %collective-permute-start.1 = (bf16[512,512]{1,0:T(8,128)(2,1)}, bf16[512,512]{1,0:T(8,128)(2,1)}, u32[]{:S(2)}, u32[]{:S(2)}) collective-permute-start(bf16[512,512]{1,0:T(8,128)(2,1)} %fusion), channel_id=1, source_target_pairs={{0,4},{2,6},{4,0},{6,2},{1,5},{3,7},{5,1},{7,3},{8,12},{10,14},{12... | collective-permute-start | bytes 1572872 | tf_op jit(solution)/shard_map/cond/branch_1_fun/ppermute | solution.py:118
  43.8 26.6 %collective-permute-start.2 = (bf16[512,512]{1,0:T(8,128)(2,1)}, bf16[512,512]{1,0:T(8,128)(2,1)}, u32[]{:S(2)}, u32[]{:S(2)}) collective-permute-start(bf16[512,512]{1,0:T(8,128)(2,1)} %fusion), channel_id=1, source_target_pairs={{0,6},{2,4},{4,2},{6,0},{1,7},{3,5},{5,3},{7,1},{8,14},{10,12},{12... | collective-permute-start | bytes 1572872 | tf_op jit(solution)/shard_map/cond/branch_1_fun/ppermute | solution.py:118
  45.9 28.8 %collective-permute-start.3 = (bf16[512,512]{1,0:T(8,128)(2,1)}, bf16[512,512]{1,0:T(8,128)(2,1)}, u32[]{:S(2)}, u32[]{:S(2)}) collective-permute-start(bf16[512,512]{1,0:T(8,128)(2,1)} %fusion), channel_id=1, source_target_pairs={{0,1},{1,0},{2,3},{3,2},{4,5},{5,4},{6,7},{7,6},{8,9},{9,8},{10,11... | collective-permute-start | bytes 1572872 | tf_op jit(solution)/shard_map/cond/branch_1_fun/ppermute | solution.py:119
  51.0 23.7 %collective-permute-start.4 = (bf16[512,512]{1,0:T(8,128)(2,1)}, bf16[512,512]{1,0:T(8,128)(2,1)}, u32[]{:S(2)}, u32[]{:S(2)}) collective-permute-start(bf16[512,512]{1,0:T(8,128)(2,1)} %collective-permute-done), channel_id=1, source_target_pairs={{0,1},{1,0},{2,3},{3,2},{4,5},{5,4},{6,7},{7,6},{8,9},{9,8},{10,11... | collective-permute-start | bytes 1572872 | tf_op jit(solution)/shard_map/cond/branch_1_fun/ppermute | solution.py:119
  64.4 10.3 %collective-permute-start.5 = (bf16[512,512]{1,0:T(8,128)(2,1)}, bf16[512,512]{1,0:T(8,128)(2,1)}, u32[]{:S(2)}, u32[]{:S(2)}) collective-permute-start(bf16[512,512]{1,0:T(8,128)(2,1)} %collective-permute-done.1), channel_id=1, source_target_pairs={{0,1},{1,0},{2,3},{3,2},{4,5},{5,4},{6,7},{7,6},{8,9},{9,8},{10,11... | collective-permute-start | bytes 1572872 | tf_op jit(solution)/shard_map/cond/branch_1_fun/ppermute | solution.py:119
  70.3 6.2 %collective-permute-start.6 = (bf16[512,512]{1,0:T(8,128)(2,1)}, bf16[512,512]{1,0:T(8,128)(2,1)}, u32[]{:S(2)}, u32[]{:S(2)}) collective-permute-start(bf16[512,512]{1,0:T(8,128)(2,1)} %collective-permute-done.2), channel_id=1, source_target_pairs={{0,1},{1,0},{2,3},{3,2},{4,5},{5,4},{6,7},{7,6},{8,9},{9,8},{10,11... | collective-permute-start | bytes 1572872 | tf_op jit(solution)/shard_map/cond/branch_1_fun/ppermute | solution.py:119
  93.1 34.4 %all-to-all-start.1 = ((f32[16,1,32]{2,1,0:T(1,128)}), f32[16,1,32]{2,1,0:T(1,128)S(1)}, u32[]{:S(2)}, u32[]{:S(2)}) async-start(f32[16,1,32]{2,1,0:T(1,128)} %broadcast_in_dim.48), calls=%async_computation.1 | async-start | bytes 16384 | tf_op jit(solution)/shard_map/all_to_all | solution.py:162

commit v6 on v5

--- a/solution.py
+++ b/solution.py
@@ -24,28 +24,55 @@
     return jnp.dot(rows, basis, preferred_element_type=jnp.float32).astype(jnp.bfloat16)
 
 
-def train_kernel(ids_ref, in_ref, out_ref, in_basis_ref, out_basis_ref, packed_ref):
+def train_kernel(
+    ids_ref, in_ref, out_ref, in_basis_ref, out_basis_ref, packed_ref,
+    tokens_vmem, basis_vmem, packed_vmem, read, write,
+):
     tokens, width = in_ref.shape
-    inside = project(in_ref[...].astype(jnp.bfloat16), in_basis_ref[...])
-    outside = project(out_ref[...].astype(jnp.bfloat16), out_basis_ref[...])
-    for at, side in ((0, inside), (width // LANES, outside)):
-        for c in range(width // LANES):
-            packed_ref[(at + c) * tokens : (at + c + 1) * tokens] = side[:, c * LANES : (c + 1) * LANES]
+    sides = ((in_ref, in_basis_ref), (out_ref, out_basis_ref))
+    reads = []
+    for k, refs in enumerate(sides):
+        for n, (ref, vmem) in enumerate(zip(refs, (tokens_vmem, basis_vmem))):
+            reads.append(pltpu.make_async_copy(ref, vmem.at[k], read.at[2 * k + n]))
+            reads[-1].start()
     row = lax.broadcasted_iota(jnp.int32, (EXTRA, LANES), 0)
     lane = lax.broadcasted_iota(jnp.int32, (EXTRA, LANES), 1)
     hit = (row == 0) & (lane == ids_ref[0])
     for s in range(1, ids_ref.shape[0]):
         hit = hit | ((row == s) & (lane == ids_ref[s]))
-    packed_ref[packed_ref.shape[0] - EXTRA :] = jnp.where(hit, 1.0, 0.0).astype(jnp.bfloat16)
+    size = tokens * width // LANES
+    packed_vmem[2 * size :] = jnp.where(hit, 1.0, 0.0).astype(jnp.bfloat16)
+    writes = []
+    for k in range(len(sides)):
+        reads[2 * k].wait()
+        reads[2 * k + 1].wait()
+        side = project(tokens_vmem[k].astype(jnp.bfloat16), basis_vmem[k])
+        for c in range(width // LANES):
+            start = k * size + c * tokens
+            packed_vmem[start : start + tokens] = side[:, c * LANES : (c + 1) * LANES]
+        part = pl.ds(k * size, size + (EXTRA if k else 0))
+        writes.append(pltpu.make_async_copy(packed_vmem.at[part], packed_ref.at[part], write.at[k]))
+        writes[-1].start()
+    for copy in writes:
+        copy.wait()
 
 
 def pack_train(train_ids, train_in, train_out, in_basis, out_basis):
     tokens, width = train_in.shape
+    packed = (2 * tokens * width // LANES + EXTRA, LANES)
+    anywhere = pl.BlockSpec(memory_space=pl.ANY)
     return pl.pallas_call(
         train_kernel,
-        out_shape=jax.ShapeDtypeStruct((2 * tokens * width // LANES + EXTRA, LANES), jnp.bfloat16),
-        in_specs=[SMEM] + [VMEM] * 4,
-        out_specs=VMEM,
+        out_shape=jax.ShapeDtypeStruct(packed, jnp.bfloat16),
+        in_specs=[SMEM] + [anywhere] * 4,
+        out_specs=anywhere,
+        scratch_shapes=[
+            pltpu.VMEM((2, tokens, width), jnp.float32),
+            pltpu.VMEM((2, width, width), jnp.bfloat16),
+            pltpu.VMEM(packed, jnp.bfloat16),
+            pltpu.SemaphoreType.DMA((4,)),
+            pltpu.SemaphoreType.DMA((2,)),
+        ],
     )(train_ids, train_in, train_out, in_basis, out_basis)
 
 
@@ -105,14 +132,17 @@
     )(packed, stack, before)
 
 
-def gather_preconds(query_in, query_out, in_basis, out_basis, eigen_values):
+def precondition(query_in, query_out, in_basis, out_basis, eigen_values):
     side_in = project(query_in, in_basis)
     side_out = project(query_out, out_basis)
     moment = lax.dot_general(
         side_out, side_in, (((0,), (0,)), ((), ())), preferred_element_type=jnp.float32
     )
     scale = query_in.shape[0] * (eigen_values + damping)
-    precond = (moment / scale).astype(jnp.bfloat16)
+    return (moment / scale).astype(jnp.bfloat16)
+
+
+def gather_preconds(precond):
     along = [precond]
     for step in range(1, X):
         along.append(lax.ppermute(precond, "x", [(i, i ^ step) for i in range(X)]))
@@ -141,11 +171,9 @@
         train_ids, train_in[0].reshape(tokens), train_out[0].reshape(tokens), in_basis, out_basis
     )
     theirs = lax.ppermute(mine, "zhi", SWAP)
+    precond = precondition(query_in[0, 0], query_out[0, 0], in_basis, out_basis, eigen_values[0])
     preconds = lax.cond(
-        lax.axis_index("x") < X,
-        gather_preconds,
-        lambda *ops: [jnp.zeros((width, width), jnp.bfloat16)] * (X * CORE),
-        query_in[0, 0], query_out[0, 0], in_basis, out_basis, eigen_values[0],
+        lax.axis_index("x") < X, gather_preconds, lambda precond: [precond] * (X * CORE), precond
     )
     stack, partial_mine = first_scores(mine, preconds, length, columns)
     partial_value = last_scores(theirs, stack, partial_mine, length, columns)

time: 129 us -> 129 us (level)
  starting transfers between devices: 71.8 us -> 73.1 us
  transfers between devices with their start and end apart: 9 -> 9, of which waited for: 5 -> 5; matrix products, arithmetic and copies ran while one was open for 3% -> 3% of each run, Pallas kernels for 3% -> 2%
where the time goes in v6:
time: 129 us
  starting transfers between devices  73.1 us (57%)
  waiting for transfers between devices  31.4 us (24%)
  blocking collectives  11.7 us (9%)
  Pallas kernels  7 us (5%)
  matrix products  3.43 us (3%)
    ppermute x1, starting transfers between devices, local(): theirs = lax.ppermute(mine, 'zhi', SWAP)  29.5 us
    all_to_all x1, waiting for transfers between devices, local(): summed = jnp.sum(lax.all_to_all(far, 'zlo', 0, 0), axis=0)  18.1 us
    ppermute x4, starting transfers between devices, gather_preconds(): beside = [lax.ppermute(p, 'core', SWAP) for p in along]  17.1 us
    all_to_all x1, starting transfers between devices, local(): summed = jnp.sum(lax.all_to_all(far, 'zlo', 0, 0), axis=0)  16.8 us
    all_to_all x1, blocking collectives, local(): near = jnp.sum(lax.all_to_all(spread, ('y', 'x', 'core'), 0, 0), axis=0)  11.7 us
    ppermute x3, waiting for transfers between devices, gather_preconds(): along.append(lax.ppermute(precond, 'x', [(i, i ^ step) for i in range(X)]))  11.4 us
    ppermute x3, starting transfers between devices, gather_preconds(): along.append(lax.ppermute(precond, 'x', [(i, i ^ step) for i in range(X)]))  9.72 us
    pallas_call x1, Pallas kernels, pack_train(): pl.pallas_call(train_kernel, out_shape=jax.ShapeDtypeStruct(packed, jnp.b...  3.08 us
  transfers between devices with their start and end apart: 9, of which 5 were waited for; matrix products, arithmetic and copies ran while one was open for 3% of the time, Pallas kernels for 2%

profile of v6, /device:TPU:1, one launch (start us, length us, event | category | flops | bytes accessed | tf_op | source)
XLA Modules:
  0.0 128.8 jit_solution(14283007764019650001)
XLA Ops:
  0.0 0.0 copy-start
  0.0 3.1 %shard_map.91.packed_ref = bf16[1032,128]{1,0:T(8,128)(2,1)} custom-call(s32[2]{0:T(128)} %ids_ref.1, f32[128,512]{1,0:T(8,128)} %bitcast.27, f32[128,512]{1,0:T(8,128)} %bitcast.28, bf16[512,512]{1,0:T(8,128)(2,1)} %bitcast.25, bf16[512,512]{1,0:T(8,128)(2,1)} %bitcast.26), custom_call_target="tpu_custom_call" | custom-call | tf_op jit(solution)/shard_map/pallas_call | solution.py:64
  3.1 29.5 %collective-permute-start.7 = (bf16[1032,128]{1,0:T(8,128)(2,1)}, bf16[1032,128]{1,0:T(8,128)(2,1)S(1)}, u32[]{:S(2)}, u32[]{:S(2)}) collective-permute-start(bf16[1032,128]{1,0:T(8,128)(2,1)} %shard_map.91.packed_ref), channel_id=1, source_target_pairs={{0,8},{8,0},{1,9},{9,1},{2,10},{10,2},{3,11},{11,3},{4,12},{12,4},... | collective-permute-start | bytes 792584 | tf_op jit(solution)/shard_map/ppermute | solution.py:173
  32.6 1.4 %convolution_convert_fusion = bf16[256,512]{1,0:T(8,128)(2,1)S(1)} fusion(bf16[1,1,256,512]{3,2,1,0:T(8,128)(2,1)} %param.13, bf16[1,512,512]{2,1,0:T(8,128)(2,1)} %param.15), kind=kOutput, calls=%fused_computation.2 | convolution fusion | flops 134348800 | bytes 1048576 | tf_op jit(solution)/shard_map/dot_general | solution.py:24
  34.1 0.0 copy-done
  34.1 2.0 %fusion.refs_0_ = bf16[512,512]{1,0:T(8,128)(2,1)S(1)} fusion(bf16[256,512]{1,0:T(8,128)(2,1)S(1)} %convolution_convert_fusion, f32[1,512,512]{2,1,0:T(8,128)} %param.17, bf16[1,1,256,512]{3,2,1,0:T(8,128)(2,1)S(1)} %copy-done, bf16[1,512,512]{2,1,0:T(8,128)(2,1)} %param.16), kind=kOutput, calls=%fused_computation.1 | convolution fusion | flops 269615104 | bytes 2621440 | tf_op jit(solution)/shard_map/dot_general | solution.py:138
  36.1 0.0 copy-start.1
  36.1 40.2 %conditional.1 = (bf16[512,512]{1,0:T(8,128)(2,1)}, bf16[512,512]{1,0:T(8,128)(2,1)}, bf16[512,512]{1,0:T(8,128)(2,1)}, bf16[512,512]{1,0:T(8,128)(2,1)}, bf16[5...) conditional(s32[]{:T(128)} %convert_element_type.21, ...), branch_computations={%region_0.0_spmd, %region_1.0_spmd} | conditional | bytes 14680400 | solution.py:175
  36.1 3.3 %collective-permute-start = (bf16[512,512]{1,0:T(8,128)(2,1)S(1)}, bf16[512,512]{1,0:T(8,128)(2,1)}, u32[]{:S(2)}, u32[]{:S(2)}) collective-permute-start(bf16[512,512]{1,0:T(8,128)(2,1)S(1)} %param.1), channel_id=1, source_target_pairs={{0,2},{2,0},{4,6},{6,4},{1,3},{3,1},{5,7},{7,5},{8,10},{10,8},{12,... | collective-permute-start | bytes 1572872 | tf_op jit(solution)/shard_map/cond/branch_1_fun/ppermute | solution.py:148
  39.4 4.4 %collective-permute-start.1 = (bf16[512,512]{1,0:T(8,128)(2,1)S(1)}, bf16[512,512]{1,0:T(8,128)(2,1)}, u32[]{:S(2)}, u32[]{:S(2)}) collective-permute-start(bf16[512,512]{1,0:T(8,128)(2,1)S(1)} %param.1), channel_id=1, source_target_pairs={{0,4},{2,6},{4,0},{6,2},{1,5},{3,7},{5,1},{7,3},{8,12},{10,14},{12... | collective-permute-start | bytes 1572872 | tf_op jit(solution)/shard_map/cond/branch_1_fun/ppermute | solution.py:148
  43.7 2.1 %collective-permute-start.2 = (bf16[512,512]{1,0:T(8,128)(2,1)S(1)}, bf16[512,512]{1,0:T(8,128)(2,1)}, u32[]{:S(2)}, u32[]{:S(2)}) collective-permute-start(bf16[512,512]{1,0:T(8,128)(2,1)S(1)} %param.1), channel_id=1, source_target_pairs={{0,6},{2,4},{4,2},{6,0},{1,7},{3,5},{5,3},{7,1},{8,14},{10,12},{12... | collective-permute-start | bytes 1572872 | tf_op jit(solution)/shard_map/cond/branch_1_fun/ppermute | solution.py:148
  45.9 3.7 %collective-permute-start.3 = (bf16[512,512]{1,0:T(8,128)(2,1)S(1)}, bf16[512,512]{1,0:T(8,128)(2,1)}, u32[]{:S(2)}, u32[]{:S(2)}) collective-permute-start(bf16[512,512]{1,0:T(8,128)(2,1)S(1)} %param.1), channel_id=1, source_target_pairs={{0,1},{1,0},{2,3},{3,2},{4,5},{5,4},{6,7},{7,6},{8,9},{9,8},{10,11... | collective-permute-start | bytes 1572872 | tf_op jit(solution)/shard_map/cond/branch_1_fun/ppermute | solution.py:149
  49.6 1.2 collective-permute-done
  50.7 5.2 %collective-permute-start.4 = (bf16[512,512]{1,0:T(8,128)(2,1)}, bf16[512,512]{1,0:T(8,128)(2,1)}, u32[]{:S(2)}, u32[]{:S(2)}) collective-permute-start(bf16[512,512]{1,0:T(8,128)(2,1)} %collective-permute-done), channel_id=1, source_target_pairs={{0,1},{1,0},{2,3},{3,2},{4,5},{5,4},{6,7},{7,6},{8,9},{9,8},{10,11... | collective-permute-start | bytes 1572872 | tf_op jit(solution)/shard_map/cond/branch_1_fun/ppermute | solution.py:149
  56.0 8.2 %collective-permute-done.1 = bf16[512,512]{1,0:T(8,128)(2,1)} collective-permute-done((bf16[512,512]{1,0:T(8,128)(2,1)S(1)}, bf16[512,512]{1,0:T(8,128)(2,1)}, u32[]{:S(2)}, u32[]{:S(2)}) %collective-permute-start.1) | collective-permute-done | bytes 524320 | tf_op jit(solution)/shard_map/cond/branch_1_fun/ppermute | solution.py:148
  64.2 3.8 %collective-permute-start.5 = (bf16[512,512]{1,0:T(8,128)(2,1)}, bf16[512,512]{1,0:T(8,128)(2,1)}, u32[]{:S(2)}, u32[]{:S(2)}) collective-permute-start(bf16[512,512]{1,0:T(8,128)(2,1)} %collective-permute-done.1), channel_id=1, source_target_pairs={{0,1},{1,0},{2,3},{3,2},{4,5},{5,4},{6,7},{7,6},{8,9},{9,8},{10,11... | collective-permute-start | bytes 1572872 | tf_op jit(solution)/shard_map/cond/branch_1_fun/ppermute | solution.py:149
  68.0 2.1 %collective-permute-done.2 = bf16[512,512]{1,0:T(8,128)(2,1)} collective-permute-done((bf16[512,512]{1,0:T(8,128)(2,1)S(1)}, bf16[512,512]{1,0:T(8,128)(2,1)}, u32[]{:S(2)}, u32[]{:S(2)}) %collective-permute-start.2) | collective-permute-done | bytes 524320 | tf_op jit(solution)/shard_map/cond/branch_1_fun/ppermute | solution.py:148
  70.1 4.3 %collective-permute-start.6 = (bf16[512,512]{1,0:T(8,128)(2,1)}, bf16[512,512]{1,0:T(8,128)(2,1)}, u32[]{:S(2)}, u32[]{:S(2)}) collective-permute-start(bf16[512,512]{1,0:T(8,128)(2,1)} %collective-permute-done.2), channel_id=1, source_target_pairs={{0,1},{1,0},{2,3},{3,2},{4,5},{5,4},{6,7},{7,6},{8,9},{9,8},{10,11... | collective-permute-start | bytes 1572872 | tf_op jit(solution)/shard_map/cond/branch_1_fun/ppermute | solution.py:149
  74.4 0.0 collective-permute-done.3
  74.4 0.0 collective-permute-done.4
  74.5 0.0 collective-permute-done.5
  74.5 1.8 %collective-permute-done.6 = bf16[512,512]{1,0:T(8,128)(2,1)} collective-permute-done((bf16[512,512]{1,0:T(8,128)(2,1)}, bf16[512,512]{1,0:T(8,128)(2,1)}, u32[]{:S(2)}, u32[]{:S(2)}) %collective-permute-start.6) | collective-permute-done | bytes 524320 | tf_op jit(solution)/shard_map/cond/branch_1_fun/ppermute | solution.py:149
  76.3 0.0 copy-done.1
  76.3 3.1 %shard_map.92 = (bf16[8,512,512]{2,1,0:T(8,128)(2,1)S(1)}, f32[8,32]{1,0:T(8,128)S(1)}) custom-call(bf16[1032,128]{1,0:T(8,128)(2,1)S(1)} %copy-done.1, bf16[512,512]{1,0:T(8,128)(2,1)S(1)} %fusion.refs_0_, bf16[512,512]{1,0:T(8,128)(2,1)} %get-tuple-element.16.refs_1_, bf16[512,512]{1,0:T(8,128)(2,1)} %get-tuple-element.17.refs_2_, ...), custom_call_target="tpu_custom_call" | custom-call | tf_op jit(solution)/shard_map/pallas_call | solution.py:109
  79.4 0.0 collective-permute-done.7.packed_ref
  79.4 0.9 shard_map.93
  80.2 0.1 select_reduce_fusion
  80.3 11.7 %all_to_all.15 = f32[32,1,32]{2,1,0:T(1,128)S(1)} all-to-all(f32[32,1,32]{2,1,0:T(1,128)S(1)} %bitcast.29), channel_id=1, replica_groups=mesh['zlo'=16,'y'=4,'zhi'=2,'x'=4,'core'=2] {'y','x','core'}, dimensions={0} | all-to-all | bytes 8192 | tf_op jit(solution)/shard_map/all_to_all | solution.py:188
  92.1 0.1 reduce_sum.28
  92.1 0.6 broadcast_in_dim.48
  92.7 16.8 %all-to-all-start.1 = ((f32[16,1,32]{2,1,0:T(1,128)}), f32[16,1,32]{2,1,0:T(1,128)S(1)}, u32[]{:S(2)}, u32[]{:S(2)}) async-start(f32[16,1,32]{2,1,0:T(1,128)} %broadcast_in_dim.48), calls=%async_computation.1 | async-start | bytes 16384 | tf_op jit(solution)/shard_map/all_to_all | solution.py:190
  110.2 18.1 %all-to-all-done.1 = f32[16,1,32]{2,1,0:T(1,128)S(1)} async-done(((f32[16,1,32]{2,1,0:T(1,128)}), f32[16,1,32]{2,1,0:T(1,128)S(1)}, u32[]{:S(2)}, u32[]{:S(2)}) %all-to-all-start.1) | async-done | bytes 2080 | tf_op jit(solution)/shard_map/all_to_all | solution.py:190
  128.3 0.5 compare_select_fusion
  (4 shorter events, 0.0 us)
Async XLA Ops:
  0.0 34.1 %copy-start = (bf16[1,1,256,512]{3,2,1,0:T(8,128)(2,1)S(1)}, bf16[1,1,256,512]{3,2,1,0:T(8,128)(2,1)}, u32[]{:S(2)}) copy-start(bf16[1,1,256,512]{3,2,1,0:T(8,128)(2,1)} %param.14) | copy-start | bytes 786436
  3.1 76.3 %collective-permute-start.7 = (bf16[1032,128]{1,0:T(8,128)(2,1)}, bf16[1032,128]{1,0:T(8,128)(2,1)S(1)}, u32[]{:S(2)}, u32[]{:S(2)}) collective-permute-start(bf16[1032,128]{1,0:T(8,128)(2,1)} %shard_map.91.packed_ref), channel_id=1, source_target_pairs={{0,8},{8,0},{1,9},{9,1},{2,10},{10,2},{3,11},{11,3},{4,12},{12,4},... | collective-permute-start | bytes 792584 | tf_op jit(solution)/shard_map/ppermute | solution.py:173
  36.1 40.2 %copy-start.1 = (bf16[1032,128]{1,0:T(8,128)(2,1)S(1)}, bf16[1032,128]{1,0:T(8,128)(2,1)}, u32[]{:S(2)}) copy-start(bf16[1032,128]{1,0:T(8,128)(2,1)} %shard_map.91.packed_ref) | copy-start | bytes 792580
  36.1 14.6 %collective-permute-start = (bf16[512,512]{1,0:T(8,128)(2,1)S(1)}, bf16[512,512]{1,0:T(8,128)(2,1)}, u32[]{:S(2)}, u32[]{:S(2)}) collective-permute-start(bf16[512,512]{1,0:T(8,128)(2,1)S(1)} %param.1), channel_id=1, source_target_pairs={{0,2},{2,0},{4,6},{6,4},{1,3},{3,1},{5,7},{7,5},{8,10},{10,8},{12,... | collective-permute-start | bytes 1572872 | tf_op jit(solution)/shard_map/cond/branch_1_fun/ppermute | solution.py:148
  39.4 24.8 %collective-permute-start.1 = (bf16[512,512]{1,0:T(8,128)(2,1)S(1)}, bf16[512,512]{1,0:T(8,128)(2,1)}, u32[]{:S(2)}, u32[]{:S(2)}) collective-permute-start(bf16[512,512]{1,0:T(8,128)(2,1)S(1)} %param.1), channel_id=1, source_target_pairs={{0,4},{2,6},{4,0},{6,2},{1,5},{3,7},{5,1},{7,3},{8,12},{10,14},{12... | collective-permute-start | bytes 1572872 | tf_op jit(solution)/shard_map/cond/branch_1_fun/ppermute | solution.py:148
  43.7 26.3 %collective-permute-start.2 = (bf16[512,512]{1,0:T(8,128)(2,1)S(1)}, bf16[512,512]{1,0:T(8,128)(2,1)}, u32[]{:S(2)}, u32[]{:S(2)}) collective-permute-start(bf16[512,512]{1,0:T(8,128)(2,1)S(1)} %param.1), channel_id=1, source_target_pairs={{0,6},{2,4},{4,2},{6,0},{1,7},{3,5},{5,3},{7,1},{8,14},{10,12},{12... | collective-permute-start | bytes 1572872 | tf_op jit(solution)/shard_map/cond/branch_1_fun/ppermute | solution.py:148
  45.9 28.6 %collective-permute-start.3 = (bf16[512,512]{1,0:T(8,128)(2,1)S(1)}, bf16[512,512]{1,0:T(8,128)(2,1)}, u32[]{:S(2)}, u32[]{:S(2)}) collective-permute-start(bf16[512,512]{1,0:T(8,128)(2,1)S(1)} %param.1), channel_id=1, source_target_pairs={{0,1},{1,0},{2,3},{3,2},{4,5},{5,4},{6,7},{7,6},{8,9},{9,8},{10,11... | collective-permute-start | bytes 1572872 | tf_op jit(solution)/shard_map/cond/branch_1_fun/ppermute | solution.py:149
  50.7 23.7 %collective-permute-start.4 = (bf16[512,512]{1,0:T(8,128)(2,1)}, bf16[512,512]{1,0:T(8,128)(2,1)}, u32[]{:S(2)}, u32[]{:S(2)}) collective-permute-start(bf16[512,512]{1,0:T(8,128)(2,1)} %collective-permute-done), channel_id=1, source_target_pairs={{0,1},{1,0},{2,3},{3,2},{4,5},{5,4},{6,7},{7,6},{8,9},{9,8},{10,11... | collective-permute-start | bytes 1572872 | tf_op jit(solution)/shard_map/cond/branch_1_fun/ppermute | solution.py:149
  64.2 10.3 %collective-permute-start.5 = (bf16[512,512]{1,0:T(8,128)(2,1)}, bf16[512,512]{1,0:T(8,128)(2,1)}, u32[]{:S(2)}, u32[]{:S(2)}) collective-permute-start(bf16[512,512]{1,0:T(8,128)(2,1)} %collective-permute-done.1), channel_id=1, source_target_pairs={{0,1},{1,0},{2,3},{3,2},{4,5},{5,4},{6,7},{7,6},{8,9},{9,8},{10,11... | collective-permute-start | bytes 1572872 | tf_op jit(solution)/shard_map/cond/branch_1_fun/ppermute | solution.py:149
  70.1 6.2 %collective-permute-start.6 = (bf16[512,512]{1,0:T(8,128)(2,1)}, bf16[512,512]{1,0:T(8,128)(2,1)}, u32[]{:S(2)}, u32[]{:S(2)}) collective-permute-start(bf16[512,512]{1,0:T(8,128)(2,1)} %collective-permute-done.2), channel_id=1, source_target_pairs={{0,1},{1,0},{2,3},{3,2},{4,5},{5,4},{6,7},{7,6},{8,9},{9,8},{10,11... | collective-permute-start | bytes 1572872 | tf_op jit(solution)/shard_map/cond/branch_1_fun/ppermute | solution.py:149
  92.7 35.5 %all-to-all-start.1 = ((f32[16,1,32]{2,1,0:T(1,128)}), f32[16,1,32]{2,1,0:T(1,128)S(1)}, u32[]{:S(2)}, u32[]{:S(2)}) async-start(f32[16,1,32]{2,1,0:T(1,128)} %broadcast_in_dim.48), calls=%async_computation.1 | async-start | bytes 16384 | tf_op jit(solution)/shard_map/all_to_all | solution.py:190

commit v7 on v5

--- a/solution.py
+++ b/solution.py
@@ -91,33 +91,47 @@
     )(packed, *preconds)
 
 
-def last_scores(packed, stack, before, length, columns):
-    def kernel(packed_ref, stack_ref, before_ref, out_ref):
+def last_scores(late, early, stack, before, length, columns):
+    def kernel(late_ref, early_ref, stack_ref, before_ref, out_ref, packed_ref):
+        packed_ref[...] = late_ref[...] + early_ref[...]
         preconds = [stack_ref.at[q] for q in range(stack_ref.shape[0])]
         out_ref[...] = before_ref[...] + packed_scores(packed_ref, preconds, length, columns)
 
     return pl.pallas_call(
         kernel,
         out_shape=jax.ShapeDtypeStruct(before.shape, jnp.float32),
-        in_specs=[VMEM] * 3,
+        in_specs=[VMEM] * 4,
         out_specs=VMEM,
+        scratch_shapes=[pltpu.VMEM(late.shape, late.dtype)],
         compiler_params=pltpu.CompilerParams(vmem_limit_bytes=40 << 20),
-    )(packed, stack, before)
+    )(late, early, stack, before)
 
 
-def gather_preconds(query_in, query_out, in_basis, out_basis, eigen_values):
+def precondition(query_in, query_out, in_basis, out_basis, eigen_values):
     side_in = project(query_in, in_basis)
     side_out = project(query_out, out_basis)
     moment = lax.dot_general(
         side_out, side_in, (((0,), (0,)), ((), ())), preferred_element_type=jnp.float32
     )
     scale = query_in.shape[0] * (eigen_values + damping)
-    precond = (moment / scale).astype(jnp.bfloat16)
-    along = [precond]
-    for step in range(1, X):
-        along.append(lax.ppermute(precond, "x", [(i, i ^ step) for i in range(X)]))
-    beside = [lax.ppermute(p, "core", SWAP) for p in along]
-    return along + beside
+    return (moment / scale).astype(jnp.bfloat16)
+
+
+def gather_preconds(precond):
+    one, two, three = [
+        lax.ppermute(precond, "x", [(i, i ^ step) for i in range(X)]) for step in range(1, X)
+    ]
+    precond, one = lax.optimization_barrier((precond, one))
+    other = lax.ppermute(precond, "core", SWAP)
+    other, one, two = lax.optimization_barrier((other, one, two))
+    return [precond, one, two, three, other] + [
+        lax.ppermute(p, "core", SWAP) for p in (one, two, three)
+    ]
+
+
+def swap_half(packed, places):
+    pairs = [(z * ZHI + i, z * ZHI + j) for z in places for i, j in SWAP]
+    return lax.ppermute(packed, ("zlo", "zhi"), pairs)
 
 
 def local(
@@ -140,15 +154,15 @@
     mine = pack_train(
         train_ids, train_in[0].reshape(tokens), train_out[0].reshape(tokens), in_basis, out_basis
     )
-    theirs = lax.ppermute(mine, "zhi", SWAP)
+    late = swap_half(mine, range(ZLO // 2, ZLO))
+    precond = precondition(query_in[0, 0], query_out[0, 0], in_basis, out_basis, eigen_values[0])
+    again, precond = lax.optimization_barrier((mine, precond))
+    early = swap_half(again, range(ZLO // 2))
     preconds = lax.cond(
-        lax.axis_index("x") < X,
-        gather_preconds,
-        lambda *ops: [jnp.zeros((width, width), jnp.bfloat16)] * (X * CORE),
-        query_in[0, 0], query_out[0, 0], in_basis, out_basis, eigen_values[0],
+        lax.axis_index("x") < X, gather_preconds, lambda precond: [precond] * (X * CORE), precond
     )
     stack, partial_mine = first_scores(mine, preconds, length, columns)
-    partial_value = last_scores(theirs, stack, partial_mine, length, columns)
+    partial_value = last_scores(late, early, stack, partial_mine, length, columns)
 
     k = jnp.arange(X * CORE, dtype=jnp.int32)
     owner = (lax.axis_index("x") ^ (k % X)) * CORE + (lax.axis_index("core") ^ (k // X))

time: 129 us -> 126 us (0.977)
  starting transfers between devices: 71.8 us -> 63.2 us
  waiting for transfers between devices: 31.6 us -> 38.9 us
    ppermute x8 -> x9, waiting for transfers between devices: 13.5 us -> 20.8 us  [the longest x3 19 us: gather_preconds(): lax.ppermute(precond, 'x', [(i, i ^ step) for i in range(X)])]
    all_to_all x1, starting transfers between devices: 15.7 us -> 9.38 us  [local(): summed = jnp.sum(lax.all_to_all(far, 'zlo', 0, 0), axis=0)]
    ppermute x8 -> x9, starting transfers between devices: 56.1 us -> 53.8 us  [the longest x2 30.3 us: swap_half(): return lax.ppermute(packed, ('zlo', 'zhi'), pairs)]
  transfers between devices with their start and end apart: 9 -> 10, of which waited for: 5 -> 4; matrix products, arithmetic and copies ran while one was open for 3% -> 3% of each run, Pallas kernels for 3% -> 2%
where the time goes in v7:
time: 126 us
  starting transfers between devices  63.2 us (50%)
  waiting for transfers between devices  38.9 us (31%)
  blocking collectives  11.8 us (9%)
  Pallas kernels  6.35 us (5%)
  matrix products  3.43 us (3%)
    ppermute x2, starting transfers between devices, swap_half(): return lax.ppermute(packed, ('zlo', 'zhi'), pairs)  30.3 us
    ppermute x3, waiting for transfers between devices, gather_preconds(): lax.ppermute(precond, 'x', [(i, i ^ step) for i in range(X)])  19 us
    all_to_all x1, waiting for transfers between devices, local(): summed = jnp.sum(lax.all_to_all(far, 'zlo', 0, 0), axis=0)  18.1 us
    all_to_all x1, blocking collectives, local(): near = jnp.sum(lax.all_to_all(spread, ('y', 'x', 'core'), 0, 0), axis=0)  11.8 us
    ppermute x3, starting transfers between devices, gather_preconds(): lax.ppermute(precond, 'x', [(i, i ^ step) for i in range(X)])  9.59 us
    all_to_all x1, starting transfers between devices, local(): summed = jnp.sum(lax.all_to_all(far, 'zlo', 0, 0), axis=0)  9.38 us
    ppermute x3, starting transfers between devices, gather_preconds(): lax.ppermute(p, 'core', SWAP)  8.66 us
    ppermute x1, starting transfers between devices, gather_preconds(): other = lax.ppermute(precond, 'core', SWAP)  5.24 us
  transfers between devices with their start and end apart: 10, of which 4 were waited for; matrix products, arithmetic and copies ran while one was open for 3% of the time, Pallas kernels for 2%

profile of v7, /device:TPU:1, one launch (start us, length us, event | category | flops | bytes accessed | tf_op | source)
XLA Modules:
  0.0 125.8 jit_solution(5313740763474900485)
XLA Ops:
  0.0 0.0 copy-start
  0.0 2.4 %shard_map.91.packed_ref = bf16[1032,128]{1,0:T(8,128)(2,1)} custom-call(s32[2]{0:T(128)} %ids_ref.1, f32[128,512]{1,0:T(8,128)} %bitcast.27, f32[128,512]{1,0:T(8,128)} %bitcast.28, bf16[512,512]{1,0:T(8,128)(2,1)} %bitcast.25, bf16[512,512]{1,0:T(8,128)(2,1)} %bitcast.26), custom_call_target="tpu_custom_call" | custom-call | tf_op jit(solution)/shard_map/pallas_call | solution.py:44
  2.4 0.0 copy-start.1
  2.4 0.8 collective-permute-start.7
  3.2 1.4 %convolution_convert_fusion = bf16[256,512]{1,0:T(8,128)(2,1)S(1)} fusion(bf16[1,1,256,512]{3,2,1,0:T(8,128)(2,1)} %param.13, bf16[1,512,512]{2,1,0:T(8,128)(2,1)} %param.15), kind=kOutput, calls=%fused_computation.2 | convolution fusion | flops 134348800 | bytes 1048576 | tf_op jit(solution)/shard_map/dot_general | solution.py:24
  4.7 0.0 copy-done
  4.7 2.0 %fusion = bf16[512,512]{1,0:T(8,128)(2,1)S(1)} fusion(bf16[256,512]{1,0:T(8,128)(2,1)S(1)} %convolution_convert_fusion, f32[1,512,512]{2,1,0:T(8,128)} %param.17, bf16[1,1,256,512]{3,2,1,0:T(8,128)(2,1)S(1)} %copy-done, bf16[1,512,512]{2,1,0:T(8,128)(2,1)} %param.16), kind=kOutput, calls=%fused_computation.1 | convolution fusion | flops 269615104 | bytes 2621440 | tf_op jit(solution)/shard_map/dot_general | solution.py:113
  6.7 0.0 copy-done.1
  6.7 29.5 %collective-permute-start.8 = (bf16[1032,128]{1,0:T(8,128)(2,1)S(1)}, bf16[1032,128]{1,0:T(8,128)(2,1)S(1)}, u32[]{:S(2)}, u32[]{:S(2)}) collective-permute-start(bf16[1032,128]{1,0:T(8,128)(2,1)S(1)} %copy-done.1), channel_id=1, source_target_pairs={{0,8},{8,0},{64,72},{72,64},{128,136},{136,128},{192,200},{200,192... | collective-permute-start | bytes 792584 | tf_op jit(solution)/shard_map/ppermute | solution.py:134
  36.3 44.4 %conditional.1 = (bf16[512,512]{1,0:T(8,128)(2,1)S(1)}, bf16[512,512]{1,0:T(8,128)(2,1)}, bf16[512,512]{1,0:T(8,128)(2,1)}, bf16[512,512]{1,0:T(8,128)(2,1)}, bf...) conditional(s32[]{:T(128)} %convert_element_type.15, ...), branch_computations={%region_0.0_spmd, %region_1.0_spmd} | conditional | bytes 14680408 | solution.py:161
  36.3 3.1 %collective-permute-start = (bf16[512,512]{1,0:T(8,128)(2,1)S(1)}, bf16[512,512]{1,0:T(8,128)(2,1)}, u32[]{:S(2)}, u32[]{:S(2)}) collective-permute-start(bf16[512,512]{1,0:T(8,128)(2,1)S(1)} %param.1), channel_id=1, source_target_pairs={{0,2},{2,0},{4,6},{6,4},{1,3},{3,1},{5,7},{7,5},{8,10},{10,8},{12,... | collective-permute-start | bytes 1572872 | tf_op jit(solution)/shard_map/cond/branch_1_fun/ppermute | solution.py:122
  39.4 4.4 %collective-permute-start.2 = (bf16[512,512]{1,0:T(8,128)(2,1)S(1)}, bf16[512,512]{1,0:T(8,128)(2,1)}, u32[]{:S(2)}, u32[]{:S(2)}) collective-permute-start(bf16[512,512]{1,0:T(8,128)(2,1)S(1)} %param.1), channel_id=1, source_target_pairs={{0,4},{2,6},{4,0},{6,2},{1,5},{3,7},{5,1},{7,3},{8,12},{10,14},{12... | collective-permute-start | bytes 1572872 | tf_op jit(solution)/shard_map/cond/branch_1_fun/ppermute | solution.py:122
  43.8 2.1 %collective-permute-start.3 = (bf16[512,512]{1,0:T(8,128)(2,1)S(1)}, bf16[512,512]{1,0:T(8,128)(2,1)}, u32[]{:S(2)}, u32[]{:S(2)}) collective-permute-start(bf16[512,512]{1,0:T(8,128)(2,1)S(1)} %param.1), channel_id=1, source_target_pairs={{0,6},{2,4},{4,2},{6,0},{1,7},{3,5},{5,3},{7,1},{8,14},{10,12},{12... | collective-permute-start | bytes 1572872 | tf_op jit(solution)/shard_map/cond/branch_1_fun/ppermute | solution.py:122
  45.9 4.9 %collective-permute-done = bf16[512,512]{1,0:T(8,128)(2,1)} collective-permute-done((bf16[512,512]{1,0:T(8,128)(2,1)S(1)}, bf16[512,512]{1,0:T(8,128)(2,1)}, u32[]{:S(2)}, u32[]{:S(2)}) %collective-permute-start) | collective-permute-done | bytes 524320 | tf_op jit(solution)/shard_map/cond/branch_1_fun/ppermute | solution.py:122
  50.7 5.2 %collective-permute-start.1 = (bf16[512,512]{1,0:T(8,128)(2,1)S(1)}, bf16[512,512]{1,0:T(8,128)(2,1)}, u32[]{:S(2)}, u32[]{:S(2)}) collective-permute-start(bf16[512,512]{1,0:T(8,128)(2,1)S(1)} %param.1), channel_id=1, source_target_pairs={{0,1},{1,0},{2,3},{3,2},{4,5},{5,4},{6,7},{7,6},{8,9},{9,8},{10,11... | collective-permute-start | bytes 1572872 | tf_op jit(solution)/shard_map/cond/branch_1_fun/ppermute | solution.py:125
  56.0 14.1 %collective-permute-done.3 = bf16[512,512]{1,0:T(8,128)(2,1)} collective-permute-done((bf16[512,512]{1,0:T(8,128)(2,1)S(1)}, bf16[512,512]{1,0:T(8,128)(2,1)}, u32[]{:S(2)}, u32[]{:S(2)}) %collective-permute-start.3) | collective-permute-done | bytes 524320 | tf_op jit(solution)/shard_map/cond/branch_1_fun/ppermute | solution.py:122
  70.1 4.3 %collective-permute-start.6 = (bf16[512,512]{1,0:T(8,128)(2,1)}, bf16[512,512]{1,0:T(8,128)(2,1)}, u32[]{:S(2)}, u32[]{:S(2)}) collective-permute-start(bf16[512,512]{1,0:T(8,128)(2,1)} %collective-permute-done.3), channel_id=1, source_target_pairs={{0,1},{1,0},{2,3},{3,2},{4,5},{5,4},{6,7},{7,6},{8,9},{9,8},{10,11... | collective-permute-start | bytes 1572872 | tf_op jit(solution)/shard_map/cond/branch_1_fun/ppermute | solution.py:128
  74.4 0.0 collective-permute-done.2
  74.5 0.0 collective-permute-done.1
  74.5 1.9 %collective-permute-start.4 = (bf16[512,512]{1,0:T(8,128)(2,1)}, bf16[512,512]{1,0:T(8,128)(2,1)}, u32[]{:S(2)}, u32[]{:S(2)}) collective-permute-start(bf16[512,512]{1,0:T(8,128)(2,1)} %collective-permute-done), channel_id=1, source_target_pairs={{0,1},{1,0},{2,3},{3,2},{4,5},{5,4},{6,7},{7,6},{8,9},{9,8},{10,11... | collective-permute-start | bytes 1572872 | tf_op jit(solution)/shard_map/cond/branch_1_fun/ppermute | solution.py:128
  76.4 2.4 %collective-permute-start.5 = (bf16[512,512]{1,0:T(8,128)(2,1)}, bf16[512,512]{1,0:T(8,128)(2,1)}, u32[]{:S(2)}, u32[]{:S(2)}) collective-permute-start(bf16[512,512]{1,0:T(8,128)(2,1)} %collective-permute-done.2), channel_id=1, source_target_pairs={{0,1},{1,0},{2,3},{3,2},{4,5},{5,4},{6,7},{7,6},{8,9},{9,8},{10,11... | collective-permute-start | bytes 1572872 | tf_op jit(solution)/shard_map/cond/branch_1_fun/ppermute | solution.py:128
  78.8 0.0 collective-permute-done.6
  78.8 0.0 collective-permute-done.4
  78.8 1.8 %collective-permute-done.5 = bf16[512,512]{1,0:T(8,128)(2,1)} collective-permute-done((bf16[512,512]{1,0:T(8,128)(2,1)}, bf16[512,512]{1,0:T(8,128)(2,1)}, u32[]{:S(2)}, u32[]{:S(2)}) %collective-permute-start.5) | collective-permute-done | bytes 524320 | tf_op jit(solution)/shard_map/cond/branch_1_fun/ppermute | solution.py:128
  80.7 3.1 %shard_map.92 = (bf16[8,512,512]{2,1,0:T(8,128)(2,1)S(1)}, f32[8,32]{1,0:T(8,128)S(1)}) custom-call(bf16[1032,128]{1,0:T(8,128)(2,1)S(1)} %copy-done.1, bf16[512,512]{1,0:T(8,128)(2,1)S(1)} %get-tuple-element.26.refs_0_, bf16[512,512]{1,0:T(8,128)(2,1)} %get-tuple-element.27.refs_1_, bf16[512,512]{1,0:T(8,128)(2,1)} %get-tuple-element.28.refs_2_, ...), custom_call_target="tpu_custom_call" | custom-call | tf_op jit(solution)/shard_map/pallas_call | solution.py:82
  83.7 0.0 collective-permute-done.8.early_ref
  83.8 0.0 collective-permute-done.7.late_ref
  83.8 0.9 shard_map.93
  84.6 0.1 select_reduce_fusion
  84.7 11.8 %all_to_all.15 = f32[32,1,32]{2,1,0:T(1,128)S(1)} all-to-all(f32[32,1,32]{2,1,0:T(1,128)S(1)} %bitcast.29), channel_id=1, replica_groups=mesh['zlo'=16,'y'=4,'zhi'=2,'x'=4,'core'=2] {'y','x','core'}, dimensions={0} | all-to-all | bytes 8192 | tf_op jit(solution)/shard_map/all_to_all | solution.py:174
  96.5 0.1 reduce_sum.28
  96.5 0.6 broadcast_in_dim.48
  97.1 9.4 %all-to-all-start.1 = ((f32[16,1,32]{2,1,0:T(1,128)}), f32[16,1,32]{2,1,0:T(1,128)S(1)}, u32[]{:S(2)}, u32[]{:S(2)}) async-start(f32[16,1,32]{2,1,0:T(1,128)} %broadcast_in_dim.48), calls=%async_computation.1 | async-start | bytes 16384 | tf_op jit(solution)/shard_map/all_to_all | solution.py:176
  107.2 18.1 %all-to-all-done.1 = f32[16,1,32]{2,1,0:T(1,128)S(1)} async-done(((f32[16,1,32]{2,1,0:T(1,128)}), f32[16,1,32]{2,1,0:T(1,128)S(1)}, u32[]{:S(2)}, u32[]{:S(2)}) %all-to-all-start.1) | async-done | bytes 2080 | tf_op jit(solution)/shard_map/all_to_all | solution.py:176
  125.3 0.5 compare_select_fusion
  (4 shorter events, 0.0 us)
Async XLA Ops:
  0.0 4.7 %copy-start = (bf16[1,1,256,512]{3,2,1,0:T(8,128)(2,1)S(1)}, bf16[1,1,256,512]{3,2,1,0:T(8,128)(2,1)}, u32[]{:S(2)}) copy-start(bf16[1,1,256,512]{3,2,1,0:T(8,128)(2,1)} %param.14) | copy-start | bytes 786436
  2.4 4.3 %copy-start.1 = (bf16[1032,128]{1,0:T(8,128)(2,1)S(1)}, bf16[1032,128]{1,0:T(8,128)(2,1)}, u32[]{:S(2)}) copy-start(bf16[1032,128]{1,0:T(8,128)(2,1)} %shard_map.91.packed_ref) | copy-start | bytes 792580
  2.4 81.3 %collective-permute-start.7 = (bf16[1032,128]{1,0:T(8,128)(2,1)}, bf16[1032,128]{1,0:T(8,128)(2,1)S(1)}, u32[]{:S(2)}, u32[]{:S(2)}) collective-permute-start(bf16[1032,128]{1,0:T(8,128)(2,1)} %shard_map.91.packed_ref), channel_id=1, source_target_pairs={{512,520},{520,512},{576,584},{584,576},{640,648},{648,640},{704,7... | collective-permute-start | bytes 792584 | tf_op jit(solution)/shard_map/ppermute | solution.py:134
  6.7 77.0 %collective-permute-start.8 = (bf16[1032,128]{1,0:T(8,128)(2,1)S(1)}, bf16[1032,128]{1,0:T(8,128)(2,1)S(1)}, u32[]{:S(2)}, u32[]{:S(2)}) collective-permute-start(bf16[1032,128]{1,0:T(8,128)(2,1)S(1)} %copy-done.1), channel_id=1, source_target_pairs={{0,8},{8,0},{64,72},{72,64},{128,136},{136,128},{192,200},{200,192... | collective-permute-start | bytes 792584 | tf_op jit(solution)/shard_map/ppermute | solution.py:134
  36.3 14.5 %collective-permute-start = (bf16[512,512]{1,0:T(8,128)(2,1)S(1)}, bf16[512,512]{1,0:T(8,128)(2,1)}, u32[]{:S(2)}, u32[]{:S(2)}) collective-permute-start(bf16[512,512]{1,0:T(8,128)(2,1)S(1)} %param.1), channel_id=1, source_target_pairs={{0,2},{2,0},{4,6},{6,4},{1,3},{3,1},{5,7},{7,5},{8,10},{10,8},{12,... | collective-permute-start | bytes 1572872 | tf_op jit(solution)/shard_map/cond/branch_1_fun/ppermute | solution.py:122
  39.4 35.1 %collective-permute-start.2 = (bf16[512,512]{1,0:T(8,128)(2,1)S(1)}, bf16[512,512]{1,0:T(8,128)(2,1)}, u32[]{:S(2)}, u32[]{:S(2)}) collective-permute-start(bf16[512,512]{1,0:T(8,128)(2,1)S(1)} %param.1), channel_id=1, source_target_pairs={{0,4},{2,6},{4,0},{6,2},{1,5},{3,7},{5,1},{7,3},{8,12},{10,14},{12... | collective-permute-start | bytes 1572872 | tf_op jit(solution)/shard_map/cond/branch_1_fun/ppermute | solution.py:122
  43.8 26.3 %collective-permute-start.3 = (bf16[512,512]{1,0:T(8,128)(2,1)S(1)}, bf16[512,512]{1,0:T(8,128)(2,1)}, u32[]{:S(2)}, u32[]{:S(2)}) collective-permute-start(bf16[512,512]{1,0:T(8,128)(2,1)S(1)} %param.1), channel_id=1, source_target_pairs={{0,6},{2,4},{4,2},{6,0},{1,7},{3,5},{5,3},{7,1},{8,14},{10,12},{12... | collective-permute-start | bytes 1572872 | tf_op jit(solution)/shard_map/cond/branch_1_fun/ppermute | solution.py:122
  50.7 23.7 %collective-permute-start.1 = (bf16[512,512]{1,0:T(8,128)(2,1)S(1)}, bf16[512,512]{1,0:T(8,128)(2,1)}, u32[]{:S(2)}, u32[]{:S(2)}) collective-permute-start(bf16[512,512]{1,0:T(8,128)(2,1)S(1)} %param.1), channel_id=1, source_target_pairs={{0,1},{1,0},{2,3},{3,2},{4,5},{5,4},{6,7},{7,6},{8,9},{9,8},{10,11... | collective-permute-start | bytes 1572872 | tf_op jit(solution)/shard_map/cond/branch_1_fun/ppermute | solution.py:125
  70.1 8.7 %collective-permute-start.6 = (bf16[512,512]{1,0:T(8,128)(2,1)}, bf16[512,512]{1,0:T(8,128)(2,1)}, u32[]{:S(2)}, u32[]{:S(2)}) collective-permute-start(bf16[512,512]{1,0:T(8,128)(2,1)} %collective-permute-done.3), channel_id=1, source_target_pairs={{0,1},{1,0},{2,3},{3,2},{4,5},{5,4},{6,7},{7,6},{8,9},{9,8},{10,11... | collective-permute-start | bytes 1572872 | tf_op jit(solution)/shard_map/cond/branch_1_fun/ppermute | solution.py:128
  74.5 4.4 %collective-permute-start.4 = (bf16[512,512]{1,0:T(8,128)(2,1)}, bf16[512,512]{1,0:T(8,128)(2,1)}, u32[]{:S(2)}, u32[]{:S(2)}) collective-permute-start(bf16[512,512]{1,0:T(8,128)(2,1)} %collective-permute-done), channel_id=1, source_target_pairs={{0,1},{1,0},{2,3},{3,2},{4,5},{5,4},{6,7},{7,6},{8,9},{9,8},{10,11... | collective-permute-start | bytes 1572872 | tf_op jit(solution)/shard_map/cond/branch_1_fun/ppermute | solution.py:128
  76.4 4.3 %collective-permute-start.5 = (bf16[512,512]{1,0:T(8,128)(2,1)}, bf16[512,512]{1,0:T(8,128)(2,1)}, u32[]{:S(2)}, u32[]{:S(2)}) collective-permute-start(bf16[512,512]{1,0:T(8,128)(2,1)} %collective-permute-done.2), channel_id=1, source_target_pairs={{0,1},{1,0},{2,3},{3,2},{4,5},{5,4},{6,7},{7,6},{8,9},{9,8},{10,11... | collective-permute-start | bytes 1572872 | tf_op jit(solution)/shard_map/cond/branch_1_fun/ppermute | solution.py:128
  97.1 28.1 %all-to-all-start.1 = ((f32[16,1,32]{2,1,0:T(1,128)}), f32[16,1,32]{2,1,0:T(1,128)S(1)}, u32[]{:S(2)}, u32[]{:S(2)}) async-start(f32[16,1,32]{2,1,0:T(1,128)} %broadcast_in_dim.48), calls=%async_computation.1 | async-start | bytes 16384 | tf_op jit(solution)/shard_map/all_to_all | solution.py:176

commit v8 on v7

--- a/solution.py
+++ b/solution.py
@@ -46,6 +46,9 @@
         out_shape=jax.ShapeDtypeStruct((2 * tokens * width // LANES + EXTRA, LANES), jnp.bfloat16),
         in_specs=[SMEM] + [VMEM] * 4,
         out_specs=VMEM,
+        cost_estimate=pl.CostEstimate(
+            flops=400 * tokens * width * width, transcendentals=0, bytes_accessed=12 * tokens * width
+        ),
     )(train_ids, train_in, train_out, in_basis, out_basis)
 
 
@@ -70,14 +73,27 @@
     return total
 
 
+class Arriving:
+    def __init__(self, ref, copy):
+        self.ref, self.copy, self.shape = ref, copy, ref.shape
+
+    def __getitem__(self, at):
+        self.copy.wait()
+        return self.ref[at]
+
+
 def first_scores(packed, preconds, length, columns):
     count = len(preconds)
 
     def kernel(packed_ref, *refs):
-        stack_ref, out_ref = refs[-2:]
-        out_ref[...] = packed_scores(packed_ref, refs[:count], length, columns)
-        for q in range(count):
-            stack_ref[q] = refs[q][...]
+        stack_ref, out_ref, sems = refs[-3:]
+        copies = [
+            pltpu.make_async_copy(refs[q], stack_ref.at[q], sems.at[q]) for q in range(count)
+        ]
+        for copy in copies:
+            copy.start()
+        arriving = [Arriving(stack_ref.at[q], copies[q]) for q in range(count)]
+        out_ref[...] = packed_scores(packed_ref, arriving, length, columns)
 
     return pl.pallas_call(
         kernel,
@@ -85,8 +101,9 @@
             jax.ShapeDtypeStruct((count,) + preconds[0].shape, jnp.bfloat16),
             jax.ShapeDtypeStruct((count, columns), jnp.float32),
         ],
-        in_specs=[VMEM] * (1 + count),
+        in_specs=[VMEM] + [pl.BlockSpec(memory_space=pl.ANY)] * count,
         out_specs=[VMEM] * 2,
+        scratch_shapes=[pltpu.SemaphoreType.DMA((count,))],
         compiler_params=pltpu.CompilerParams(vmem_limit_bytes=40 << 20),
     )(packed, *preconds)
 
@@ -123,7 +140,7 @@
     ]
     precond, one = lax.optimization_barrier((precond, one))
     other = lax.ppermute(precond, "core", SWAP)
-    other, one, two = lax.optimization_barrier((other, one, two))
+    one, other = lax.optimization_barrier((one, other))
     return [precond, one, two, three, other] + [
         lax.ppermute(p, "core", SWAP) for p in (one, two, three)
     ]

time: 126 us -> 129 us (1.024)
  starting transfers between devices: 63.2 us -> 72.3 us
  waiting for transfers between devices: 38.9 us -> 35.5 us
  matrix products: 3.43 us -> 0.92 us
    all_to_all x1, starting transfers between devices: 9.38 us -> 17.1 us  [local(): summed = jnp.sum(lax.all_to_all(far, 'zlo', 0, 0), axis=0)]
    ppermute x3, waiting for transfers between devices: 19 us -> 15.2 us  [gather_preconds(): lax.ppermute(precond, 'x', [(i, i ^ step) for i in range(X)])]
    ppermute x3, starting transfers between devices: 8.66 us -> 10.1 us  [gather_preconds(): lax.ppermute(p, 'core', SWAP)]
    dot_general x1, matrix products: 2.01 us -> 0.62 us  [precondition(): lax.dot_general(side_out, side_in, (((0,), (0,)), ((), ())), preferred_el...]
  transfers between devices with their start and end apart: 10 -> 10, of which waited for: 4 -> 5; matrix products, arithmetic and copies ran while one was open for 3% -> 1% of each run, Pallas kernels for 2% -> 2%
where the time goes in v8:
time: 129 us
  starting transfers between devices  72.3 us (56%)
  waiting for transfers between devices  35.5 us (28%)
  blocking collectives  11.5 us (9%)
  Pallas kernels  6.42 us (5%)
    ppermute x2, starting transfers between devices, swap_half(): return lax.ppermute(packed, ('zlo', 'zhi'), pairs)  30.3 us
    all_to_all x1, waiting for transfers between devices, local(): summed = jnp.sum(lax.all_to_all(far, 'zlo', 0, 0), axis=0)  18.1 us
    all_to_all x1, starting transfers between devices, local(): summed = jnp.sum(lax.all_to_all(far, 'zlo', 0, 0), axis=0)  17.1 us
    ppermute x3, waiting for transfers between devices, gather_preconds(): lax.ppermute(precond, 'x', [(i, i ^ step) for i in range(X)])  15.2 us
    all_to_all x1, blocking collectives, local(): near = jnp.sum(lax.all_to_all(spread, ('y', 'x', 'core'), 0, 0), axis=0)  11.5 us
    ppermute x3, starting transfers between devices, gather_preconds(): lax.ppermute(p, 'core', SWAP)  10.1 us
    ppermute x3, starting transfers between devices, gather_preconds(): lax.ppermute(precond, 'x', [(i, i ^ step) for i in range(X)])  9.59 us
    ppermute x1, starting transfers between devices, gather_preconds(): other = lax.ppermute(precond, 'core', SWAP)  5.24 us
  transfers between devices with their start and end apart: 10, of which 5 were waited for; matrix products, arithmetic and copies ran while one was open for 1% of the time, Pallas kernels for 2%

profile of v8, /device:TPU:1, one launch (start us, length us, event | category | flops | bytes accessed | tf_op | source)
XLA Modules:
  0.0 128.9 jit_solution(3662474611321147486)
XLA Ops:
  0.0 0.0 copy-start
  0.0 0.0 copy-start.2
  0.0 0.0 copy-start.3
  0.0 0.0 copy-start.4
  0.0 0.0 copy-start.5
  0.0 2.5 %shard_map.91.packed_ref = bf16[1032,128]{1,0:T(8,128)(2,1)} custom-call(s32[2]{0:T(128)} %ids_ref.1, f32[128,512]{1,0:T(8,128)} %bitcast.29, f32[128,512]{1,0:T(8,128)} %bitcast.30, bf16[512,512]{1,0:T(8,128)(2,1)} %bitcast.25, bf16[512,512]{1,0:T(8,128)(2,1)} %bitcast.28), custom_call_target="tpu_custom_call" | custom-call | flops 13421772800 | bytes 786432 | tf_op jit(solution)/shard_map/pallas_call | solution.py:44
  2.6 0.0 copy-start.1
  2.6 0.8 collective-permute-start.7
  3.4 0.0 copy-done.2
  3.4 0.0 copy-done.3
  3.4 0.3 convolution_convert_fusion
  3.7 0.0 copy-done
  3.7 0.0 copy-done.4
  3.7 0.0 copy-done.5
  3.7 0.6 fusion
  4.4 0.0 copy-done.1
  4.4 29.5 %collective-permute-start.8 = (bf16[1032,128]{1,0:T(8,128)(2,1)S(1)}, bf16[1032,128]{1,0:T(8,128)(2,1)S(1)}, u32[]{:S(2)}, u32[]{:S(2)}) collective-permute-start(bf16[1032,128]{1,0:T(8,128)(2,1)S(1)} %copy-done.1), channel_id=1, source_target_pairs={{0,8},{8,0},{64,72},{72,64},{128,136},{136,128},{192,200},{200,192... | collective-permute-start | bytes 792584 | tf_op jit(solution)/shard_map/ppermute | solution.py:151
  33.9 42.4 %conditional.1 = (bf16[512,512]{1,0:T(8,128)(2,1)S(1)}, bf16[512,512]{1,0:T(8,128)(2,1)}, bf16[512,512]{1,0:T(8,128)(2,1)}, bf16[512,512]{1,0:T(8,128)(2,1)}, bf...) conditional(s32[]{:T(128)} %convert_element_type.15, ...), branch_computations={%region_0.0_spmd, %region_1.0_spmd} | conditional | bytes 14680408 | solution.py:178
  33.9 3.1 %collective-permute-start = (bf16[512,512]{1,0:T(8,128)(2,1)S(1)}, bf16[512,512]{1,0:T(8,128)(2,1)}, u32[]{:S(2)}, u32[]{:S(2)}) collective-permute-start(bf16[512,512]{1,0:T(8,128)(2,1)S(1)} %param.1), channel_id=1, source_target_pairs={{0,2},{2,0},{4,6},{6,4},{1,3},{3,1},{5,7},{7,5},{8,10},{10,8},{12,... | collective-permute-start | bytes 1572872 | tf_op jit(solution)/shard_map/cond/branch_1_fun/ppermute | solution.py:139
  37.1 4.4 %collective-permute-start.2 = (bf16[512,512]{1,0:T(8,128)(2,1)S(1)}, bf16[512,512]{1,0:T(8,128)(2,1)}, u32[]{:S(2)}, u32[]{:S(2)}) collective-permute-start(bf16[512,512]{1,0:T(8,128)(2,1)S(1)} %param.1), channel_id=1, source_target_pairs={{0,4},{2,6},{4,0},{6,2},{1,5},{3,7},{5,1},{7,3},{8,12},{10,14},{12... | collective-permute-start | bytes 1572872 | tf_op jit(solution)/shard_map/cond/branch_1_fun/ppermute | solution.py:139
  41.4 2.1 %collective-permute-start.3 = (bf16[512,512]{1,0:T(8,128)(2,1)S(1)}, bf16[512,512]{1,0:T(8,128)(2,1)}, u32[]{:S(2)}, u32[]{:S(2)}) collective-permute-start(bf16[512,512]{1,0:T(8,128)(2,1)S(1)} %param.1), channel_id=1, source_target_pairs={{0,6},{2,4},{4,2},{6,0},{1,7},{3,5},{5,3},{7,1},{8,14},{10,12},{12... | collective-permute-start | bytes 1572872 | tf_op jit(solution)/shard_map/cond/branch_1_fun/ppermute | solution.py:139
  43.5 4.9 %collective-permute-done = bf16[512,512]{1,0:T(8,128)(2,1)} collective-permute-done((bf16[512,512]{1,0:T(8,128)(2,1)S(1)}, bf16[512,512]{1,0:T(8,128)(2,1)}, u32[]{:S(2)}, u32[]{:S(2)}) %collective-permute-start) | collective-permute-done | bytes 524320 | tf_op jit(solution)/shard_map/cond/branch_1_fun/ppermute | solution.py:139
  48.4 5.2 %collective-permute-start.1 = (bf16[512,512]{1,0:T(8,128)(2,1)S(1)}, bf16[512,512]{1,0:T(8,128)(2,1)}, u32[]{:S(2)}, u32[]{:S(2)}) collective-permute-start(bf16[512,512]{1,0:T(8,128)(2,1)S(1)} %param.1), channel_id=1, source_target_pairs={{0,1},{1,0},{2,3},{3,2},{4,5},{5,4},{6,7},{7,6},{8,9},{9,8},{10,11... | collective-permute-start | bytes 1572872 | tf_op jit(solution)/shard_map/cond/branch_1_fun/ppermute | solution.py:142
  53.6 8.2 %collective-permute-done.2 = bf16[512,512]{1,0:T(8,128)(2,1)} collective-permute-done((bf16[512,512]{1,0:T(8,128)(2,1)S(1)}, bf16[512,512]{1,0:T(8,128)(2,1)}, u32[]{:S(2)}, u32[]{:S(2)}) %collective-permute-start.2) | collective-permute-done | bytes 524320 | tf_op jit(solution)/shard_map/cond/branch_1_fun/ppermute | solution.py:139
  61.9 3.8 %collective-permute-start.5 = (bf16[512,512]{1,0:T(8,128)(2,1)}, bf16[512,512]{1,0:T(8,128)(2,1)}, u32[]{:S(2)}, u32[]{:S(2)}) collective-permute-start(bf16[512,512]{1,0:T(8,128)(2,1)} %collective-permute-done.2), channel_id=1, source_target_pairs={{0,1},{1,0},{2,3},{3,2},{4,5},{5,4},{6,7},{7,6},{8,9},{9,8},{10,11... | collective-permute-start | bytes 1572872 | tf_op jit(solution)/shard_map/cond/branch_1_fun/ppermute | solution.py:145
  65.7 2.1 %collective-permute-done.3 = bf16[512,512]{1,0:T(8,128)(2,1)} collective-permute-done((bf16[512,512]{1,0:T(8,128)(2,1)S(1)}, bf16[512,512]{1,0:T(8,128)(2,1)}, u32[]{:S(2)}, u32[]{:S(2)}) %collective-permute-start.3) | collective-permute-done | bytes 524320 | tf_op jit(solution)/shard_map/cond/branch_1_fun/ppermute | solution.py:139
  67.8 4.3 %collective-permute-start.6 = (bf16[512,512]{1,0:T(8,128)(2,1)}, bf16[512,512]{1,0:T(8,128)(2,1)}, u32[]{:S(2)}, u32[]{:S(2)}) collective-permute-start(bf16[512,512]{1,0:T(8,128)(2,1)} %collective-permute-done.3), channel_id=1, source_target_pairs={{0,1},{1,0},{2,3},{3,2},{4,5},{5,4},{6,7},{7,6},{8,9},{9,8},{10,11... | collective-permute-start | bytes 1572872 | tf_op jit(solution)/shard_map/cond/branch_1_fun/ppermute | solution.py:145
  72.1 0.0 collective-permute-done.1
  72.1 1.9 %collective-permute-start.4 = (bf16[512,512]{1,0:T(8,128)(2,1)}, bf16[512,512]{1,0:T(8,128)(2,1)}, u32[]{:S(2)}, u32[]{:S(2)}) collective-permute-start(bf16[512,512]{1,0:T(8,128)(2,1)} %collective-permute-done), channel_id=1, source_target_pairs={{0,1},{1,0},{2,3},{3,2},{4,5},{5,4},{6,7},{7,6},{8,9},{9,8},{10,11... | collective-permute-start | bytes 1572872 | tf_op jit(solution)/shard_map/cond/branch_1_fun/ppermute | solution.py:145
  74.1 0.0 collective-permute-done.5
  74.1 0.0 collective-permute-done.6
  74.1 2.2 %collective-permute-done.4 = bf16[512,512]{1,0:T(8,128)(2,1)} collective-permute-done((bf16[512,512]{1,0:T(8,128)(2,1)}, bf16[512,512]{1,0:T(8,128)(2,1)}, u32[]{:S(2)}, u32[]{:S(2)}) %collective-permute-start.4) | collective-permute-done | bytes 524320 | tf_op jit(solution)/shard_map/cond/branch_1_fun/ppermute | solution.py:145
  76.3 2.9 %shard_map.92 = (bf16[8,512,512]{2,1,0:T(8,128)(2,1)S(1)}, f32[8,32]{1,0:T(8,128)S(1)}) custom-call(bf16[1032,128]{1,0:T(8,128)(2,1)S(1)} %copy-done.1, bf16[512,512]{1,0:T(8,128)(2,1)S(1)} %get-tuple-element.25.refs_0_, bf16[512,512]{1,0:T(8,128)(2,1)} %get-tuple-element.26.refs_1_, bf16[512,512]{1,0:T(8,128)(2,1)} %get-tuple-element.27.refs_2_, ...), custom_call_target="tpu_custom_call" | custom-call | tf_op jit(solution)/shard_map/pallas_call | solution.py:98
  79.2 0.0 collective-permute-done.8.early_ref
  79.2 0.0 collective-permute-done.7.late_ref
  79.3 0.9 shard_map.93
  80.2 0.1 select_reduce_fusion
  80.3 11.5 %all_to_all.15 = f32[32,1,32]{2,1,0:T(1,128)S(1)} all-to-all(f32[32,1,32]{2,1,0:T(1,128)S(1)} %bitcast.26), channel_id=1, replica_groups=mesh['zlo'=16,'y'=4,'zhi'=2,'x'=4,'core'=2] {'y','x','core'}, dimensions={0} | all-to-all | bytes 8192 | tf_op jit(solution)/shard_map/all_to_all | solution.py:191
  91.8 0.1 reduce_sum.28
  91.9 0.6 broadcast_in_dim.48
  92.5 17.1 %all-to-all-start.1 = ((f32[16,1,32]{2,1,0:T(1,128)}), f32[16,1,32]{2,1,0:T(1,128)S(1)}, u32[]{:S(2)}, u32[]{:S(2)}) async-start(f32[16,1,32]{2,1,0:T(1,128)} %broadcast_in_dim.48), calls=%async_computation.1 | async-start | bytes 16384 | tf_op jit(solution)/shard_map/all_to_all | solution.py:193
  110.2 18.1 %all-to-all-done.1 = f32[16,1,32]{2,1,0:T(1,128)S(1)} async-done(((f32[16,1,32]{2,1,0:T(1,128)}), f32[16,1,32]{2,1,0:T(1,128)S(1)}, u32[]{:S(2)}, u32[]{:S(2)}) %all-to-all-start.1) | async-done | bytes 2080 | tf_op jit(solution)/shard_map/all_to_all | solution.py:193
  128.3 0.5 compare_select_fusion
  (4 shorter events, 0.0 us)
Async XLA Ops:
  0.0 3.7 %copy-start = (bf16[1,1,256,512]{3,2,1,0:T(8,128)(2,1)S(1)}, bf16[1,1,256,512]{3,2,1,0:T(8,128)(2,1)}, u32[]{:S(2)}) copy-start(bf16[1,1,256,512]{3,2,1,0:T(8,128)(2,1)} %param.14) | copy-start | bytes 786436
  0.0 3.4 %copy-start.2 = (bf16[1,512,512]{2,1,0:T(8,128)(2,1)S(1)}, bf16[1,512,512]{2,1,0:T(8,128)(2,1)}, u32[]{:S(2)}) copy-start(bf16[1,512,512]{2,1,0:T(8,128)(2,1)} %param.15) | copy-start | bytes 1572868
  0.0 3.4 %copy-start.3 = (bf16[1,1,256,512]{3,2,1,0:T(8,128)(2,1)S(1)}, bf16[1,1,256,512]{3,2,1,0:T(8,128)(2,1)}, u32[]{:S(2)}) copy-start(bf16[1,1,256,512]{3,2,1,0:T(8,128)(2,1)} %param.13) | copy-start | bytes 786436
  0.0 3.7 %copy-start.4 = (f32[1,512,512]{2,1,0:T(8,128)S(1)}, f32[1,512,512]{2,1,0:T(8,128)}, u32[]{:S(2)}) copy-start(f32[1,512,512]{2,1,0:T(8,128)} %param.17) | copy-start | bytes 3145732
  0.0 3.7 %copy-start.5 = (bf16[1,512,512]{2,1,0:T(8,128)(2,1)S(1)}, bf16[1,512,512]{2,1,0:T(8,128)(2,1)}, u32[]{:S(2)}) copy-start(bf16[1,512,512]{2,1,0:T(8,128)(2,1)} %param.16) | copy-start | bytes 1572868
  2.6 1.8 %copy-start.1 = (bf16[1032,128]{1,0:T(8,128)(2,1)S(1)}, bf16[1032,128]{1,0:T(8,128)(2,1)}, u32[]{:S(2)}) copy-start(bf16[1032,128]{1,0:T(8,128)(2,1)} %shard_map.91.packed_ref) | copy-start | bytes 792580
  2.6 76.7 %collective-permute-start.7 = (bf16[1032,128]{1,0:T(8,128)(2,1)}, bf16[1032,128]{1,0:T(8,128)(2,1)S(1)}, u32[]{:S(2)}, u32[]{:S(2)}) collective-permute-start(bf16[1032,128]{1,0:T(8,128)(2,1)} %shard_map.91.packed_ref), channel_id=1, source_target_pairs={{512,520},{520,512},{576,584},{584,576},{640,648},{648,640},{704,7... | collective-permute-start | bytes 792584 | tf_op jit(solution)/shard_map/ppermute | solution.py:151
  4.4 74.9 %collective-permute-start.8 = (bf16[1032,128]{1,0:T(8,128)(2,1)S(1)}, bf16[1032,128]{1,0:T(8,128)(2,1)S(1)}, u32[]{:S(2)}, u32[]{:S(2)}) collective-permute-start(bf16[1032,128]{1,0:T(8,128)(2,1)S(1)} %copy-done.1), channel_id=1, source_target_pairs={{0,8},{8,0},{64,72},{72,64},{128,136},{136,128},{192,200},{200,192... | collective-permute-start | bytes 792584 | tf_op jit(solution)/shard_map/ppermute | solution.py:151
  33.9 14.5 %collective-permute-start = (bf16[512,512]{1,0:T(8,128)(2,1)S(1)}, bf16[512,512]{1,0:T(8,128)(2,1)}, u32[]{:S(2)}, u32[]{:S(2)}) collective-permute-start(bf16[512,512]{1,0:T(8,128)(2,1)S(1)} %param.1), channel_id=1, source_target_pairs={{0,2},{2,0},{4,6},{6,4},{1,3},{3,1},{5,7},{7,5},{8,10},{10,8},{12,... | collective-permute-start | bytes 1572872 | tf_op jit(solution)/shard_map/cond/branch_1_fun/ppermute | solution.py:139
  37.1 24.8 %collective-permute-start.2 = (bf16[512,512]{1,0:T(8,128)(2,1)S(1)}, bf16[512,512]{1,0:T(8,128)(2,1)}, u32[]{:S(2)}, u32[]{:S(2)}) collective-permute-start(bf16[512,512]{1,0:T(8,128)(2,1)S(1)} %param.1), channel_id=1, source_target_pairs={{0,4},{2,6},{4,0},{6,2},{1,5},{3,7},{5,1},{7,3},{8,12},{10,14},{12... | collective-permute-start | bytes 1572872 | tf_op jit(solution)/shard_map/cond/branch_1_fun/ppermute | solution.py:139
  41.4 26.3 %collective-permute-start.3 = (bf16[512,512]{1,0:T(8,128)(2,1)S(1)}, bf16[512,512]{1,0:T(8,128)(2,1)}, u32[]{:S(2)}, u32[]{:S(2)}) collective-permute-start(bf16[512,512]{1,0:T(8,128)(2,1)S(1)} %param.1), channel_id=1, source_target_pairs={{0,6},{2,4},{4,2},{6,0},{1,7},{3,5},{5,3},{7,1},{8,14},{10,12},{12... | collective-permute-start | bytes 1572872 | tf_op jit(solution)/shard_map/cond/branch_1_fun/ppermute | solution.py:139
  48.4 23.7 %collective-permute-start.1 = (bf16[512,512]{1,0:T(8,128)(2,1)S(1)}, bf16[512,512]{1,0:T(8,128)(2,1)}, u32[]{:S(2)}, u32[]{:S(2)}) collective-permute-start(bf16[512,512]{1,0:T(8,128)(2,1)S(1)} %param.1), channel_id=1, source_target_pairs={{0,1},{1,0},{2,3},{3,2},{4,5},{5,4},{6,7},{7,6},{8,9},{9,8},{10,11... | collective-permute-start | bytes 1572872 | tf_op jit(solution)/shard_map/cond/branch_1_fun/ppermute | solution.py:142
  61.9 12.2 %collective-permute-start.5 = (bf16[512,512]{1,0:T(8,128)(2,1)}, bf16[512,512]{1,0:T(8,128)(2,1)}, u32[]{:S(2)}, u32[]{:S(2)}) collective-permute-start(bf16[512,512]{1,0:T(8,128)(2,1)} %collective-permute-done.2), channel_id=1, source_target_pairs={{0,1},{1,0},{2,3},{3,2},{4,5},{5,4},{6,7},{7,6},{8,9},{9,8},{10,11... | collective-permute-start | bytes 1572872 | tf_op jit(solution)/shard_map/cond/branch_1_fun/ppermute | solution.py:145
  67.8 6.3 %collective-permute-start.6 = (bf16[512,512]{1,0:T(8,128)(2,1)}, bf16[512,512]{1,0:T(8,128)(2,1)}, u32[]{:S(2)}, u32[]{:S(2)}) collective-permute-start(bf16[512,512]{1,0:T(8,128)(2,1)} %collective-permute-done.3), channel_id=1, source_target_pairs={{0,1},{1,0},{2,3},{3,2},{4,5},{5,4},{6,7},{7,6},{8,9},{9,8},{10,11... | collective-permute-start | bytes 1572872 | tf_op jit(solution)/shard_map/cond/branch_1_fun/ppermute | solution.py:145
  72.1 4.1 %collective-permute-start.4 = (bf16[512,512]{1,0:T(8,128)(2,1)}, bf16[512,512]{1,0:T(8,128)(2,1)}, u32[]{:S(2)}, u32[]{:S(2)}) collective-permute-start(bf16[512,512]{1,0:T(8,128)(2,1)} %collective-permute-done), channel_id=1, source_target_pairs={{0,1},{1,0},{2,3},{3,2},{4,5},{5,4},{6,7},{7,6},{8,9},{9,8},{10,11... | collective-permute-start | bytes 1572872 | tf_op jit(solution)/shard_map/cond/branch_1_fun/ppermute | solution.py:145
  92.5 35.9 %all-to-all-start.1 = ((f32[16,1,32]{2,1,0:T(1,128)}), f32[16,1,32]{2,1,0:T(1,128)S(1)}, u32[]{:S(2)}, u32[]{:S(2)}) async-start(f32[16,1,32]{2,1,0:T(1,128)} %broadcast_in_dim.48), calls=%async_computation.1 | async-start | bytes 16384 | tf_op jit(solution)/shard_map/all_to_all | solution.py:193

commit v9 on v8

--- a/solution.py
+++ b/solution.py
@@ -46,9 +46,6 @@
         out_shape=jax.ShapeDtypeStruct((2 * tokens * width // LANES + EXTRA, LANES), jnp.bfloat16),
         in_specs=[SMEM] + [VMEM] * 4,
         out_specs=VMEM,
-        cost_estimate=pl.CostEstimate(
-            flops=400 * tokens * width * width, transcendentals=0, bytes_accessed=12 * tokens * width
-        ),
     )(train_ids, train_in, train_out, in_basis, out_basis)
 
 

time: 129 us -> 126 us (0.977)
  starting transfers between devices: 72.3 us -> 67 us
  matrix products: 0.92 us -> 3.43 us
    all_to_all x1, starting transfers between devices: 17.1 us -> 11.8 us  [local(): summed = jnp.sum(lax.all_to_all(far, 'zlo', 0, 0), axis=0)]
    dot_general x1, matrix products: 0.62 us -> 2.01 us  [precondition(): lax.dot_general(side_out, side_in, (((0,), (0,)), ((), ())), preferred_el...]
  transfers between devices with their start and end apart: 10 -> 10, of which waited for: 5 -> 5; matrix products, arithmetic and copies ran while one was open for 1% -> 3% of each run, Pallas kernels for 2% -> 2%
where the time goes in v9:
time: 126 us
  starting transfers between devices  67 us (53%)
  waiting for transfers between devices  35.5 us (28%)
  blocking collectives  11.5 us (9%)
  Pallas kernels  6.21 us (5%)
  matrix products  3.43 us (3%)
    ppermute x2, starting transfers between devices, swap_half(): return lax.ppermute(packed, ('zlo', 'zhi'), pairs)  30.3 us
    all_to_all x1, waiting for transfers between devices, local(): summed = jnp.sum(lax.all_to_all(far, 'zlo', 0, 0), axis=0)  18.1 us
    ppermute x3, waiting for transfers between devices, gather_preconds(): lax.ppermute(precond, 'x', [(i, i ^ step) for i in range(X)])  15.2 us
    all_to_all x1, starting transfers between devices, local(): summed = jnp.sum(lax.all_to_all(far, 'zlo', 0, 0), axis=0)  11.8 us
    all_to_all x1, blocking collectives, local(): near = jnp.sum(lax.all_to_all(spread, ('y', 'x', 'core'), 0, 0), axis=0)  11.5 us
    ppermute x3, starting transfers between devices, gather_preconds(): lax.ppermute(p, 'core', SWAP)  10.1 us
    ppermute x3, starting transfers between devices, gather_preconds(): lax.ppermute(precond, 'x', [(i, i ^ step) for i in range(X)])  9.59 us
    ppermute x1, starting transfers between devices, gather_preconds(): other = lax.ppermute(precond, 'core', SWAP)  5.24 us
  transfers between devices with their start and end apart: 10, of which 5 were waited for; matrix products, arithmetic and copies ran while one was open for 3% of the time, Pallas kernels for 2%

profile of v9, /device:TPU:1, one launch (start us, length us, event | category | flops | bytes accessed | tf_op | source)
XLA Modules:
  0.0 125.8 jit_solution(15418656423139408193)
XLA Ops:
  0.0 0.0 copy-start
  0.0 2.4 %shard_map.91.packed_ref = bf16[1032,128]{1,0:T(8,128)(2,1)} custom-call(s32[2]{0:T(128)} %ids_ref.1, f32[128,512]{1,0:T(8,128)} %bitcast.27, f32[128,512]{1,0:T(8,128)} %bitcast.28, bf16[512,512]{1,0:T(8,128)(2,1)} %bitcast.25, bf16[512,512]{1,0:T(8,128)(2,1)} %bitcast.26), custom_call_target="tpu_custom_call" | custom-call | tf_op jit(solution)/shard_map/pallas_call | solution.py:44
  2.4 0.0 copy-start.1
  2.4 0.8 collective-permute-start.7
  3.2 1.4 %convolution_convert_fusion = bf16[256,512]{1,0:T(8,128)(2,1)S(1)} fusion(bf16[1,1,256,512]{3,2,1,0:T(8,128)(2,1)} %param.13, bf16[1,512,512]{2,1,0:T(8,128)(2,1)} %param.15), kind=kOutput, calls=%fused_computation.2 | convolution fusion | flops 134348800 | bytes 1048576 | tf_op jit(solution)/shard_map/dot_general | solution.py:24
  4.7 0.0 copy-done
  4.7 2.0 %fusion = bf16[512,512]{1,0:T(8,128)(2,1)S(1)} fusion(bf16[256,512]{1,0:T(8,128)(2,1)S(1)} %convolution_convert_fusion, f32[1,512,512]{2,1,0:T(8,128)} %param.17, bf16[1,1,256,512]{3,2,1,0:T(8,128)(2,1)S(1)} %copy-done, bf16[1,512,512]{2,1,0:T(8,128)(2,1)} %param.16), kind=kOutput, calls=%fused_computation.1 | convolution fusion | flops 269615104 | bytes 2621440 | tf_op jit(solution)/shard_map/dot_general | solution.py:127
  6.7 0.0 copy-done.1
  6.7 29.5 %collective-permute-start.8 = (bf16[1032,128]{1,0:T(8,128)(2,1)S(1)}, bf16[1032,128]{1,0:T(8,128)(2,1)S(1)}, u32[]{:S(2)}, u32[]{:S(2)}) collective-permute-start(bf16[1032,128]{1,0:T(8,128)(2,1)S(1)} %copy-done.1), channel_id=1, source_target_pairs={{0,8},{8,0},{64,72},{72,64},{128,136},{136,128},{192,200},{200,192... | collective-permute-start | bytes 792584 | tf_op jit(solution)/shard_map/ppermute | solution.py:148
  36.3 42.4 %conditional.1 = (bf16[512,512]{1,0:T(8,128)(2,1)S(1)}, bf16[512,512]{1,0:T(8,128)(2,1)}, bf16[512,512]{1,0:T(8,128)(2,1)}, bf16[512,512]{1,0:T(8,128)(2,1)}, bf...) conditional(s32[]{:T(128)} %convert_element_type.15, ...), branch_computations={%region_0.0_spmd, %region_1.0_spmd} | conditional | bytes 14680408 | solution.py:175
  36.3 3.1 %collective-permute-start = (bf16[512,512]{1,0:T(8,128)(2,1)S(1)}, bf16[512,512]{1,0:T(8,128)(2,1)}, u32[]{:S(2)}, u32[]{:S(2)}) collective-permute-start(bf16[512,512]{1,0:T(8,128)(2,1)S(1)} %param.1), channel_id=1, source_target_pairs={{0,2},{2,0},{4,6},{6,4},{1,3},{3,1},{5,7},{7,5},{8,10},{10,8},{12,... | collective-permute-start | bytes 1572872 | tf_op jit(solution)/shard_map/cond/branch_1_fun/ppermute | solution.py:136
  39.4 4.4 %collective-permute-start.2 = (bf16[512,512]{1,0:T(8,128)(2,1)S(1)}, bf16[512,512]{1,0:T(8,128)(2,1)}, u32[]{:S(2)}, u32[]{:S(2)}) collective-permute-start(bf16[512,512]{1,0:T(8,128)(2,1)S(1)} %param.1), channel_id=1, source_target_pairs={{0,4},{2,6},{4,0},{6,2},{1,5},{3,7},{5,1},{7,3},{8,12},{10,14},{12... | collective-permute-start | bytes 1572872 | tf_op jit(solution)/shard_map/cond/branch_1_fun/ppermute | solution.py:136
  43.8 2.1 %collective-permute-start.3 = (bf16[512,512]{1,0:T(8,128)(2,1)S(1)}, bf16[512,512]{1,0:T(8,128)(2,1)}, u32[]{:S(2)}, u32[]{:S(2)}) collective-permute-start(bf16[512,512]{1,0:T(8,128)(2,1)S(1)} %param.1), channel_id=1, source_target_pairs={{0,6},{2,4},{4,2},{6,0},{1,7},{3,5},{5,3},{7,1},{8,14},{10,12},{12... | collective-permute-start | bytes 1572872 | tf_op jit(solution)/shard_map/cond/branch_1_fun/ppermute | solution.py:136
  45.9 4.9 %collective-permute-done = bf16[512,512]{1,0:T(8,128)(2,1)} collective-permute-done((bf16[512,512]{1,0:T(8,128)(2,1)S(1)}, bf16[512,512]{1,0:T(8,128)(2,1)}, u32[]{:S(2)}, u32[]{:S(2)}) %collective-permute-start) | collective-permute-done | bytes 524320 | tf_op jit(solution)/shard_map/cond/branch_1_fun/ppermute | solution.py:136
  50.7 5.2 %collective-permute-start.1 = (bf16[512,512]{1,0:T(8,128)(2,1)S(1)}, bf16[512,512]{1,0:T(8,128)(2,1)}, u32[]{:S(2)}, u32[]{:S(2)}) collective-permute-start(bf16[512,512]{1,0:T(8,128)(2,1)S(1)} %param.1), channel_id=1, source_target_pairs={{0,1},{1,0},{2,3},{3,2},{4,5},{5,4},{6,7},{7,6},{8,9},{9,8},{10,11... | collective-permute-start | bytes 1572872 | tf_op jit(solution)/shard_map/cond/branch_1_fun/ppermute | solution.py:139
  56.0 8.2 %collective-permute-done.2 = bf16[512,512]{1,0:T(8,128)(2,1)} collective-permute-done((bf16[512,512]{1,0:T(8,128)(2,1)S(1)}, bf16[512,512]{1,0:T(8,128)(2,1)}, u32[]{:S(2)}, u32[]{:S(2)}) %collective-permute-start.2) | collective-permute-done | bytes 524320 | tf_op jit(solution)/shard_map/cond/branch_1_fun/ppermute | solution.py:136
  64.2 3.8 %collective-permute-start.5 = (bf16[512,512]{1,0:T(8,128)(2,1)}, bf16[512,512]{1,0:T(8,128)(2,1)}, u32[]{:S(2)}, u32[]{:S(2)}) collective-permute-start(bf16[512,512]{1,0:T(8,128)(2,1)} %collective-permute-done.2), channel_id=1, source_target_pairs={{0,1},{1,0},{2,3},{3,2},{4,5},{5,4},{6,7},{7,6},{8,9},{9,8},{10,11... | collective-permute-start | bytes 1572872 | tf_op jit(solution)/shard_map/cond/branch_1_fun/ppermute | solution.py:142
  68.0 2.1 %collective-permute-done.3 = bf16[512,512]{1,0:T(8,128)(2,1)} collective-permute-done((bf16[512,512]{1,0:T(8,128)(2,1)S(1)}, bf16[512,512]{1,0:T(8,128)(2,1)}, u32[]{:S(2)}, u32[]{:S(2)}) %collective-permute-start.3) | collective-permute-done | bytes 524320 | tf_op jit(solution)/shard_map/cond/branch_1_fun/ppermute | solution.py:136
  70.1 4.3 %collective-permute-start.6 = (bf16[512,512]{1,0:T(8,128)(2,1)}, bf16[512,512]{1,0:T(8,128)(2,1)}, u32[]{:S(2)}, u32[]{:S(2)}) collective-permute-start(bf16[512,512]{1,0:T(8,128)(2,1)} %collective-permute-done.3), channel_id=1, source_target_pairs={{0,1},{1,0},{2,3},{3,2},{4,5},{5,4},{6,7},{7,6},{8,9},{9,8},{10,11... | collective-permute-start | bytes 1572872 | tf_op jit(solution)/shard_map/cond/branch_1_fun/ppermute | solution.py:142
  74.4 0.0 collective-permute-done.1
  74.5 1.9 %collective-permute-start.4 = (bf16[512,512]{1,0:T(8,128)(2,1)}, bf16[512,512]{1,0:T(8,128)(2,1)}, u32[]{:S(2)}, u32[]{:S(2)}) collective-permute-start(bf16[512,512]{1,0:T(8,128)(2,1)} %collective-permute-done), channel_id=1, source_target_pairs={{0,1},{1,0},{2,3},{3,2},{4,5},{5,4},{6,7},{7,6},{8,9},{9,8},{10,11... | collective-permute-start | bytes 1572872 | tf_op jit(solution)/shard_map/cond/branch_1_fun/ppermute | solution.py:142
  76.4 0.0 collective-permute-done.5
  76.4 0.0 collective-permute-done.6
  76.4 2.2 %collective-permute-done.4 = bf16[512,512]{1,0:T(8,128)(2,1)} collective-permute-done((bf16[512,512]{1,0:T(8,128)(2,1)}, bf16[512,512]{1,0:T(8,128)(2,1)}, u32[]{:S(2)}, u32[]{:S(2)}) %collective-permute-start.4) | collective-permute-done | bytes 524320 | tf_op jit(solution)/shard_map/cond/branch_1_fun/ppermute | solution.py:142
  78.6 2.9 %shard_map.92 = (bf16[8,512,512]{2,1,0:T(8,128)(2,1)S(1)}, f32[8,32]{1,0:T(8,128)S(1)}) custom-call(bf16[1032,128]{1,0:T(8,128)(2,1)S(1)} %copy-done.1, bf16[512,512]{1,0:T(8,128)(2,1)S(1)} %get-tuple-element.25.refs_0_, bf16[512,512]{1,0:T(8,128)(2,1)} %get-tuple-element.26.refs_1_, bf16[512,512]{1,0:T(8,128)(2,1)} %get-tuple-element.27.refs_2_, ...), custom_call_target="tpu_custom_call" | custom-call | tf_op jit(solution)/shard_map/pallas_call | solution.py:95
  81.6 0.0 collective-permute-done.8.early_ref
  81.6 0.0 collective-permute-done.7.late_ref
  81.6 0.9 shard_map.93
  82.4 0.1 select_reduce_fusion
  82.5 11.5 %all_to_all.15 = f32[32,1,32]{2,1,0:T(1,128)S(1)} all-to-all(f32[32,1,32]{2,1,0:T(1,128)S(1)} %bitcast.29), channel_id=1, replica_groups=mesh['zlo'=16,'y'=4,'zhi'=2,'x'=4,'core'=2] {'y','x','core'}, dimensions={0} | all-to-all | bytes 8192 | tf_op jit(solution)/shard_map/all_to_all | solution.py:188
  94.1 0.1 reduce_sum.28
  94.1 0.6 broadcast_in_dim.48
  94.7 11.8 %all-to-all-start.1 = ((f32[16,1,32]{2,1,0:T(1,128)}), f32[16,1,32]{2,1,0:T(1,128)S(1)}, u32[]{:S(2)}, u32[]{:S(2)}) async-start(f32[16,1,32]{2,1,0:T(1,128)} %broadcast_in_dim.48), calls=%async_computation.1 | async-start | bytes 16384 | tf_op jit(solution)/shard_map/all_to_all | solution.py:190
  107.2 18.1 %all-to-all-done.1 = f32[16,1,32]{2,1,0:T(1,128)S(1)} async-done(((f32[16,1,32]{2,1,0:T(1,128)}), f32[16,1,32]{2,1,0:T(1,128)S(1)}, u32[]{:S(2)}, u32[]{:S(2)}) %all-to-all-start.1) | async-done | bytes 2080 | tf_op jit(solution)/shard_map/all_to_all | solution.py:190
  125.3 0.5 compare_select_fusion
  (4 shorter events, 0.0 us)
Async XLA Ops:
  0.0 4.7 %copy-start = (bf16[1,1,256,512]{3,2,1,0:T(8,128)(2,1)S(1)}, bf16[1,1,256,512]{3,2,1,0:T(8,128)(2,1)}, u32[]{:S(2)}) copy-start(bf16[1,1,256,512]{3,2,1,0:T(8,128)(2,1)} %param.14) | copy-start | bytes 786436
  2.4 4.3 %copy-start.1 = (bf16[1032,128]{1,0:T(8,128)(2,1)S(1)}, bf16[1032,128]{1,0:T(8,128)(2,1)}, u32[]{:S(2)}) copy-start(bf16[1032,128]{1,0:T(8,128)(2,1)} %shard_map.91.packed_ref) | copy-start | bytes 792580
  2.4 79.1 %collective-permute-start.7 = (bf16[1032,128]{1,0:T(8,128)(2,1)}, bf16[1032,128]{1,0:T(8,128)(2,1)S(1)}, u32[]{:S(2)}, u32[]{:S(2)}) collective-permute-start(bf16[1032,128]{1,0:T(8,128)(2,1)} %shard_map.91.packed_ref), channel_id=1, source_target_pairs={{512,520},{520,512},{576,584},{584,576},{640,648},{648,640},{704,7... | collective-permute-start | bytes 792584 | tf_op jit(solution)/shard_map/ppermute | solution.py:148
  6.7 74.9 %collective-permute-start.8 = (bf16[1032,128]{1,0:T(8,128)(2,1)S(1)}, bf16[1032,128]{1,0:T(8,128)(2,1)S(1)}, u32[]{:S(2)}, u32[]{:S(2)}) collective-permute-start(bf16[1032,128]{1,0:T(8,128)(2,1)S(1)} %copy-done.1), channel_id=1, source_target_pairs={{0,8},{8,0},{64,72},{72,64},{128,136},{136,128},{192,200},{200,192... | collective-permute-start | bytes 792584 | tf_op jit(solution)/shard_map/ppermute | solution.py:148
  36.3 14.5 %collective-permute-start = (bf16[512,512]{1,0:T(8,128)(2,1)S(1)}, bf16[512,512]{1,0:T(8,128)(2,1)}, u32[]{:S(2)}, u32[]{:S(2)}) collective-permute-start(bf16[512,512]{1,0:T(8,128)(2,1)S(1)} %param.1), channel_id=1, source_target_pairs={{0,2},{2,0},{4,6},{6,4},{1,3},{3,1},{5,7},{7,5},{8,10},{10,8},{12,... | collective-permute-start | bytes 1572872 | tf_op jit(solution)/shard_map/cond/branch_1_fun/ppermute | solution.py:136
  39.4 24.8 %collective-permute-start.2 = (bf16[512,512]{1,0:T(8,128)(2,1)S(1)}, bf16[512,512]{1,0:T(8,128)(2,1)}, u32[]{:S(2)}, u32[]{:S(2)}) collective-permute-start(bf16[512,512]{1,0:T(8,128)(2,1)S(1)} %param.1), channel_id=1, source_target_pairs={{0,4},{2,6},{4,0},{6,2},{1,5},{3,7},{5,1},{7,3},{8,12},{10,14},{12... | collective-permute-start | bytes 1572872 | tf_op jit(solution)/shard_map/cond/branch_1_fun/ppermute | solution.py:136
  43.8 26.3 %collective-permute-start.3 = (bf16[512,512]{1,0:T(8,128)(2,1)S(1)}, bf16[512,512]{1,0:T(8,128)(2,1)}, u32[]{:S(2)}, u32[]{:S(2)}) collective-permute-start(bf16[512,512]{1,0:T(8,128)(2,1)S(1)} %param.1), channel_id=1, source_target_pairs={{0,6},{2,4},{4,2},{6,0},{1,7},{3,5},{5,3},{7,1},{8,14},{10,12},{12... | collective-permute-start | bytes 1572872 | tf_op jit(solution)/shard_map/cond/branch_1_fun/ppermute | solution.py:136
  50.7 23.7 %collective-permute-start.1 = (bf16[512,512]{1,0:T(8,128)(2,1)S(1)}, bf16[512,512]{1,0:T(8,128)(2,1)}, u32[]{:S(2)}, u32[]{:S(2)}) collective-permute-start(bf16[512,512]{1,0:T(8,128)(2,1)S(1)} %param.1), channel_id=1, source_target_pairs={{0,1},{1,0},{2,3},{3,2},{4,5},{5,4},{6,7},{7,6},{8,9},{9,8},{10,11... | collective-permute-start | bytes 1572872 | tf_op jit(solution)/shard_map/cond/branch_1_fun/ppermute | solution.py:139
  64.2 12.2 %collective-permute-start.5 = (bf16[512,512]{1,0:T(8,128)(2,1)}, bf16[512,512]{1,0:T(8,128)(2,1)}, u32[]{:S(2)}, u32[]{:S(2)}) collective-permute-start(bf16[512,512]{1,0:T(8,128)(2,1)} %collective-permute-done.2), channel_id=1, source_target_pairs={{0,1},{1,0},{2,3},{3,2},{4,5},{5,4},{6,7},{7,6},{8,9},{9,8},{10,11... | collective-permute-start | bytes 1572872 | tf_op jit(solution)/shard_map/cond/branch_1_fun/ppermute | solution.py:142
  70.1 6.3 %collective-permute-start.6 = (bf16[512,512]{1,0:T(8,128)(2,1)}, bf16[512,512]{1,0:T(8,128)(2,1)}, u32[]{:S(2)}, u32[]{:S(2)}) collective-permute-start(bf16[512,512]{1,0:T(8,128)(2,1)} %collective-permute-done.3), channel_id=1, source_target_pairs={{0,1},{1,0},{2,3},{3,2},{4,5},{5,4},{6,7},{7,6},{8,9},{9,8},{10,11... | collective-permute-start | bytes 1572872 | tf_op jit(solution)/shard_map/cond/branch_1_fun/ppermute | solution.py:142
  74.5 4.1 %collective-permute-start.4 = (bf16[512,512]{1,0:T(8,128)(2,1)}, bf16[512,512]{1,0:T(8,128)(2,1)}, u32[]{:S(2)}, u32[]{:S(2)}) collective-permute-start(bf16[512,512]{1,0:T(8,128)(2,1)} %collective-permute-done), channel_id=1, source_target_pairs={{0,1},{1,0},{2,3},{3,2},{4,5},{5,4},{6,7},{7,6},{8,9},{9,8},{10,11... | collective-permute-start | bytes 1572872 | tf_op jit(solution)/shard_map/cond/branch_1_fun/ppermute | solution.py:142
  94.7 30.6 %all-to-all-start.1 = ((f32[16,1,32]{2,1,0:T(1,128)}), f32[16,1,32]{2,1,0:T(1,128)S(1)}, u32[]{:S(2)}, u32[]{:S(2)}) async-start(f32[16,1,32]{2,1,0:T(1,128)} %broadcast_in_dim.48), calls=%async_computation.1 | async-start | bytes 16384 | tf_op jit(solution)/shard_map/all_to_all | solution.py:190

commit v10 on v8

--- a/solution.py
+++ b/solution.py
@@ -108,8 +108,8 @@
     )(packed, *preconds)
 
 
-def last_scores(late, early, stack, before, length, columns):
-    def kernel(late_ref, early_ref, stack_ref, before_ref, out_ref, packed_ref):
+def last_scores(late, early, token, stack, before, length, columns):
+    def kernel(late_ref, early_ref, token_ref, stack_ref, before_ref, out_ref, packed_ref):
         packed_ref[...] = late_ref[...] + early_ref[...]
         preconds = [stack_ref.at[q] for q in range(stack_ref.shape[0])]
         out_ref[...] = before_ref[...] + packed_scores(packed_ref, preconds, length, columns)
@@ -117,11 +117,11 @@
     return pl.pallas_call(
         kernel,
         out_shape=jax.ShapeDtypeStruct(before.shape, jnp.float32),
-        in_specs=[VMEM] * 4,
+        in_specs=[VMEM] * 5,
         out_specs=VMEM,
         scratch_shapes=[pltpu.VMEM(late.shape, late.dtype)],
         compiler_params=pltpu.CompilerParams(vmem_limit_bytes=40 << 20),
-    )(late, early, stack, before)
+    )(late, early, token, stack, before)
 
 
 def precondition(query_in, query_out, in_basis, out_basis, eigen_values):
@@ -173,13 +173,18 @@
     )
     late = swap_half(mine, range(ZLO // 2, ZLO))
     precond = precondition(query_in[0, 0], query_out[0, 0], in_basis, out_basis, eigen_values[0])
-    again, precond = lax.optimization_barrier((mine, precond))
+    token = lax.ppermute(
+        mine[:EXTRA],
+        ("zlo", "core"),
+        [(z * CORE + i, z * CORE + j) for z in range(ZLO // 2) for i, j in SWAP],
+    )
+    again, precond, token = lax.optimization_barrier((mine, precond, token))
     early = swap_half(again, range(ZLO // 2))
     preconds = lax.cond(
         lax.axis_index("x") < X, gather_preconds, lambda precond: [precond] * (X * CORE), precond
     )
     stack, partial_mine = first_scores(mine, preconds, length, columns)
-    partial_value = last_scores(late, early, stack, partial_mine, length, columns)
+    partial_value = last_scores(late, early, token, stack, partial_mine, length, columns)
 
     k = jnp.arange(X * CORE, dtype=jnp.int32)
     owner = (lax.axis_index("x") ^ (k % X)) * CORE + (lax.axis_index("core") ^ (k // X))

time: 129 us -> 125 us (0.969)
  starting transfers between devices: 72.3 us -> 60.6 us
  waiting for transfers between devices: 35.5 us -> 43.9 us
  blocking collectives: 11.5 us -> 10.1 us
    ppermute x0 -> x1, starting transfers between devices: none -> 16 us  [local(): lax.ppermute(mine[:EXTRA], ('zlo', 'core'), [(z * CORE + i, z * CORE + j)...]
    ppermute x2, starting transfers between devices: 30.3 us -> 16.8 us  [swap_half(): return lax.ppermute(packed, ('zlo', 'zhi'), pairs)]
    all_to_all x1, starting transfers between devices: 17.1 us -> 5.13 us  [local(): summed = jnp.sum(lax.all_to_all(far, 'zlo', 0, 0), axis=0)]
    ppermute x2, waiting for transfers between devices: 0.01 us -> 6.06 us  [swap_half(): return lax.ppermute(packed, ('zlo', 'zhi'), pairs)]
    ppermute x3, waiting for transfers between devices: 15.2 us -> 17.5 us  [gather_preconds(): lax.ppermute(precond, 'x', [(i, i ^ step) for i in range(X)])]
    all_to_all x1, blocking collectives: 11.5 us -> 10.1 us  [local(): near = jnp.sum(lax.all_to_all(spread, ('y', 'x', 'core'), 0, 0), axis=0)]
  transfers between devices with their start and end apart: 10 -> 11, of which waited for: 5 -> 6; matrix products, arithmetic and copies ran while one was open for 1% -> 1% of each run, Pallas kernels for 2% -> 2%
where the time goes in v10:
time: 125 us
  starting transfers between devices  60.6 us (48%)
  waiting for transfers between devices  43.9 us (35%)
  blocking collectives  10.1 us (8%)
  Pallas kernels  6.33 us (5%)
  local copies, waits for them, and re-layouts  1.3 us (1%)
    all_to_all x1, waiting for transfers between devices, local(): summed = jnp.sum(lax.all_to_all(far, 'zlo', 0, 0), axis=0)  18.1 us
    ppermute x3, waiting for transfers between devices, gather_preconds(): lax.ppermute(precond, 'x', [(i, i ^ step) for i in range(X)])  17.5 us
    ppermute x2, starting transfers between devices, swap_half(): return lax.ppermute(packed, ('zlo', 'zhi'), pairs)  16.8 us
    ppermute x1, starting transfers between devices, local(): lax.ppermute(mine[:EXTRA], ('zlo', 'core'), [(z * CORE + i, z * CORE + j)...  16 us
    all_to_all x1, blocking collectives, local(): near = jnp.sum(lax.all_to_all(spread, ('y', 'x', 'core'), 0, 0), axis=0)  10.1 us
    ppermute x3, starting transfers between devices, gather_preconds(): lax.ppermute(precond, 'x', [(i, i ^ step) for i in range(X)])  9.59 us
    ppermute x3, starting transfers between devices, gather_preconds(): lax.ppermute(p, 'core', SWAP)  8.95 us
    ppermute x2, waiting for transfers between devices, swap_half(): return lax.ppermute(packed, ('zlo', 'zhi'), pairs)  6.06 us
  transfers between devices with their start and end apart: 11, of which 6 were waited for; matrix products, arithmetic and copies ran while one was open for 1% of the time, Pallas kernels for 2%

profile of v10, /device:TPU:1, one launch (start us, length us, event | category | flops | bytes accessed | tf_op | source)
XLA Modules:
  0.0 124.7 jit_solution(1761518005662977352)
XLA Ops:
  0.0 0.0 copy-start
  0.0 0.0 copy-start.2
  0.0 0.0 copy-start.3
  0.0 0.0 copy-start.4
  0.0 0.0 copy-start.5
  0.0 2.5 %shard_map.91.packed_ref = bf16[1032,128]{1,0:T(8,128)(2,1)} custom-call(s32[2]{0:T(128)} %ids_ref.1, f32[128,512]{1,0:T(8,128)} %bitcast.29, f32[128,512]{1,0:T(8,128)} %bitcast.30, bf16[512,512]{1,0:T(8,128)(2,1)} %bitcast.25, bf16[512,512]{1,0:T(8,128)(2,1)} %bitcast.28), custom_call_target="tpu_custom_call" | custom-call | flops 13421772800 | bytes 786432 | tf_op jit(solution)/shard_map/pallas_call | solution.py:44
  2.6 0.0 copy-start.1
  2.6 0.8 collective-permute-start.7
  3.4 0.7 slice.4
  4.0 16.0 %collective-permute-start.8 = (bf16[8,128]{1,0:T(8,128)(2,1)S(1)}, bf16[8,128]{1,0:T(8,128)(2,1)S(1)}, u32[]{:S(2)}, u32[]{:S(2)}) collective-permute-start(bf16[8,128]{1,0:T(8,128)(2,1)S(1)} %slice.4), channel_id=1, source_target_pairs={{0,1},{1,0},{64,65},{65,64},{128,129},{129,128},{192,193},{193,192... | collective-permute-start | bytes 6152 | tf_op jit(solution)/shard_map/ppermute | solution.py:176
  20.1 0.0 copy-done.2
  20.1 0.0 copy-done.3
  20.1 0.3 convolution_convert_fusion
  20.4 0.0 copy-done
  20.4 0.0 copy-done.4
  20.4 0.0 copy-done.5
  20.5 0.6 fusion
  21.1 0.0 collective-permute-done.8.token_ref
  21.1 0.0 copy-done.1
  21.1 16.1 %collective-permute-start.9 = (bf16[1032,128]{1,0:T(8,128)(2,1)S(1)}, bf16[1032,128]{1,0:T(8,128)(2,1)S(1)}, u32[]{:S(2)}, u32[]{:S(2)}) collective-permute-start(bf16[1032,128]{1,0:T(8,128)(2,1)S(1)} %copy-done.1), channel_id=1, source_target_pairs={{0,8},{8,0},{64,72},{72,64},{128,136},{136,128},{192,200},{200,192... | collective-permute-start | bytes 792584 | tf_op jit(solution)/shard_map/ppermute | solution.py:151
  37.2 42.4 %conditional.1 = (bf16[512,512]{1,0:T(8,128)(2,1)S(1)}, bf16[512,512]{1,0:T(8,128)(2,1)}, bf16[512,512]{1,0:T(8,128)(2,1)}, bf16[512,512]{1,0:T(8,128)(2,1)}, bf...) conditional(s32[]{:T(128)} %convert_element_type.15, ...), branch_computations={%region_0.0_spmd, %region_1.0_spmd} | conditional | bytes 14680408 | solution.py:183
  37.2 3.1 %collective-permute-start = (bf16[512,512]{1,0:T(8,128)(2,1)S(1)}, bf16[512,512]{1,0:T(8,128)(2,1)}, u32[]{:S(2)}, u32[]{:S(2)}) collective-permute-start(bf16[512,512]{1,0:T(8,128)(2,1)S(1)} %param.1), channel_id=1, source_target_pairs={{0,2},{2,0},{4,6},{6,4},{1,3},{3,1},{5,7},{7,5},{8,10},{10,8},{12,... | collective-permute-start | bytes 1572872 | tf_op jit(solution)/shard_map/cond/branch_1_fun/ppermute | solution.py:139
  40.3 4.4 %collective-permute-start.2 = (bf16[512,512]{1,0:T(8,128)(2,1)S(1)}, bf16[512,512]{1,0:T(8,128)(2,1)}, u32[]{:S(2)}, u32[]{:S(2)}) collective-permute-start(bf16[512,512]{1,0:T(8,128)(2,1)S(1)} %param.1), channel_id=1, source_target_pairs={{0,4},{2,6},{4,0},{6,2},{1,5},{3,7},{5,1},{7,3},{8,12},{10,14},{12... | collective-permute-start | bytes 1572872 | tf_op jit(solution)/shard_map/cond/branch_1_fun/ppermute | solution.py:139
  44.7 2.1 %collective-permute-start.3 = (bf16[512,512]{1,0:T(8,128)(2,1)S(1)}, bf16[512,512]{1,0:T(8,128)(2,1)}, u32[]{:S(2)}, u32[]{:S(2)}) collective-permute-start(bf16[512,512]{1,0:T(8,128)(2,1)S(1)} %param.1), channel_id=1, source_target_pairs={{0,6},{2,4},{4,2},{6,0},{1,7},{3,5},{5,3},{7,1},{8,14},{10,12},{12... | collective-permute-start | bytes 1572872 | tf_op jit(solution)/shard_map/cond/branch_1_fun/ppermute | solution.py:139
  46.8 5.5 %collective-permute-done = bf16[512,512]{1,0:T(8,128)(2,1)} collective-permute-done((bf16[512,512]{1,0:T(8,128)(2,1)S(1)}, bf16[512,512]{1,0:T(8,128)(2,1)}, u32[]{:S(2)}, u32[]{:S(2)}) %collective-permute-start) | collective-permute-done | bytes 524320 | tf_op jit(solution)/shard_map/cond/branch_1_fun/ppermute | solution.py:139
  52.3 4.0 %collective-permute-start.1 = (bf16[512,512]{1,0:T(8,128)(2,1)S(1)}, bf16[512,512]{1,0:T(8,128)(2,1)}, u32[]{:S(2)}, u32[]{:S(2)}) collective-permute-start(bf16[512,512]{1,0:T(8,128)(2,1)S(1)} %param.1), channel_id=1, source_target_pairs={{0,1},{1,0},{2,3},{3,2},{4,5},{5,4},{6,7},{7,6},{8,9},{9,8},{10,11... | collective-permute-start | bytes 1572872 | tf_op jit(solution)/shard_map/cond/branch_1_fun/ppermute | solution.py:142
  56.3 9.4 %collective-permute-done.2 = bf16[512,512]{1,0:T(8,128)(2,1)} collective-permute-done((bf16[512,512]{1,0:T(8,128)(2,1)S(1)}, bf16[512,512]{1,0:T(8,128)(2,1)}, u32[]{:S(2)}, u32[]{:S(2)}) %collective-permute-start.2) | collective-permute-done | bytes 524320 | tf_op jit(solution)/shard_map/cond/branch_1_fun/ppermute | solution.py:139
  65.7 3.2 %collective-permute-start.5 = (bf16[512,512]{1,0:T(8,128)(2,1)}, bf16[512,512]{1,0:T(8,128)(2,1)}, u32[]{:S(2)}, u32[]{:S(2)}) collective-permute-start(bf16[512,512]{1,0:T(8,128)(2,1)} %collective-permute-done.2), channel_id=1, source_target_pairs={{0,1},{1,0},{2,3},{3,2},{4,5},{5,4},{6,7},{7,6},{8,9},{9,8},{10,11... | collective-permute-start | bytes 1572872 | tf_op jit(solution)/shard_map/cond/branch_1_fun/ppermute | solution.py:145
  69.0 2.6 %collective-permute-done.3 = bf16[512,512]{1,0:T(8,128)(2,1)} collective-permute-done((bf16[512,512]{1,0:T(8,128)(2,1)S(1)}, bf16[512,512]{1,0:T(8,128)(2,1)}, u32[]{:S(2)}, u32[]{:S(2)}) %collective-permute-start.3) | collective-permute-done | bytes 524320 | tf_op jit(solution)/shard_map/cond/branch_1_fun/ppermute | solution.py:139
  71.6 3.8 %collective-permute-start.6 = (bf16[512,512]{1,0:T(8,128)(2,1)}, bf16[512,512]{1,0:T(8,128)(2,1)}, u32[]{:S(2)}, u32[]{:S(2)}) collective-permute-start(bf16[512,512]{1,0:T(8,128)(2,1)} %collective-permute-done.3), channel_id=1, source_target_pairs={{0,1},{1,0},{2,3},{3,2},{4,5},{5,4},{6,7},{7,6},{8,9},{9,8},{10,11... | collective-permute-start | bytes 1572872 | tf_op jit(solution)/shard_map/cond/branch_1_fun/ppermute | solution.py:145
  75.4 0.0 collective-permute-done.1
  75.4 1.9 %collective-permute-start.4 = (bf16[512,512]{1,0:T(8,128)(2,1)}, bf16[512,512]{1,0:T(8,128)(2,1)}, u32[]{:S(2)}, u32[]{:S(2)}) collective-permute-start(bf16[512,512]{1,0:T(8,128)(2,1)} %collective-permute-done), channel_id=1, source_target_pairs={{0,1},{1,0},{2,3},{3,2},{4,5},{5,4},{6,7},{7,6},{8,9},{9,8},{10,11... | collective-permute-start | bytes 1572872 | tf_op jit(solution)/shard_map/cond/branch_1_fun/ppermute | solution.py:145
  77.3 0.0 collective-permute-done.5
  77.3 0.0 collective-permute-done.6
  77.3 2.2 %collective-permute-done.4 = bf16[512,512]{1,0:T(8,128)(2,1)} collective-permute-done((bf16[512,512]{1,0:T(8,128)(2,1)}, bf16[512,512]{1,0:T(8,128)(2,1)}, u32[]{:S(2)}, u32[]{:S(2)}) %collective-permute-start.4) | collective-permute-done | bytes 524320 | tf_op jit(solution)/shard_map/cond/branch_1_fun/ppermute | solution.py:145
  79.5 2.9 %shard_map.92 = (bf16[8,512,512]{2,1,0:T(8,128)(2,1)S(1)}, f32[8,32]{1,0:T(8,128)S(1)}) custom-call(bf16[1032,128]{1,0:T(8,128)(2,1)S(1)} %copy-done.1, bf16[512,512]{1,0:T(8,128)(2,1)S(1)} %get-tuple-element.27.refs_0_, bf16[512,512]{1,0:T(8,128)(2,1)} %get-tuple-element.28.refs_1_, bf16[512,512]{1,0:T(8,128)(2,1)} %get-tuple-element.29.refs_2_, ...), custom_call_target="tpu_custom_call" | custom-call | tf_op jit(solution)/shard_map/pallas_call | solution.py:98
  82.5 0.0 collective-permute-done.7.late_ref
  82.5 6.1 %collective-permute-done.9.early_ref = bf16[1032,128]{1,0:T(8,128)(2,1)S(1)} collective-permute-done((bf16[1032,128]{1,0:T(8,128)(2,1)S(1)}, bf16[1032,128]{1,0:T(8,128)(2,1)S(1)}, u32[]{:S(2)}, u32[]{:S(2)}) %collective-permute-start.9) | collective-permute-done | bytes 264224 | tf_op jit(solution)/shard_map/ppermute | solution.py:151
  88.5 0.9 shard_map.93
  89.4 0.1 select_reduce_fusion
  89.5 10.1 %all_to_all.15 = f32[32,1,32]{2,1,0:T(1,128)S(1)} all-to-all(f32[32,1,32]{2,1,0:T(1,128)S(1)} %bitcast.26), channel_id=1, replica_groups=mesh['zlo'=16,'y'=4,'zhi'=2,'x'=4,'core'=2] {'y','x','core'}, dimensions={0} | all-to-all | bytes 8192 | tf_op jit(solution)/shard_map/all_to_all | solution.py:196
  99.6 0.1 reduce_sum.28
  99.7 0.6 broadcast_in_dim.48
  100.3 5.1 %all-to-all-start.1 = ((f32[16,1,32]{2,1,0:T(1,128)}), f32[16,1,32]{2,1,0:T(1,128)S(1)}, u32[]{:S(2)}, u32[]{:S(2)}) async-start(f32[16,1,32]{2,1,0:T(1,128)} %broadcast_in_dim.48), calls=%async_computation.1 | async-start | bytes 16384 | tf_op jit(solution)/shard_map/all_to_all | solution.py:198
  106.1 18.1 %all-to-all-done.1 = f32[16,1,32]{2,1,0:T(1,128)S(1)} async-done(((f32[16,1,32]{2,1,0:T(1,128)}), f32[16,1,32]{2,1,0:T(1,128)S(1)}, u32[]{:S(2)}, u32[]{:S(2)}) %all-to-all-start.1) | async-done | bytes 2080 | tf_op jit(solution)/shard_map/all_to_all | solution.py:198
  124.2 0.5 compare_select_fusion
  (4 shorter events, 0.0 us)
Async XLA Ops:
  0.0 20.4 %copy-start = (bf16[1,1,256,512]{3,2,1,0:T(8,128)(2,1)S(1)}, bf16[1,1,256,512]{3,2,1,0:T(8,128)(2,1)}, u32[]{:S(2)}) copy-start(bf16[1,1,256,512]{3,2,1,0:T(8,128)(2,1)} %param.14) | copy-start | bytes 786436
  0.0 20.1 %copy-start.2 = (bf16[1,512,512]{2,1,0:T(8,128)(2,1)S(1)}, bf16[1,512,512]{2,1,0:T(8,128)(2,1)}, u32[]{:S(2)}) copy-start(bf16[1,512,512]{2,1,0:T(8,128)(2,1)} %param.15) | copy-start | bytes 1572868
  0.0 20.1 %copy-start.3 = (bf16[1,1,256,512]{3,2,1,0:T(8,128)(2,1)S(1)}, bf16[1,1,256,512]{3,2,1,0:T(8,128)(2,1)}, u32[]{:S(2)}) copy-start(bf16[1,1,256,512]{3,2,1,0:T(8,128)(2,1)} %param.13) | copy-start | bytes 786436
  0.0 20.4 %copy-start.4 = (f32[1,512,512]{2,1,0:T(8,128)S(1)}, f32[1,512,512]{2,1,0:T(8,128)}, u32[]{:S(2)}) copy-start(f32[1,512,512]{2,1,0:T(8,128)} %param.17) | copy-start | bytes 3145732
  0.0 20.4 %copy-start.5 = (bf16[1,512,512]{2,1,0:T(8,128)(2,1)S(1)}, bf16[1,512,512]{2,1,0:T(8,128)(2,1)}, u32[]{:S(2)}) copy-start(bf16[1,512,512]{2,1,0:T(8,128)(2,1)} %param.16) | copy-start | bytes 1572868
  2.6 18.5 %copy-start.1 = (bf16[1032,128]{1,0:T(8,128)(2,1)S(1)}, bf16[1032,128]{1,0:T(8,128)(2,1)}, u32[]{:S(2)}) copy-start(bf16[1032,128]{1,0:T(8,128)(2,1)} %shard_map.91.packed_ref) | copy-start | bytes 792580
  2.6 79.9 %collective-permute-start.7 = (bf16[1032,128]{1,0:T(8,128)(2,1)}, bf16[1032,128]{1,0:T(8,128)(2,1)S(1)}, u32[]{:S(2)}, u32[]{:S(2)}) collective-permute-start(bf16[1032,128]{1,0:T(8,128)(2,1)} %shard_map.91.packed_ref), channel_id=1, source_target_pairs={{512,520},{520,512},{576,584},{584,576},{640,648},{648,640},{704,7... | collective-permute-start | bytes 792584 | tf_op jit(solution)/shard_map/ppermute | solution.py:151
  4.0 17.0 %collective-permute-start.8 = (bf16[8,128]{1,0:T(8,128)(2,1)S(1)}, bf16[8,128]{1,0:T(8,128)(2,1)S(1)}, u32[]{:S(2)}, u32[]{:S(2)}) collective-permute-start(bf16[8,128]{1,0:T(8,128)(2,1)S(1)} %slice.4), channel_id=1, source_target_pairs={{0,1},{1,0},{64,65},{65,64},{128,129},{129,128},{192,193},{193,192... | collective-permute-start | bytes 6152 | tf_op jit(solution)/shard_map/ppermute | solution.py:176
  21.1 67.4 %collective-permute-start.9 = (bf16[1032,128]{1,0:T(8,128)(2,1)S(1)}, bf16[1032,128]{1,0:T(8,128)(2,1)S(1)}, u32[]{:S(2)}, u32[]{:S(2)}) collective-permute-start(bf16[1032,128]{1,0:T(8,128)(2,1)S(1)} %copy-done.1), channel_id=1, source_target_pairs={{0,8},{8,0},{64,72},{72,64},{128,136},{136,128},{192,200},{200,192... | collective-permute-start | bytes 792584 | tf_op jit(solution)/shard_map/ppermute | solution.py:151
  37.2 15.1 %collective-permute-start = (bf16[512,512]{1,0:T(8,128)(2,1)S(1)}, bf16[512,512]{1,0:T(8,128)(2,1)}, u32[]{:S(2)}, u32[]{:S(2)}) collective-permute-start(bf16[512,512]{1,0:T(8,128)(2,1)S(1)} %param.1), channel_id=1, source_target_pairs={{0,2},{2,0},{4,6},{6,4},{1,3},{3,1},{5,7},{7,5},{8,10},{10,8},{12,... | collective-permute-start | bytes 1572872 | tf_op jit(solution)/shard_map/cond/branch_1_fun/ppermute | solution.py:139
  40.3 25.4 %collective-permute-start.2 = (bf16[512,512]{1,0:T(8,128)(2,1)S(1)}, bf16[512,512]{1,0:T(8,128)(2,1)}, u32[]{:S(2)}, u32[]{:S(2)}) collective-permute-start(bf16[512,512]{1,0:T(8,128)(2,1)S(1)} %param.1), channel_id=1, source_target_pairs={{0,4},{2,6},{4,0},{6,2},{1,5},{3,7},{5,1},{7,3},{8,12},{10,14},{12... | collective-permute-start | bytes 1572872 | tf_op jit(solution)/shard_map/cond/branch_1_fun/ppermute | solution.py:139
  44.7 26.9 %collective-permute-start.3 = (bf16[512,512]{1,0:T(8,128)(2,1)S(1)}, bf16[512,512]{1,0:T(8,128)(2,1)}, u32[]{:S(2)}, u32[]{:S(2)}) collective-permute-start(bf16[512,512]{1,0:T(8,128)(2,1)S(1)} %param.1), channel_id=1, source_target_pairs={{0,6},{2,4},{4,2},{6,0},{1,7},{3,5},{5,3},{7,1},{8,14},{10,12},{12... | collective-permute-start | bytes 1572872 | tf_op jit(solution)/shard_map/cond/branch_1_fun/ppermute | solution.py:139
  52.3 23.1 %collective-permute-start.1 = (bf16[512,512]{1,0:T(8,128)(2,1)S(1)}, bf16[512,512]{1,0:T(8,128)(2,1)}, u32[]{:S(2)}, u32[]{:S(2)}) collective-permute-start(bf16[512,512]{1,0:T(8,128)(2,1)S(1)} %param.1), channel_id=1, source_target_pairs={{0,1},{1,0},{2,3},{3,2},{4,5},{5,4},{6,7},{7,6},{8,9},{9,8},{10,11... | collective-permute-start | bytes 1572872 | tf_op jit(solution)/shard_map/cond/branch_1_fun/ppermute | solution.py:142
  65.7 11.6 %collective-permute-start.5 = (bf16[512,512]{1,0:T(8,128)(2,1)}, bf16[512,512]{1,0:T(8,128)(2,1)}, u32[]{:S(2)}, u32[]{:S(2)}) collective-permute-start(bf16[512,512]{1,0:T(8,128)(2,1)} %collective-permute-done.2), channel_id=1, source_target_pairs={{0,1},{1,0},{2,3},{3,2},{4,5},{5,4},{6,7},{7,6},{8,9},{9,8},{10,11... | collective-permute-start | bytes 1572872 | tf_op jit(solution)/shard_map/cond/branch_1_fun/ppermute | solution.py:145
  71.6 5.8 %collective-permute-start.6 = (bf16[512,512]{1,0:T(8,128)(2,1)}, bf16[512,512]{1,0:T(8,128)(2,1)}, u32[]{:S(2)}, u32[]{:S(2)}) collective-permute-start(bf16[512,512]{1,0:T(8,128)(2,1)} %collective-permute-done.3), channel_id=1, source_target_pairs={{0,1},{1,0},{2,3},{3,2},{4,5},{5,4},{6,7},{7,6},{8,9},{9,8},{10,11... | collective-permute-start | bytes 1572872 | tf_op jit(solution)/shard_map/cond/branch_1_fun/ppermute | solution.py:145
  75.4 4.1 %collective-permute-start.4 = (bf16[512,512]{1,0:T(8,128)(2,1)}, bf16[512,512]{1,0:T(8,128)(2,1)}, u32[]{:S(2)}, u32[]{:S(2)}) collective-permute-start(bf16[512,512]{1,0:T(8,128)(2,1)} %collective-permute-done), channel_id=1, source_target_pairs={{0,1},{1,0},{2,3},{3,2},{4,5},{5,4},{6,7},{7,6},{8,9},{9,8},{10,11... | collective-permute-start | bytes 1572872 | tf_op jit(solution)/shard_map/cond/branch_1_fun/ppermute | solution.py:145
  100.3 23.9 %all-to-all-start.1 = ((f32[16,1,32]{2,1,0:T(1,128)}), f32[16,1,32]{2,1,0:T(1,128)S(1)}, u32[]{:S(2)}, u32[]{:S(2)}) async-start(f32[16,1,32]{2,1,0:T(1,128)} %broadcast_in_dim.48), calls=%async_computation.1 | async-start | bytes 16384 | tf_op jit(solution)/shard_map/all_to_all | solution.py:198

commit v11 on v10

--- a/solution.py
+++ b/solution.py
@@ -135,15 +135,14 @@
 
 
 def gather_preconds(precond):
-    one, two, three = [
-        lax.ppermute(precond, "x", [(i, i ^ step) for i in range(X)]) for step in range(1, X)
+    other = lax.ppermute(precond, "core", SWAP)
+    again, other = lax.optimization_barrier((precond, other))
+    along = [
+        lax.ppermute(again if step == 1 else precond, "x", [(i, i ^ step) for i in range(X)])
+        for step in range(1, X)
     ]
-    precond, one = lax.optimization_barrier((precond, one))
-    other = lax.ppermute(precond, "core", SWAP)
-    one, other = lax.optimization_barrier((one, other))
-    return [precond, one, two, three, other] + [
-        lax.ppermute(p, "core", SWAP) for p in (one, two, three)
-    ]
+    beside = [lax.ppermute(p, "core", SWAP) for p in along]
+    return [precond] + along + [other] + beside
 
 
 def swap_half(packed, places):

time: 125 us -> 125 us (level)
  starting transfers between devices: 60.6 us -> 57.3 us
  waiting for transfers between devices: 43.9 us -> 47.2 us
    ppermute x2, waiting for transfers between devices: 6.06 us -> 10.9 us  [swap_half(): return lax.ppermute(packed, ('zlo', 'zhi'), pairs)]
    ppermute x1, starting transfers between devices: 4.03 us -> 2.34 us  [gather_preconds(): other = lax.ppermute(precond, 'core', SWAP)]
    ppermute x6, starting transfers between devices: 18.5 us -> 16.9 us  [the longest x3 9.36 us: gather_preconds(): lax.ppermute(again if step == 1 else precond, 'x', [(i, i ^ step) for i i...]
    ppermute x6, waiting for transfers between devices: 19.7 us -> 18.2 us  [the longest x3 16 us: gather_preconds(): lax.ppermute(again if step == 1 else precond, 'x', [(i, i ^ step) for i i...]
  transfers between devices with their start and end apart: 11 -> 11, of which waited for: 6 -> 5; matrix products, arithmetic and copies ran while one was open for 1% -> 1% of each run, Pallas kernels for 2% -> 2%
where the time goes in v11:
time: 125 us
  starting transfers between devices  57.3 us (46%)
  waiting for transfers between devices  47.2 us (38%)
  blocking collectives  10.1 us (8%)
  Pallas kernels  6.33 us (5%)
  local copies, waits for them, and re-layouts  1.3 us (1%)
    all_to_all x1, waiting for transfers between devices, local(): summed = jnp.sum(lax.all_to_all(far, 'zlo', 0, 0), axis=0)  18.1 us
    ppermute x2, starting transfers between devices, swap_half(): return lax.ppermute(packed, ('zlo', 'zhi'), pairs)  16.8 us
    ppermute x1, starting transfers between devices, local(): lax.ppermute(mine[:EXTRA], ('zlo', 'core'), [(z * CORE + i, z * CORE + j)...  16 us
    ppermute x3, waiting for transfers between devices, gather_preconds(): lax.ppermute(again if step == 1 else precond, 'x', [(i, i ^ step) for i i...  16 us
    ppermute x2, waiting for transfers between devices, swap_half(): return lax.ppermute(packed, ('zlo', 'zhi'), pairs)  10.9 us
    all_to_all x1, blocking collectives, local(): near = jnp.sum(lax.all_to_all(spread, ('y', 'x', 'core'), 0, 0), axis=0)  10.1 us
    ppermute x3, starting transfers between devices, gather_preconds(): lax.ppermute(again if step == 1 else precond, 'x', [(i, i ^ step) for i i...  9.36 us
    ppermute x3, starting transfers between devices, gather_preconds(): beside = [lax.ppermute(p, 'core', SWAP) for p in along]  7.54 us
  transfers between devices with their start and end apart: 11, of which 5 were waited for; matrix products, arithmetic and copies ran while one was open for 1% of the time, Pallas kernels for 2%

profile of v11, /device:TPU:1, one launch (start us, length us, event | category | flops | bytes accessed | tf_op | source)
XLA Modules:
  0.0 124.7 jit_solution(13624398377077012657)
XLA Ops:
  0.0 0.0 copy-start
  0.0 0.0 copy-start.2
  0.0 0.0 copy-start.3
  0.0 0.0 copy-start.4
  0.0 0.0 copy-start.5
  0.0 2.5 %shard_map.91.packed_ref = bf16[1032,128]{1,0:T(8,128)(2,1)} custom-call(s32[2]{0:T(128)} %ids_ref.1, f32[128,512]{1,0:T(8,128)} %bitcast.29, f32[128,512]{1,0:T(8,128)} %bitcast.30, bf16[512,512]{1,0:T(8,128)(2,1)} %bitcast.25, bf16[512,512]{1,0:T(8,128)(2,1)} %bitcast.28), custom_call_target="tpu_custom_call" | custom-call | flops 13421772800 | bytes 786432 | tf_op jit(solution)/shard_map/pallas_call | solution.py:44
  2.6 0.0 copy-start.1
  2.6 0.8 collective-permute-start.7
  3.4 0.7 slice.4
  4.0 16.0 %collective-permute-start.8 = (bf16[8,128]{1,0:T(8,128)(2,1)S(1)}, bf16[8,128]{1,0:T(8,128)(2,1)S(1)}, u32[]{:S(2)}, u32[]{:S(2)}) collective-permute-start(bf16[8,128]{1,0:T(8,128)(2,1)S(1)} %slice.4), channel_id=1, source_target_pairs={{0,1},{1,0},{64,65},{65,64},{128,129},{129,128},{192,193},{193,192... | collective-permute-start | bytes 6152 | tf_op jit(solution)/shard_map/ppermute | solution.py:175
  20.1 0.0 copy-done.2
  20.1 0.0 copy-done.3
  20.1 0.3 convolution_convert_fusion
  20.4 0.0 copy-done
  20.4 0.0 copy-done.4
  20.4 0.0 copy-done.5
  20.5 0.6 fusion.refs_0_
  21.1 0.0 collective-permute-done.8.token_ref
  21.1 0.0 copy-done.1
  21.1 16.1 %collective-permute-start.9 = (bf16[1032,128]{1,0:T(8,128)(2,1)S(1)}, bf16[1032,128]{1,0:T(8,128)(2,1)S(1)}, u32[]{:S(2)}, u32[]{:S(2)}) collective-permute-start(bf16[1032,128]{1,0:T(8,128)(2,1)S(1)} %copy-done.1), channel_id=1, source_target_pairs={{0,8},{8,0},{64,72},{72,64},{128,136},{136,128},{192,200},{200,192... | collective-permute-start | bytes 792584 | tf_op jit(solution)/shard_map/ppermute | solution.py:150
  37.2 37.5 %conditional.1 = (bf16[512,512]{1,0:T(8,128)(2,1)}, bf16[512,512]{1,0:T(8,128)(2,1)}, bf16[512,512]{1,0:T(8,128)(2,1)}, bf16[512,512]{1,0:T(8,128)(2,1)}, bf16[5...) conditional(s32[]{:T(128)} %convert_element_type.15, ...), branch_computations={%region_0.0_spmd, %region_1.0_spmd} | conditional | bytes 14680400 | solution.py:182
  37.2 2.3 %collective-permute-start = (bf16[512,512]{1,0:T(8,128)(2,1)S(1)}, bf16[512,512]{1,0:T(8,128)(2,1)}, u32[]{:S(2)}, u32[]{:S(2)}) collective-permute-start(bf16[512,512]{1,0:T(8,128)(2,1)S(1)} %param.1), channel_id=1, source_target_pairs={{0,1},{1,0},{2,3},{3,2},{4,5},{5,4},{6,7},{7,6},{8,9},{9,8},{10,11... | collective-permute-start | bytes 1572872 | tf_op jit(solution)/shard_map/cond/branch_1_fun/ppermute | solution.py:138
  39.5 4.7 %collective-permute-start.2 = (bf16[512,512]{1,0:T(8,128)(2,1)S(1)}, bf16[512,512]{1,0:T(8,128)(2,1)}, u32[]{:S(2)}, u32[]{:S(2)}) collective-permute-start(bf16[512,512]{1,0:T(8,128)(2,1)S(1)} %param.1), channel_id=1, source_target_pairs={{0,4},{2,6},{4,0},{6,2},{1,5},{3,7},{5,1},{7,3},{8,12},{10,14},{12... | collective-permute-start | bytes 1572872 | tf_op jit(solution)/shard_map/cond/branch_1_fun/ppermute | solution.py:141
  44.2 2.8 %collective-permute-start.3 = (bf16[512,512]{1,0:T(8,128)(2,1)S(1)}, bf16[512,512]{1,0:T(8,128)(2,1)}, u32[]{:S(2)}, u32[]{:S(2)}) collective-permute-start(bf16[512,512]{1,0:T(8,128)(2,1)S(1)} %param.1), channel_id=1, source_target_pairs={{0,6},{2,4},{4,2},{6,0},{1,7},{3,5},{5,3},{7,1},{8,14},{10,12},{12... | collective-permute-start | bytes 1572872 | tf_op jit(solution)/shard_map/cond/branch_1_fun/ppermute | solution.py:141
  47.0 0.0 collective-permute-done
  47.0 1.9 %collective-permute-start.1 = (bf16[512,512]{1,0:T(8,128)(2,1)S(1)}, bf16[512,512]{1,0:T(8,128)(2,1)}, u32[]{:S(2)}, u32[]{:S(2)}) collective-permute-start(bf16[512,512]{1,0:T(8,128)(2,1)S(1)} %param.1), channel_id=1, source_target_pairs={{0,2},{2,0},{4,6},{6,4},{1,3},{3,1},{5,7},{7,5},{8,10},{10,8},{12,... | collective-permute-start | bytes 1572872 | tf_op jit(solution)/shard_map/cond/branch_1_fun/ppermute | solution.py:141
  48.9 7.6 %collective-permute-done.2 = bf16[512,512]{1,0:T(8,128)(2,1)} collective-permute-done((bf16[512,512]{1,0:T(8,128)(2,1)S(1)}, bf16[512,512]{1,0:T(8,128)(2,1)}, u32[]{:S(2)}, u32[]{:S(2)}) %collective-permute-start.2) | collective-permute-done | bytes 524320 | tf_op jit(solution)/shard_map/cond/branch_1_fun/ppermute | solution.py:141
  56.6 3.2 %collective-permute-start.5 = (bf16[512,512]{1,0:T(8,128)(2,1)}, bf16[512,512]{1,0:T(8,128)(2,1)}, u32[]{:S(2)}, u32[]{:S(2)}) collective-permute-start(bf16[512,512]{1,0:T(8,128)(2,1)} %collective-permute-done.2), channel_id=1, source_target_pairs={{0,1},{1,0},{2,3},{3,2},{4,5},{5,4},{6,7},{7,6},{8,9},{9,8},{10,11... | collective-permute-start | bytes 1572872 | tf_op jit(solution)/shard_map/cond/branch_1_fun/ppermute | solution.py:144
  59.8 8.4 %collective-permute-done.3 = bf16[512,512]{1,0:T(8,128)(2,1)} collective-permute-done((bf16[512,512]{1,0:T(8,128)(2,1)S(1)}, bf16[512,512]{1,0:T(8,128)(2,1)}, u32[]{:S(2)}, u32[]{:S(2)}) %collective-permute-start.3) | collective-permute-done | bytes 524320 | tf_op jit(solution)/shard_map/cond/branch_1_fun/ppermute | solution.py:141
  68.2 2.4 %collective-permute-start.6 = (bf16[512,512]{1,0:T(8,128)(2,1)}, bf16[512,512]{1,0:T(8,128)(2,1)}, u32[]{:S(2)}, u32[]{:S(2)}) collective-permute-start(bf16[512,512]{1,0:T(8,128)(2,1)} %collective-permute-done.3), channel_id=1, source_target_pairs={{0,1},{1,0},{2,3},{3,2},{4,5},{5,4},{6,7},{7,6},{8,9},{9,8},{10,11... | collective-permute-start | bytes 1572872 | tf_op jit(solution)/shard_map/cond/branch_1_fun/ppermute | solution.py:144
  70.5 0.0 collective-permute-done.1
  70.5 1.9 %collective-permute-start.4 = (bf16[512,512]{1,0:T(8,128)(2,1)}, bf16[512,512]{1,0:T(8,128)(2,1)}, u32[]{:S(2)}, u32[]{:S(2)}) collective-permute-start(bf16[512,512]{1,0:T(8,128)(2,1)} %collective-permute-done.1), channel_id=1, source_target_pairs={{0,1},{1,0},{2,3},{3,2},{4,5},{5,4},{6,7},{7,6},{8,9},{9,8},{10,11... | collective-permute-start | bytes 1572872 | tf_op jit(solution)/shard_map/cond/branch_1_fun/ppermute | solution.py:144
  72.5 0.0 collective-permute-done.5
  72.5 0.0 collective-permute-done.6
  72.5 2.2 %collective-permute-done.4 = bf16[512,512]{1,0:T(8,128)(2,1)} collective-permute-done((bf16[512,512]{1,0:T(8,128)(2,1)}, bf16[512,512]{1,0:T(8,128)(2,1)}, u32[]{:S(2)}, u32[]{:S(2)}) %collective-permute-start.4) | collective-permute-done | bytes 524320 | tf_op jit(solution)/shard_map/cond/branch_1_fun/ppermute | solution.py:144
  74.7 2.9 %shard_map.92 = (bf16[8,512,512]{2,1,0:T(8,128)(2,1)S(1)}, f32[8,32]{1,0:T(8,128)S(1)}) custom-call(bf16[1032,128]{1,0:T(8,128)(2,1)S(1)} %copy-done.1, bf16[512,512]{1,0:T(8,128)(2,1)S(1)} %fusion.refs_0_, bf16[512,512]{1,0:T(8,128)(2,1)} %get-tuple-element.24.refs_1_, bf16[512,512]{1,0:T(8,128)(2,1)} %get-tuple-element.25.refs_2_, ...), custom_call_target="tpu_custom_call" | custom-call | tf_op jit(solution)/shard_map/pallas_call | solution.py:98
  77.6 0.0 collective-permute-done.7.late_ref
  77.6 10.9 %collective-permute-done.9.early_ref = bf16[1032,128]{1,0:T(8,128)(2,1)S(1)} collective-permute-done((bf16[1032,128]{1,0:T(8,128)(2,1)S(1)}, bf16[1032,128]{1,0:T(8,128)(2,1)S(1)}, u32[]{:S(2)}, u32[]{:S(2)}) %collective-permute-start.9) | collective-permute-done | bytes 264224 | tf_op jit(solution)/shard_map/ppermute | solution.py:150
  88.5 0.9 shard_map.93
  89.4 0.1 select_reduce_fusion
  89.5 10.1 %all_to_all.15 = f32[32,1,32]{2,1,0:T(1,128)S(1)} all-to-all(f32[32,1,32]{2,1,0:T(1,128)S(1)} %bitcast.26), channel_id=1, replica_groups=mesh['zlo'=16,'y'=4,'zhi'=2,'x'=4,'core'=2] {'y','x','core'}, dimensions={0} | all-to-all | bytes 8192 | tf_op jit(solution)/shard_map/all_to_all | solution.py:195
  99.6 0.1 reduce_sum.28
  99.7 0.6 broadcast_in_dim.48
  100.3 5.1 %all-to-all-start.1 = ((f32[16,1,32]{2,1,0:T(1,128)}), f32[16,1,32]{2,1,0:T(1,128)S(1)}, u32[]{:S(2)}, u32[]{:S(2)}) async-start(f32[16,1,32]{2,1,0:T(1,128)} %broadcast_in_dim.48), calls=%async_computation.1 | async-start | bytes 16384 | tf_op jit(solution)/shard_map/all_to_all | solution.py:197
  106.1 18.1 %all-to-all-done.1 = f32[16,1,32]{2,1,0:T(1,128)S(1)} async-done(((f32[16,1,32]{2,1,0:T(1,128)}), f32[16,1,32]{2,1,0:T(1,128)S(1)}, u32[]{:S(2)}, u32[]{:S(2)}) %all-to-all-start.1) | async-done | bytes 2080 | tf_op jit(solution)/shard_map/all_to_all | solution.py:197
  124.2 0.5 compare_select_fusion
  (4 shorter events, 0.0 us)
Async XLA Ops:
  0.0 20.4 %copy-start = (bf16[1,1,256,512]{3,2,1,0:T(8,128)(2,1)S(1)}, bf16[1,1,256,512]{3,2,1,0:T(8,128)(2,1)}, u32[]{:S(2)}) copy-start(bf16[1,1,256,512]{3,2,1,0:T(8,128)(2,1)} %param.14) | copy-start | bytes 786436
  0.0 20.1 %copy-start.2 = (bf16[1,512,512]{2,1,0:T(8,128)(2,1)S(1)}, bf16[1,512,512]{2,1,0:T(8,128)(2,1)}, u32[]{:S(2)}) copy-start(bf16[1,512,512]{2,1,0:T(8,128)(2,1)} %param.15) | copy-start | bytes 1572868
  0.0 20.1 %copy-start.3 = (bf16[1,1,256,512]{3,2,1,0:T(8,128)(2,1)S(1)}, bf16[1,1,256,512]{3,2,1,0:T(8,128)(2,1)}, u32[]{:S(2)}) copy-start(bf16[1,1,256,512]{3,2,1,0:T(8,128)(2,1)} %param.13) | copy-start | bytes 786436
  0.0 20.4 %copy-start.4 = (f32[1,512,512]{2,1,0:T(8,128)S(1)}, f32[1,512,512]{2,1,0:T(8,128)}, u32[]{:S(2)}) copy-start(f32[1,512,512]{2,1,0:T(8,128)} %param.17) | copy-start | bytes 3145732
  0.0 20.4 %copy-start.5 = (bf16[1,512,512]{2,1,0:T(8,128)(2,1)S(1)}, bf16[1,512,512]{2,1,0:T(8,128)(2,1)}, u32[]{:S(2)}) copy-start(bf16[1,512,512]{2,1,0:T(8,128)(2,1)} %param.16) | copy-start | bytes 1572868
  2.6 18.5 %copy-start.1 = (bf16[1032,128]{1,0:T(8,128)(2,1)S(1)}, bf16[1032,128]{1,0:T(8,128)(2,1)}, u32[]{:S(2)}) copy-start(bf16[1032,128]{1,0:T(8,128)(2,1)} %shard_map.91.packed_ref) | copy-start | bytes 792580
  2.6 75.1 %collective-permute-start.7 = (bf16[1032,128]{1,0:T(8,128)(2,1)}, bf16[1032,128]{1,0:T(8,128)(2,1)S(1)}, u32[]{:S(2)}, u32[]{:S(2)}) collective-permute-start(bf16[1032,128]{1,0:T(8,128)(2,1)} %shard_map.91.packed_ref), channel_id=1, source_target_pairs={{512,520},{520,512},{576,584},{584,576},{640,648},{648,640},{704,7... | collective-permute-start | bytes 792584 | tf_op jit(solution)/shard_map/ppermute | solution.py:150
  4.0 17.0 %collective-permute-start.8 = (bf16[8,128]{1,0:T(8,128)(2,1)S(1)}, bf16[8,128]{1,0:T(8,128)(2,1)S(1)}, u32[]{:S(2)}, u32[]{:S(2)}) collective-permute-start(bf16[8,128]{1,0:T(8,128)(2,1)S(1)} %slice.4), channel_id=1, source_target_pairs={{0,1},{1,0},{64,65},{65,64},{128,129},{129,128},{192,193},{193,192... | collective-permute-start | bytes 6152 | tf_op jit(solution)/shard_map/ppermute | solution.py:175
  21.1 67.4 %collective-permute-start.9 = (bf16[1032,128]{1,0:T(8,128)(2,1)S(1)}, bf16[1032,128]{1,0:T(8,128)(2,1)S(1)}, u32[]{:S(2)}, u32[]{:S(2)}) collective-permute-start(bf16[1032,128]{1,0:T(8,128)(2,1)S(1)} %copy-done.1), channel_id=1, source_target_pairs={{0,8},{8,0},{64,72},{72,64},{128,136},{136,128},{192,200},{200,192... | collective-permute-start | bytes 792584 | tf_op jit(solution)/shard_map/ppermute | solution.py:150
  37.2 9.8 %collective-permute-start = (bf16[512,512]{1,0:T(8,128)(2,1)S(1)}, bf16[512,512]{1,0:T(8,128)(2,1)}, u32[]{:S(2)}, u32[]{:S(2)}) collective-permute-start(bf16[512,512]{1,0:T(8,128)(2,1)S(1)} %param.1), channel_id=1, source_target_pairs={{0,1},{1,0},{2,3},{3,2},{4,5},{5,4},{6,7},{7,6},{8,9},{9,8},{10,11... | collective-permute-start | bytes 1572872 | tf_op jit(solution)/shard_map/cond/branch_1_fun/ppermute | solution.py:138
  39.5 17.0 %collective-permute-start.2 = (bf16[512,512]{1,0:T(8,128)(2,1)S(1)}, bf16[512,512]{1,0:T(8,128)(2,1)}, u32[]{:S(2)}, u32[]{:S(2)}) collective-permute-start(bf16[512,512]{1,0:T(8,128)(2,1)S(1)} %param.1), channel_id=1, source_target_pairs={{0,4},{2,6},{4,0},{6,2},{1,5},{3,7},{5,1},{7,3},{8,12},{10,14},{12... | collective-permute-start | bytes 1572872 | tf_op jit(solution)/shard_map/cond/branch_1_fun/ppermute | solution.py:141
  44.2 23.9 %collective-permute-start.3 = (bf16[512,512]{1,0:T(8,128)(2,1)S(1)}, bf16[512,512]{1,0:T(8,128)(2,1)}, u32[]{:S(2)}, u32[]{:S(2)}) collective-permute-start(bf16[512,512]{1,0:T(8,128)(2,1)S(1)} %param.1), channel_id=1, source_target_pairs={{0,6},{2,4},{4,2},{6,0},{1,7},{3,5},{5,3},{7,1},{8,14},{10,12},{12... | collective-permute-start | bytes 1572872 | tf_op jit(solution)/shard_map/cond/branch_1_fun/ppermute | solution.py:141
  47.0 23.5 %collective-permute-start.1 = (bf16[512,512]{1,0:T(8,128)(2,1)S(1)}, bf16[512,512]{1,0:T(8,128)(2,1)}, u32[]{:S(2)}, u32[]{:S(2)}) collective-permute-start(bf16[512,512]{1,0:T(8,128)(2,1)S(1)} %param.1), channel_id=1, source_target_pairs={{0,2},{2,0},{4,6},{6,4},{1,3},{3,1},{5,7},{7,5},{8,10},{10,8},{12,... | collective-permute-start | bytes 1572872 | tf_op jit(solution)/shard_map/cond/branch_1_fun/ppermute | solution.py:141
  56.6 15.9 %collective-permute-start.5 = (bf16[512,512]{1,0:T(8,128)(2,1)}, bf16[512,512]{1,0:T(8,128)(2,1)}, u32[]{:S(2)}, u32[]{:S(2)}) collective-permute-start(bf16[512,512]{1,0:T(8,128)(2,1)} %collective-permute-done.2), channel_id=1, source_target_pairs={{0,1},{1,0},{2,3},{3,2},{4,5},{5,4},{6,7},{7,6},{8,9},{9,8},{10,11... | collective-permute-start | bytes 1572872 | tf_op jit(solution)/shard_map/cond/branch_1_fun/ppermute | solution.py:144
  68.2 4.4 %collective-permute-start.6 = (bf16[512,512]{1,0:T(8,128)(2,1)}, bf16[512,512]{1,0:T(8,128)(2,1)}, u32[]{:S(2)}, u32[]{:S(2)}) collective-permute-start(bf16[512,512]{1,0:T(8,128)(2,1)} %collective-permute-done.3), channel_id=1, source_target_pairs={{0,1},{1,0},{2,3},{3,2},{4,5},{5,4},{6,7},{7,6},{8,9},{9,8},{10,11... | collective-permute-start | bytes 1572872 | tf_op jit(solution)/shard_map/cond/branch_1_fun/ppermute | solution.py:144
  70.5 4.1 %collective-permute-start.4 = (bf16[512,512]{1,0:T(8,128)(2,1)}, bf16[512,512]{1,0:T(8,128)(2,1)}, u32[]{:S(2)}, u32[]{:S(2)}) collective-permute-start(bf16[512,512]{1,0:T(8,128)(2,1)} %collective-permute-done.1), channel_id=1, source_target_pairs={{0,1},{1,0},{2,3},{3,2},{4,5},{5,4},{6,7},{7,6},{8,9},{9,8},{10,11... | collective-permute-start | bytes 1572872 | tf_op jit(solution)/shard_map/cond/branch_1_fun/ppermute | solution.py:144
  100.3 23.9 %all-to-all-start.1 = ((f32[16,1,32]{2,1,0:T(1,128)}), f32[16,1,32]{2,1,0:T(1,128)S(1)}, u32[]{:S(2)}, u32[]{:S(2)}) async-start(f32[16,1,32]{2,1,0:T(1,128)} %broadcast_in_dim.48), calls=%async_computation.1 | async-start | bytes 16384 | tf_op jit(solution)/shard_map/all_to_all | solution.py:197

commit v12 on v11

--- a/solution.py
+++ b/solution.py
@@ -172,11 +172,13 @@
     )
     late = swap_half(mine, range(ZLO // 2, ZLO))
     precond = precondition(query_in[0, 0], query_out[0, 0], in_basis, out_basis, eigen_values[0])
-    token = lax.ppermute(
-        mine[:EXTRA],
-        ("zlo", "core"),
-        [(z * CORE + i, z * CORE + j) for z in range(ZLO // 2) for i, j in SWAP],
-    )
+    token = mine[:EXTRA]
+    for _ in range(2):
+        token = lax.ppermute(
+            token,
+            ("zlo", "core"),
+            [(z * CORE + i, z * CORE + j) for z in range(ZLO // 2) for i, j in SWAP],
+        )
     again, precond, token = lax.optimization_barrier((mine, precond, token))
     early = swap_half(again, range(ZLO // 2))
     preconds = lax.cond(

time: 125 us -> 127 us (1.016)
  starting transfers between devices: 57.3 us -> 64.9 us
  waiting for transfers between devices: 47.2 us -> 40.7 us
    ppermute x2, waiting for transfers between devices: 10.9 us -> 3.67 us  [swap_half(): return lax.ppermute(packed, ('zlo', 'zhi'), pairs)]
    all_to_all x1, starting transfers between devices: 5.13 us -> 10.5 us  [local(): summed = jnp.sum(lax.all_to_all(far, 'zlo', 0, 0), axis=0)]
    ppermute x1 -> x2, starting transfers between devices: 16 us -> 18.3 us  [local(): lax.ppermute(token, ('zlo', 'core'), [(z * CORE + i, z * CORE + j) for z...]
  transfers between devices with their start and end apart: 11 -> 12, of which waited for: 5 -> 7; matrix products, arithmetic and copies ran while one was open for 1% -> 1% of each run, Pallas kernels for 2% -> 2%
where the time goes in v12:
time: 127 us; the launch traced here: 126 us
  starting transfers between devices  64.9 us (51%)
  waiting for transfers between devices  40.7 us (32%)
  blocking collectives  10.3 us (8%)
  Pallas kernels  6.34 us (5%)
  local copies, waits for them, and re-layouts  1.3 us (1%)
    ppermute x2, starting transfers between devices, local(): lax.ppermute(token, ('zlo', 'core'), [(z * CORE + i, z * CORE + j) for z...  18.3 us
    all_to_all x1, waiting for transfers between devices, local(): summed = jnp.sum(lax.all_to_all(far, 'zlo', 0, 0), axis=0)  18.1 us
    ppermute x2, starting transfers between devices, swap_half(): return lax.ppermute(packed, ('zlo', 'zhi'), pairs)  16.8 us
    ppermute x3, waiting for transfers between devices, gather_preconds(): lax.ppermute(again if step == 1 else precond, 'x', [(i, i ^ step) for i i...  16.1 us
    all_to_all x1, starting transfers between devices, local(): summed = jnp.sum(lax.all_to_all(far, 'zlo', 0, 0), axis=0)  10.5 us
    all_to_all x1, blocking collectives, local(): near = jnp.sum(lax.all_to_all(spread, ('y', 'x', 'core'), 0, 0), axis=0)  10.3 us
    ppermute x3, starting transfers between devices, gather_preconds(): lax.ppermute(again if step == 1 else precond, 'x', [(i, i ^ step) for i i...  9.34 us
    ppermute x3, starting transfers between devices, gather_preconds(): beside = [lax.ppermute(p, 'core', SWAP) for p in along]  7.41 us
  transfers between devices with their start and end apart: 12, of which 7 were waited for; matrix products, arithmetic and copies ran while one was open for 1% of the time, Pallas kernels for 2%

profile of v12, /device:TPU:1, one launch (start us, length us, event | category | flops | bytes accessed | tf_op | source)
XLA Modules:
  0.0 126.0 jit_solution(17935491509334056127)
XLA Ops:
  0.0 0.0 copy-start
  0.0 0.0 copy-start.2
  0.0 0.0 copy-start.3
  0.0 0.0 copy-start.4
  0.0 0.0 copy-start.5
  0.0 2.6 %shard_map.91.packed_ref = bf16[1032,128]{1,0:T(8,128)(2,1)} custom-call(s32[2]{0:T(128)} %ids_ref.1, f32[128,512]{1,0:T(8,128)} %bitcast.29, f32[128,512]{1,0:T(8,128)} %bitcast.30, bf16[512,512]{1,0:T(8,128)(2,1)} %bitcast.25, bf16[512,512]{1,0:T(8,128)(2,1)} %bitcast.28), custom_call_target="tpu_custom_call" | custom-call | flops 13421772800 | bytes 786432 | tf_op jit(solution)/shard_map/pallas_call | solution.py:44
  2.6 0.0 copy-start.1
  2.6 0.8 collective-permute-start.7
  3.4 0.7 slice.4
  4.1 16.0 %collective-permute-start.8 = (bf16[8,128]{1,0:T(8,128)(2,1)S(1)}, bf16[8,128]{1,0:T(8,128)(2,1)S(1)}, u32[]{:S(2)}, u32[]{:S(2)}) collective-permute-start(bf16[8,128]{1,0:T(8,128)(2,1)S(1)} %slice.4), channel_id=1, source_target_pairs={{0,1},{1,0},{64,65},{65,64},{128,129},{129,128},{192,193},{193,192... | collective-permute-start | bytes 6152 | tf_op jit(solution)/shard_map/ppermute | solution.py:177
  20.1 0.0 copy-done.2
  20.1 0.0 copy-done.3
  20.1 0.3 convolution_convert_fusion
  20.4 0.5 collective-permute-done.8
  20.9 2.2 %collective-permute-start.9 = (bf16[8,128]{1,0:T(8,128)(2,1)S(1)}, bf16[8,128]{1,0:T(8,128)(2,1)S(1)}, u32[]{:S(2)}, u32[]{:S(2)}) collective-permute-start(bf16[8,128]{1,0:T(8,128)(2,1)S(1)} %collective-permute-done.8), channel_id=1, source_target_pairs={{0,1},{1,0},{64,65},{65,64},{128,129},{129,128},{192,193},{193,192... | collective-permute-start | bytes 6152 | tf_op jit(solution)/shard_map/ppermute | solution.py:177
  23.1 0.0 copy-done
  23.2 0.0 copy-done.4
  23.2 0.0 copy-done.5
  23.2 0.6 fusion.refs_0_
  23.8 0.1 collective-permute-done.9.token_ref
  23.9 0.0 copy-done.1
  24.0 16.0 %collective-permute-start.10 = (bf16[1032,128]{1,0:T(8,128)(2,1)S(1)}, bf16[1032,128]{1,0:T(8,128)(2,1)S(1)}, u32[]{:S(2)}, u32[]{:S(2)}) collective-permute-start(bf16[1032,128]{1,0:T(8,128)(2,1)S(1)} %copy-done.1), channel_id=1, source_target_pairs={{0,8},{8,0},{64,72},{72,64},{128,136},{136,128},{192,200},{200,192... | collective-permute-start | bytes 792584 | tf_op jit(solution)/shard_map/ppermute | solution.py:150
  40.0 37.7 %conditional.1 = (bf16[512,512]{1,0:T(8,128)(2,1)}, bf16[512,512]{1,0:T(8,128)(2,1)}, bf16[512,512]{1,0:T(8,128)(2,1)}, bf16[512,512]{1,0:T(8,128)(2,1)}, bf16[5...) conditional(s32[]{:T(128)} %convert_element_type.15, ...), branch_computations={%region_0.0_spmd, %region_1.0_spmd} | conditional | bytes 14680400 | solution.py:184
  40.0 2.5 %collective-permute-start = (bf16[512,512]{1,0:T(8,128)(2,1)S(1)}, bf16[512,512]{1,0:T(8,128)(2,1)}, u32[]{:S(2)}, u32[]{:S(2)}) collective-permute-start(bf16[512,512]{1,0:T(8,128)(2,1)S(1)} %param.1), channel_id=1, source_target_pairs={{0,1},{1,0},{2,3},{3,2},{4,5},{5,4},{6,7},{7,6},{8,9},{9,8},{10,11... | collective-permute-start | bytes 1572872 | tf_op jit(solution)/shard_map/cond/branch_1_fun/ppermute | solution.py:138
  42.6 4.7 %collective-permute-start.2 = (bf16[512,512]{1,0:T(8,128)(2,1)S(1)}, bf16[512,512]{1,0:T(8,128)(2,1)}, u32[]{:S(2)}, u32[]{:S(2)}) collective-permute-start(bf16[512,512]{1,0:T(8,128)(2,1)S(1)} %param.1), channel_id=1, source_target_pairs={{0,4},{2,6},{4,0},{6,2},{1,5},{3,7},{5,1},{7,3},{8,12},{10,14},{12... | collective-permute-start | bytes 1572872 | tf_op jit(solution)/shard_map/cond/branch_1_fun/ppermute | solution.py:141
  47.2 2.8 %collective-permute-start.3 = (bf16[512,512]{1,0:T(8,128)(2,1)S(1)}, bf16[512,512]{1,0:T(8,128)(2,1)}, u32[]{:S(2)}, u32[]{:S(2)}) collective-permute-start(bf16[512,512]{1,0:T(8,128)(2,1)S(1)} %param.1), channel_id=1, source_target_pairs={{0,6},{2,4},{4,2},{6,0},{1,7},{3,5},{5,3},{7,1},{8,14},{10,12},{12... | collective-permute-start | bytes 1572872 | tf_op jit(solution)/shard_map/cond/branch_1_fun/ppermute | solution.py:141
  50.0 0.0 collective-permute-done
  50.0 1.9 %collective-permute-start.1 = (bf16[512,512]{1,0:T(8,128)(2,1)S(1)}, bf16[512,512]{1,0:T(8,128)(2,1)}, u32[]{:S(2)}, u32[]{:S(2)}) collective-permute-start(bf16[512,512]{1,0:T(8,128)(2,1)S(1)} %param.1), channel_id=1, source_target_pairs={{0,2},{2,0},{4,6},{6,4},{1,3},{3,1},{5,7},{7,5},{8,10},{10,8},{12,... | collective-permute-start | bytes 1572872 | tf_op jit(solution)/shard_map/cond/branch_1_fun/ppermute | solution.py:141
  51.9 7.7 %collective-permute-done.2 = bf16[512,512]{1,0:T(8,128)(2,1)} collective-permute-done((bf16[512,512]{1,0:T(8,128)(2,1)S(1)}, bf16[512,512]{1,0:T(8,128)(2,1)}, u32[]{:S(2)}, u32[]{:S(2)}) %collective-permute-start.2) | collective-permute-done | bytes 524320 | tf_op jit(solution)/shard_map/cond/branch_1_fun/ppermute | solution.py:141
  59.7 3.1 %collective-permute-start.5 = (bf16[512,512]{1,0:T(8,128)(2,1)}, bf16[512,512]{1,0:T(8,128)(2,1)}, u32[]{:S(2)}, u32[]{:S(2)}) collective-permute-start(bf16[512,512]{1,0:T(8,128)(2,1)} %collective-permute-done.2), channel_id=1, source_target_pairs={{0,1},{1,0},{2,3},{3,2},{4,5},{5,4},{6,7},{7,6},{8,9},{9,8},{10,11... | collective-permute-start | bytes 1572872 | tf_op jit(solution)/shard_map/cond/branch_1_fun/ppermute | solution.py:144
  62.8 8.4 %collective-permute-done.3 = bf16[512,512]{1,0:T(8,128)(2,1)} collective-permute-done((bf16[512,512]{1,0:T(8,128)(2,1)S(1)}, bf16[512,512]{1,0:T(8,128)(2,1)}, u32[]{:S(2)}, u32[]{:S(2)}) %collective-permute-start.3) | collective-permute-done | bytes 524320 | tf_op jit(solution)/shard_map/cond/branch_1_fun/ppermute | solution.py:141
  71.2 2.4 %collective-permute-start.6 = (bf16[512,512]{1,0:T(8,128)(2,1)}, bf16[512,512]{1,0:T(8,128)(2,1)}, u32[]{:S(2)}, u32[]{:S(2)}) collective-permute-start(bf16[512,512]{1,0:T(8,128)(2,1)} %collective-permute-done.3), channel_id=1, source_target_pairs={{0,1},{1,0},{2,3},{3,2},{4,5},{5,4},{6,7},{7,6},{8,9},{9,8},{10,11... | collective-permute-start | bytes 1572872 | tf_op jit(solution)/shard_map/cond/branch_1_fun/ppermute | solution.py:144
  73.6 0.0 collective-permute-done.1
  73.6 2.0 %collective-permute-start.4 = (bf16[512,512]{1,0:T(8,128)(2,1)}, bf16[512,512]{1,0:T(8,128)(2,1)}, u32[]{:S(2)}, u32[]{:S(2)}) collective-permute-start(bf16[512,512]{1,0:T(8,128)(2,1)} %collective-permute-done.1), channel_id=1, source_target_pairs={{0,1},{1,0},{2,3},{3,2},{4,5},{5,4},{6,7},{7,6},{8,9},{9,8},{10,11... | collective-permute-start | bytes 1572872 | tf_op jit(solution)/shard_map/cond/branch_1_fun/ppermute | solution.py:144
  75.5 0.0 collective-permute-done.5
  75.5 0.0 collective-permute-done.6
  75.5 2.2 %collective-permute-done.4 = bf16[512,512]{1,0:T(8,128)(2,1)} collective-permute-done((bf16[512,512]{1,0:T(8,128)(2,1)}, bf16[512,512]{1,0:T(8,128)(2,1)}, u32[]{:S(2)}, u32[]{:S(2)}) %collective-permute-start.4) | collective-permute-done | bytes 524320 | tf_op jit(solution)/shard_map/cond/branch_1_fun/ppermute | solution.py:144
  77.7 2.9 %shard_map.92 = (bf16[8,512,512]{2,1,0:T(8,128)(2,1)S(1)}, f32[8,32]{1,0:T(8,128)S(1)}) custom-call(bf16[1032,128]{1,0:T(8,128)(2,1)S(1)} %copy-done.1, bf16[512,512]{1,0:T(8,128)(2,1)S(1)} %fusion.refs_0_, bf16[512,512]{1,0:T(8,128)(2,1)} %get-tuple-element.24.refs_1_, bf16[512,512]{1,0:T(8,128)(2,1)} %get-tuple-element.25.refs_2_, ...), custom_call_target="tpu_custom_call" | custom-call | tf_op jit(solution)/shard_map/pallas_call | solution.py:98
  80.7 0.0 collective-permute-done.7.late_ref
  80.7 3.7 %collective-permute-done.10.early_ref = bf16[1032,128]{1,0:T(8,128)(2,1)S(1)} collective-permute-done((bf16[1032,128]{1,0:T(8,128)(2,1)S(1)}, bf16[1032,128]{1,0:T(8,128)(2,1)S(1)}, u32[]{:S(2)}, u32[]{:S(2)}) %collective-permute-start.10) | collective-permute-done | bytes 264224 | tf_op jit(solution)/shard_map/ppermute | solution.py:150
  84.3 0.9 shard_map.93
  85.2 0.1 select_reduce_fusion
  85.3 10.3 %all_to_all.15 = f32[32,1,32]{2,1,0:T(1,128)S(1)} all-to-all(f32[32,1,32]{2,1,0:T(1,128)S(1)} %bitcast.26), channel_id=1, replica_groups=mesh['zlo'=16,'y'=4,'zhi'=2,'x'=4,'core'=2] {'y','x','core'}, dimensions={0} | all-to-all | bytes 8192 | tf_op jit(solution)/shard_map/all_to_all | solution.py:197
  95.6 0.1 reduce_sum.28
  95.7 0.6 broadcast_in_dim.48
  96.3 10.5 %all-to-all-start.1 = ((f32[16,1,32]{2,1,0:T(1,128)}), f32[16,1,32]{2,1,0:T(1,128)S(1)}, u32[]{:S(2)}, u32[]{:S(2)}) async-start(f32[16,1,32]{2,1,0:T(1,128)} %broadcast_in_dim.48), calls=%async_computation.1 | async-start | bytes 16384 | tf_op jit(solution)/shard_map/all_to_all | solution.py:199
  107.4 18.1 %all-to-all-done.1 = f32[16,1,32]{2,1,0:T(1,128)S(1)} async-done(((f32[16,1,32]{2,1,0:T(1,128)}), f32[16,1,32]{2,1,0:T(1,128)S(1)}, u32[]{:S(2)}, u32[]{:S(2)}) %all-to-all-start.1) | async-done | bytes 2080 | tf_op jit(solution)/shard_map/all_to_all | solution.py:199
  125.5 0.5 compare_select_fusion
  (4 shorter events, 0.0 us)
Async XLA Ops:
  0.0 23.2 %copy-start = (bf16[1,1,256,512]{3,2,1,0:T(8,128)(2,1)S(1)}, bf16[1,1,256,512]{3,2,1,0:T(8,128)(2,1)}, u32[]{:S(2)}) copy-start(bf16[1,1,256,512]{3,2,1,0:T(8,128)(2,1)} %param.14) | copy-start | bytes 786436
  0.0 20.1 %copy-start.2 = (bf16[1,512,512]{2,1,0:T(8,128)(2,1)S(1)}, bf16[1,512,512]{2,1,0:T(8,128)(2,1)}, u32[]{:S(2)}) copy-start(bf16[1,512,512]{2,1,0:T(8,128)(2,1)} %param.15) | copy-start | bytes 1572868
  0.0 20.1 %copy-start.3 = (bf16[1,1,256,512]{3,2,1,0:T(8,128)(2,1)S(1)}, bf16[1,1,256,512]{3,2,1,0:T(8,128)(2,1)}, u32[]{:S(2)}) copy-start(bf16[1,1,256,512]{3,2,1,0:T(8,128)(2,1)} %param.13) | copy-start | bytes 786436
  0.0 23.2 %copy-start.4 = (f32[1,512,512]{2,1,0:T(8,128)S(1)}, f32[1,512,512]{2,1,0:T(8,128)}, u32[]{:S(2)}) copy-start(f32[1,512,512]{2,1,0:T(8,128)} %param.17) | copy-start | bytes 3145732
  0.0 23.2 %copy-start.5 = (bf16[1,512,512]{2,1,0:T(8,128)(2,1)S(1)}, bf16[1,512,512]{2,1,0:T(8,128)(2,1)}, u32[]{:S(2)}) copy-start(bf16[1,512,512]{2,1,0:T(8,128)(2,1)} %param.16) | copy-start | bytes 1572868
  2.6 21.4 %copy-start.1 = (bf16[1032,128]{1,0:T(8,128)(2,1)S(1)}, bf16[1032,128]{1,0:T(8,128)(2,1)}, u32[]{:S(2)}) copy-start(bf16[1032,128]{1,0:T(8,128)(2,1)} %shard_map.91.packed_ref) | copy-start | bytes 792580
  2.6 78.1 %collective-permute-start.7 = (bf16[1032,128]{1,0:T(8,128)(2,1)}, bf16[1032,128]{1,0:T(8,128)(2,1)S(1)}, u32[]{:S(2)}, u32[]{:S(2)}) collective-permute-start(bf16[1032,128]{1,0:T(8,128)(2,1)} %shard_map.91.packed_ref), channel_id=1, source_target_pairs={{512,520},{520,512},{576,584},{584,576},{640,648},{648,640},{704,7... | collective-permute-start | bytes 792584 | tf_op jit(solution)/shard_map/ppermute | solution.py:150
  4.1 16.8 %collective-permute-start.8 = (bf16[8,128]{1,0:T(8,128)(2,1)S(1)}, bf16[8,128]{1,0:T(8,128)(2,1)S(1)}, u32[]{:S(2)}, u32[]{:S(2)}) collective-permute-start(bf16[8,128]{1,0:T(8,128)(2,1)S(1)} %slice.4), channel_id=1, source_target_pairs={{0,1},{1,0},{64,65},{65,64},{128,129},{129,128},{192,193},{193,192... | collective-permute-start | bytes 6152 | tf_op jit(solution)/shard_map/ppermute | solution.py:177
  20.9 3.0 %collective-permute-start.9 = (bf16[8,128]{1,0:T(8,128)(2,1)S(1)}, bf16[8,128]{1,0:T(8,128)(2,1)S(1)}, u32[]{:S(2)}, u32[]{:S(2)}) collective-permute-start(bf16[8,128]{1,0:T(8,128)(2,1)S(1)} %collective-permute-done.8), channel_id=1, source_target_pairs={{0,1},{1,0},{64,65},{65,64},{128,129},{129,128},{192,193},{193,192... | collective-permute-start | bytes 6152 | tf_op jit(solution)/shard_map/ppermute | solution.py:177
  24.0 60.4 %collective-permute-start.10 = (bf16[1032,128]{1,0:T(8,128)(2,1)S(1)}, bf16[1032,128]{1,0:T(8,128)(2,1)S(1)}, u32[]{:S(2)}, u32[]{:S(2)}) collective-permute-start(bf16[1032,128]{1,0:T(8,128)(2,1)S(1)} %copy-done.1), channel_id=1, source_target_pairs={{0,8},{8,0},{64,72},{72,64},{128,136},{136,128},{192,200},{200,192... | collective-permute-start | bytes 792584 | tf_op jit(solution)/shard_map/ppermute | solution.py:150
  40.0 10.0 %collective-permute-start = (bf16[512,512]{1,0:T(8,128)(2,1)S(1)}, bf16[512,512]{1,0:T(8,128)(2,1)}, u32[]{:S(2)}, u32[]{:S(2)}) collective-permute-start(bf16[512,512]{1,0:T(8,128)(2,1)S(1)} %param.1), channel_id=1, source_target_pairs={{0,1},{1,0},{2,3},{3,2},{4,5},{5,4},{6,7},{7,6},{8,9},{9,8},{10,11... | collective-permute-start | bytes 1572872 | tf_op jit(solution)/shard_map/cond/branch_1_fun/ppermute | solution.py:138
  42.6 17.1 %collective-permute-start.2 = (bf16[512,512]{1,0:T(8,128)(2,1)S(1)}, bf16[512,512]{1,0:T(8,128)(2,1)}, u32[]{:S(2)}, u32[]{:S(2)}) collective-permute-start(bf16[512,512]{1,0:T(8,128)(2,1)S(1)} %param.1), channel_id=1, source_target_pairs={{0,4},{2,6},{4,0},{6,2},{1,5},{3,7},{5,1},{7,3},{8,12},{10,14},{12... | collective-permute-start | bytes 1572872 | tf_op jit(solution)/shard_map/cond/branch_1_fun/ppermute | solution.py:141
  47.2 24.0 %collective-permute-start.3 = (bf16[512,512]{1,0:T(8,128)(2,1)S(1)}, bf16[512,512]{1,0:T(8,128)(2,1)}, u32[]{:S(2)}, u32[]{:S(2)}) collective-permute-start(bf16[512,512]{1,0:T(8,128)(2,1)S(1)} %param.1), channel_id=1, source_target_pairs={{0,6},{2,4},{4,2},{6,0},{1,7},{3,5},{5,3},{7,1},{8,14},{10,12},{12... | collective-permute-start | bytes 1572872 | tf_op jit(solution)/shard_map/cond/branch_1_fun/ppermute | solution.py:141
  50.0 23.5 %collective-permute-start.1 = (bf16[512,512]{1,0:T(8,128)(2,1)S(1)}, bf16[512,512]{1,0:T(8,128)(2,1)}, u32[]{:S(2)}, u32[]{:S(2)}) collective-permute-start(bf16[512,512]{1,0:T(8,128)(2,1)S(1)} %param.1), channel_id=1, source_target_pairs={{0,2},{2,0},{4,6},{6,4},{1,3},{3,1},{5,7},{7,5},{8,10},{10,8},{12,... | collective-permute-start | bytes 1572872 | tf_op jit(solution)/shard_map/cond/branch_1_fun/ppermute | solution.py:141
  59.7 15.9 %collective-permute-start.5 = (bf16[512,512]{1,0:T(8,128)(2,1)}, bf16[512,512]{1,0:T(8,128)(2,1)}, u32[]{:S(2)}, u32[]{:S(2)}) collective-permute-start(bf16[512,512]{1,0:T(8,128)(2,1)} %collective-permute-done.2), channel_id=1, source_target_pairs={{0,1},{1,0},{2,3},{3,2},{4,5},{5,4},{6,7},{7,6},{8,9},{9,8},{10,11... | collective-permute-start | bytes 1572872 | tf_op jit(solution)/shard_map/cond/branch_1_fun/ppermute | solution.py:144
  71.2 4.4 %collective-permute-start.6 = (bf16[512,512]{1,0:T(8,128)(2,1)}, bf16[512,512]{1,0:T(8,128)(2,1)}, u32[]{:S(2)}, u32[]{:S(2)}) collective-permute-start(bf16[512,512]{1,0:T(8,128)(2,1)} %collective-permute-done.3), channel_id=1, source_target_pairs={{0,1},{1,0},{2,3},{3,2},{4,5},{5,4},{6,7},{7,6},{8,9},{9,8},{10,11... | collective-permute-start | bytes 1572872 | tf_op jit(solution)/shard_map/cond/branch_1_fun/ppermute | solution.py:144
  73.6 4.1 %collective-permute-start.4 = (bf16[512,512]{1,0:T(8,128)(2,1)}, bf16[512,512]{1,0:T(8,128)(2,1)}, u32[]{:S(2)}, u32[]{:S(2)}) collective-permute-start(bf16[512,512]{1,0:T(8,128)(2,1)} %collective-permute-done.1), channel_id=1, source_target_pairs={{0,1},{1,0},{2,3},{3,2},{4,5},{5,4},{6,7},{7,6},{8,9},{9,8},{10,11... | collective-permute-start | bytes 1572872 | tf_op jit(solution)/shard_map/cond/branch_1_fun/ppermute | solution.py:144
  96.3 29.2 %all-to-all-start.1 = ((f32[16,1,32]{2,1,0:T(1,128)}), f32[16,1,32]{2,1,0:T(1,128)S(1)}, u32[]{:S(2)}, u32[]{:S(2)}) async-start(f32[16,1,32]{2,1,0:T(1,128)} %broadcast_in_dim.48), calls=%async_computation.1 | async-start | bytes 16384 | tf_op jit(solution)/shard_map/all_to_all | solution.py:199

commit v13 on v11

--- a/solution.py
+++ b/solution.py
@@ -13,6 +13,7 @@
 ZLO, Y, ZHI, X, CORE = 16, 4, 2, 4, 2
 NAMES = ("zlo", "y", "zhi", "x", "core")
 SWAP = [(0, 1), (1, 0)]
+EARLY = 6
 LANES = 128
 EXTRA = 8
 
@@ -170,15 +171,15 @@
     mine = pack_train(
         train_ids, train_in[0].reshape(tokens), train_out[0].reshape(tokens), in_basis, out_basis
     )
-    late = swap_half(mine, range(ZLO // 2, ZLO))
+    late = swap_half(mine, range(EARLY, ZLO))
     precond = precondition(query_in[0, 0], query_out[0, 0], in_basis, out_basis, eigen_values[0])
     token = lax.ppermute(
         mine[:EXTRA],
         ("zlo", "core"),
-        [(z * CORE + i, z * CORE + j) for z in range(ZLO // 2) for i, j in SWAP],
+        [(z * CORE + i, z * CORE + j) for z in range(EARLY) for i, j in SWAP],
     )
     again, precond, token = lax.optimization_barrier((mine, precond, token))
-    early = swap_half(again, range(ZLO // 2))
+    early = swap_half(again, range(EARLY))
     preconds = lax.cond(
         lax.axis_index("x") < X, gather_preconds, lambda precond: [precond] * (X * CORE), precond
     )

time: 125 us -> 128 us (1.024)
  starting transfers between devices: 57.3 us -> 60.5 us
    all_to_all x1, starting transfers between devices: 5.13 us -> 8.36 us  [local(): summed = jnp.sum(lax.all_to_all(far, 'zlo', 0, 0), axis=0)]
where the time goes in v13:
time: 128 us
  starting transfers between devices  60.5 us (47%)
  waiting for transfers between devices  47 us (37%)
  blocking collectives  10.1 us (8%)
  Pallas kernels  6.33 us (5%)
  local copies, waits for them, and re-layouts  1.3 us (1%)
    all_to_all x1, waiting for transfers between devices, local(): summed = jnp.sum(lax.all_to_all(far, 'zlo', 0, 0), axis=0)  18.1 us
    ppermute x2, starting transfers between devices, swap_half(): return lax.ppermute(packed, ('zlo', 'zhi'), pairs)  16.8 us
    ppermute x1, starting transfers between devices, local(): lax.ppermute(mine[:EXTRA], ('zlo', 'core'), [(z * CORE + i, z * CORE + j)...  16 us
    ppermute x3, waiting for transfers between devices, gather_preconds(): lax.ppermute(again if step == 1 else precond, 'x', [(i, i ^ step) for i i...  16 us
    ppermute x2, waiting for transfers between devices, swap_half(): return lax.ppermute(packed, ('zlo', 'zhi'), pairs)  10.7 us
    all_to_all x1, blocking collectives, local(): near = jnp.sum(lax.all_to_all(spread, ('y', 'x', 'core'), 0, 0), axis=0)  10.1 us
    ppermute x3, starting transfers between devices, gather_preconds(): lax.ppermute(again if step == 1 else precond, 'x', [(i, i ^ step) for i i...  9.36 us
    all_to_all x1, starting transfers between devices, local(): summed = jnp.sum(lax.all_to_all(far, 'zlo', 0, 0), axis=0)  8.36 us
  transfers between devices with their start and end apart: 11, of which 5 were waited for; matrix products, arithmetic and copies ran while one was open for 1% of the time, Pallas kernels for 2%

profile of v13, /device:TPU:1, one launch (start us, length us, event | category | flops | bytes accessed | tf_op | source)
XLA Modules:
  0.0 127.8 jit_solution(17524664483229456076)
XLA Ops:
  0.0 0.0 copy-start
  0.0 0.0 copy-start.2
  0.0 0.0 copy-start.3
  0.0 0.0 copy-start.4
  0.0 0.0 copy-start.5
  0.0 2.5 %shard_map.91.packed_ref = bf16[1032,128]{1,0:T(8,128)(2,1)} custom-call(s32[2]{0:T(128)} %ids_ref.1, f32[128,512]{1,0:T(8,128)} %bitcast.29, f32[128,512]{1,0:T(8,128)} %bitcast.30, bf16[512,512]{1,0:T(8,128)(2,1)} %bitcast.25, bf16[512,512]{1,0:T(8,128)(2,1)} %bitcast.28), custom_call_target="tpu_custom_call" | custom-call | flops 13421772800 | bytes 786432 | tf_op jit(solution)/shard_map/pallas_call | solution.py:45
  2.6 0.0 copy-start.1
  2.6 0.8 collective-permute-start.7
  3.4 0.7 slice.4
  4.0 16.0 %collective-permute-start.8 = (bf16[8,128]{1,0:T(8,128)(2,1)S(1)}, bf16[8,128]{1,0:T(8,128)(2,1)S(1)}, u32[]{:S(2)}, u32[]{:S(2)}) collective-permute-start(bf16[8,128]{1,0:T(8,128)(2,1)S(1)} %slice.4), channel_id=1, source_target_pairs={{0,1},{1,0},{64,65},{65,64},{128,129},{129,128},{192,193},{193,192... | collective-permute-start | bytes 6152 | tf_op jit(solution)/shard_map/ppermute | solution.py:176
  20.1 0.0 copy-done.2
  20.1 0.0 copy-done.3
  20.1 0.3 convolution_convert_fusion
  20.4 0.0 copy-done
  20.4 0.0 copy-done.4
  20.4 0.0 copy-done.5
  20.5 0.6 fusion.refs_0_
  21.1 0.0 collective-permute-done.8.token_ref
  21.1 0.0 copy-done.1
  21.1 16.1 %collective-permute-start.9 = (bf16[1032,128]{1,0:T(8,128)(2,1)S(1)}, bf16[1032,128]{1,0:T(8,128)(2,1)S(1)}, u32[]{:S(2)}, u32[]{:S(2)}) collective-permute-start(bf16[1032,128]{1,0:T(8,128)(2,1)S(1)} %copy-done.1), channel_id=1, source_target_pairs={{0,8},{8,0},{64,72},{72,64},{128,136},{136,128},{192,200},{200,192... | collective-permute-start | bytes 792584 | tf_op jit(solution)/shard_map/ppermute | solution.py:151
  37.2 37.5 %conditional.1 = (bf16[512,512]{1,0:T(8,128)(2,1)}, bf16[512,512]{1,0:T(8,128)(2,1)}, bf16[512,512]{1,0:T(8,128)(2,1)}, bf16[512,512]{1,0:T(8,128)(2,1)}, bf16[5...) conditional(s32[]{:T(128)} %convert_element_type.15, ...), branch_computations={%region_0.0_spmd, %region_1.0_spmd} | conditional | bytes 14680400 | solution.py:183
  37.2 2.3 %collective-permute-start = (bf16[512,512]{1,0:T(8,128)(2,1)S(1)}, bf16[512,512]{1,0:T(8,128)(2,1)}, u32[]{:S(2)}, u32[]{:S(2)}) collective-permute-start(bf16[512,512]{1,0:T(8,128)(2,1)S(1)} %param.1), channel_id=1, source_target_pairs={{0,1},{1,0},{2,3},{3,2},{4,5},{5,4},{6,7},{7,6},{8,9},{9,8},{10,11... | collective-permute-start | bytes 1572872 | tf_op jit(solution)/shard_map/cond/branch_1_fun/ppermute | solution.py:139
  39.5 4.7 %collective-permute-start.2 = (bf16[512,512]{1,0:T(8,128)(2,1)S(1)}, bf16[512,512]{1,0:T(8,128)(2,1)}, u32[]{:S(2)}, u32[]{:S(2)}) collective-permute-start(bf16[512,512]{1,0:T(8,128)(2,1)S(1)} %param.1), channel_id=1, source_target_pairs={{0,4},{2,6},{4,0},{6,2},{1,5},{3,7},{5,1},{7,3},{8,12},{10,14},{12... | collective-permute-start | bytes 1572872 | tf_op jit(solution)/shard_map/cond/branch_1_fun/ppermute | solution.py:142
  44.2 2.8 %collective-permute-start.3 = (bf16[512,512]{1,0:T(8,128)(2,1)S(1)}, bf16[512,512]{1,0:T(8,128)(2,1)}, u32[]{:S(2)}, u32[]{:S(2)}) collective-permute-start(bf16[512,512]{1,0:T(8,128)(2,1)S(1)} %param.1), channel_id=1, source_target_pairs={{0,6},{2,4},{4,2},{6,0},{1,7},{3,5},{5,3},{7,1},{8,14},{10,12},{12... | collective-permute-start | bytes 1572872 | tf_op jit(solution)/shard_map/cond/branch_1_fun/ppermute | solution.py:142
  47.0 0.0 collective-permute-done
  47.0 1.9 %collective-permute-start.1 = (bf16[512,512]{1,0:T(8,128)(2,1)S(1)}, bf16[512,512]{1,0:T(8,128)(2,1)}, u32[]{:S(2)}, u32[]{:S(2)}) collective-permute-start(bf16[512,512]{1,0:T(8,128)(2,1)S(1)} %param.1), channel_id=1, source_target_pairs={{0,2},{2,0},{4,6},{6,4},{1,3},{3,1},{5,7},{7,5},{8,10},{10,8},{12,... | collective-permute-start | bytes 1572872 | tf_op jit(solution)/shard_map/cond/branch_1_fun/ppermute | solution.py:142
  48.9 7.6 %collective-permute-done.2 = bf16[512,512]{1,0:T(8,128)(2,1)} collective-permute-done((bf16[512,512]{1,0:T(8,128)(2,1)S(1)}, bf16[512,512]{1,0:T(8,128)(2,1)}, u32[]{:S(2)}, u32[]{:S(2)}) %collective-permute-start.2) | collective-permute-done | bytes 524320 | tf_op jit(solution)/shard_map/cond/branch_1_fun/ppermute | solution.py:142
  56.6 3.2 %collective-permute-start.5 = (bf16[512,512]{1,0:T(8,128)(2,1)}, bf16[512,512]{1,0:T(8,128)(2,1)}, u32[]{:S(2)}, u32[]{:S(2)}) collective-permute-start(bf16[512,512]{1,0:T(8,128)(2,1)} %collective-permute-done.2), channel_id=1, source_target_pairs={{0,1},{1,0},{2,3},{3,2},{4,5},{5,4},{6,7},{7,6},{8,9},{9,8},{10,11... | collective-permute-start | bytes 1572872 | tf_op jit(solution)/shard_map/cond/branch_1_fun/ppermute | solution.py:145
  59.8 8.4 %collective-permute-done.3 = bf16[512,512]{1,0:T(8,128)(2,1)} collective-permute-done((bf16[512,512]{1,0:T(8,128)(2,1)S(1)}, bf16[512,512]{1,0:T(8,128)(2,1)}, u32[]{:S(2)}, u32[]{:S(2)}) %collective-permute-start.3) | collective-permute-done | bytes 524320 | tf_op jit(solution)/shard_map/cond/branch_1_fun/ppermute | solution.py:142
  68.2 2.4 %collective-permute-start.6 = (bf16[512,512]{1,0:T(8,128)(2,1)}, bf16[512,512]{1,0:T(8,128)(2,1)}, u32[]{:S(2)}, u32[]{:S(2)}) collective-permute-start(bf16[512,512]{1,0:T(8,128)(2,1)} %collective-permute-done.3), channel_id=1, source_target_pairs={{0,1},{1,0},{2,3},{3,2},{4,5},{5,4},{6,7},{7,6},{8,9},{9,8},{10,11... | collective-permute-start | bytes 1572872 | tf_op jit(solution)/shard_map/cond/branch_1_fun/ppermute | solution.py:145
  70.5 0.0 collective-permute-done.1
  70.5 1.9 %collective-permute-start.4 = (bf16[512,512]{1,0:T(8,128)(2,1)}, bf16[512,512]{1,0:T(8,128)(2,1)}, u32[]{:S(2)}, u32[]{:S(2)}) collective-permute-start(bf16[512,512]{1,0:T(8,128)(2,1)} %collective-permute-done.1), channel_id=1, source_target_pairs={{0,1},{1,0},{2,3},{3,2},{4,5},{5,4},{6,7},{7,6},{8,9},{9,8},{10,11... | collective-permute-start | bytes 1572872 | tf_op jit(solution)/shard_map/cond/branch_1_fun/ppermute | solution.py:145
  72.5 0.0 collective-permute-done.5
  72.5 0.0 collective-permute-done.6
  72.5 2.2 %collective-permute-done.4 = bf16[512,512]{1,0:T(8,128)(2,1)} collective-permute-done((bf16[512,512]{1,0:T(8,128)(2,1)}, bf16[512,512]{1,0:T(8,128)(2,1)}, u32[]{:S(2)}, u32[]{:S(2)}) %collective-permute-start.4) | collective-permute-done | bytes 524320 | tf_op jit(solution)/shard_map/cond/branch_1_fun/ppermute | solution.py:145
  74.7 2.9 %shard_map.92 = (bf16[8,512,512]{2,1,0:T(8,128)(2,1)S(1)}, f32[8,32]{1,0:T(8,128)S(1)}) custom-call(bf16[1032,128]{1,0:T(8,128)(2,1)S(1)} %copy-done.1, bf16[512,512]{1,0:T(8,128)(2,1)S(1)} %fusion.refs_0_, bf16[512,512]{1,0:T(8,128)(2,1)} %get-tuple-element.24.refs_1_, bf16[512,512]{1,0:T(8,128)(2,1)} %get-tuple-element.25.refs_2_, ...), custom_call_target="tpu_custom_call" | custom-call | tf_op jit(solution)/shard_map/pallas_call | solution.py:99
  77.6 0.0 collective-permute-done.7.late_ref
  77.6 10.7 %collective-permute-done.9.early_ref = bf16[1032,128]{1,0:T(8,128)(2,1)S(1)} collective-permute-done((bf16[1032,128]{1,0:T(8,128)(2,1)S(1)}, bf16[1032,128]{1,0:T(8,128)(2,1)S(1)}, u32[]{:S(2)}, u32[]{:S(2)}) %collective-permute-start.9) | collective-permute-done | bytes 264224 | tf_op jit(solution)/shard_map/ppermute | solution.py:151
  88.4 0.9 shard_map.93
  89.2 0.1 select_reduce_fusion
  89.3 10.1 %all_to_all.15 = f32[32,1,32]{2,1,0:T(1,128)S(1)} all-to-all(f32[32,1,32]{2,1,0:T(1,128)S(1)} %bitcast.26), channel_id=1, replica_groups=mesh['zlo'=16,'y'=4,'zhi'=2,'x'=4,'core'=2] {'y','x','core'}, dimensions={0} | all-to-all | bytes 8192 | tf_op jit(solution)/shard_map/all_to_all | solution.py:196
  99.5 0.1 reduce_sum.28
  99.5 0.6 broadcast_in_dim.48
  100.1 8.4 %all-to-all-start.1 = ((f32[16,1,32]{2,1,0:T(1,128)}), f32[16,1,32]{2,1,0:T(1,128)S(1)}, u32[]{:S(2)}, u32[]{:S(2)}) async-start(f32[16,1,32]{2,1,0:T(1,128)} %broadcast_in_dim.48), calls=%async_computation.1 | async-start | bytes 16384 | tf_op jit(solution)/shard_map/all_to_all | solution.py:198
  109.1 18.1 %all-to-all-done.1 = f32[16,1,32]{2,1,0:T(1,128)S(1)} async-done(((f32[16,1,32]{2,1,0:T(1,128)}), f32[16,1,32]{2,1,0:T(1,128)S(1)}, u32[]{:S(2)}, u32[]{:S(2)}) %all-to-all-start.1) | async-done | bytes 2080 | tf_op jit(solution)/shard_map/all_to_all | solution.py:198
  127.3 0.5 compare_select_fusion
  (4 shorter events, 0.0 us)
Async XLA Ops:
  0.0 20.4 %copy-start = (bf16[1,1,256,512]{3,2,1,0:T(8,128)(2,1)S(1)}, bf16[1,1,256,512]{3,2,1,0:T(8,128)(2,1)}, u32[]{:S(2)}) copy-start(bf16[1,1,256,512]{3,2,1,0:T(8,128)(2,1)} %param.14) | copy-start | bytes 786436
  0.0 20.1 %copy-start.2 = (bf16[1,512,512]{2,1,0:T(8,128)(2,1)S(1)}, bf16[1,512,512]{2,1,0:T(8,128)(2,1)}, u32[]{:S(2)}) copy-start(bf16[1,512,512]{2,1,0:T(8,128)(2,1)} %param.15) | copy-start | bytes 1572868
  0.0 20.1 %copy-start.3 = (bf16[1,1,256,512]{3,2,1,0:T(8,128)(2,1)S(1)}, bf16[1,1,256,512]{3,2,1,0:T(8,128)(2,1)}, u32[]{:S(2)}) copy-start(bf16[1,1,256,512]{3,2,1,0:T(8,128)(2,1)} %param.13) | copy-start | bytes 786436
  0.0 20.4 %copy-start.4 = (f32[1,512,512]{2,1,0:T(8,128)S(1)}, f32[1,512,512]{2,1,0:T(8,128)}, u32[]{:S(2)}) copy-start(f32[1,512,512]{2,1,0:T(8,128)} %param.17) | copy-start | bytes 3145732
  0.0 20.4 %copy-start.5 = (bf16[1,512,512]{2,1,0:T(8,128)(2,1)S(1)}, bf16[1,512,512]{2,1,0:T(8,128)(2,1)}, u32[]{:S(2)}) copy-start(bf16[1,512,512]{2,1,0:T(8,128)(2,1)} %param.16) | copy-start | bytes 1572868
  2.6 18.5 %copy-start.1 = (bf16[1032,128]{1,0:T(8,128)(2,1)S(1)}, bf16[1032,128]{1,0:T(8,128)(2,1)}, u32[]{:S(2)}) copy-start(bf16[1032,128]{1,0:T(8,128)(2,1)} %shard_map.91.packed_ref) | copy-start | bytes 792580
  2.6 75.1 %collective-permute-start.7 = (bf16[1032,128]{1,0:T(8,128)(2,1)}, bf16[1032,128]{1,0:T(8,128)(2,1)S(1)}, u32[]{:S(2)}, u32[]{:S(2)}) collective-permute-start(bf16[1032,128]{1,0:T(8,128)(2,1)} %shard_map.91.packed_ref), channel_id=1, source_target_pairs={{384,392},{392,384},{448,456},{456,448},{512,520},{520,512},{576,5... | collective-permute-start | bytes 792584 | tf_op jit(solution)/shard_map/ppermute | solution.py:151
  4.0 17.0 %collective-permute-start.8 = (bf16[8,128]{1,0:T(8,128)(2,1)S(1)}, bf16[8,128]{1,0:T(8,128)(2,1)S(1)}, u32[]{:S(2)}, u32[]{:S(2)}) collective-permute-start(bf16[8,128]{1,0:T(8,128)(2,1)S(1)} %slice.4), channel_id=1, source_target_pairs={{0,1},{1,0},{64,65},{65,64},{128,129},{129,128},{192,193},{193,192... | collective-permute-start | bytes 6152 | tf_op jit(solution)/shard_map/ppermute | solution.py:176
  21.1 67.3 %collective-permute-start.9 = (bf16[1032,128]{1,0:T(8,128)(2,1)S(1)}, bf16[1032,128]{1,0:T(8,128)(2,1)S(1)}, u32[]{:S(2)}, u32[]{:S(2)}) collective-permute-start(bf16[1032,128]{1,0:T(8,128)(2,1)S(1)} %copy-done.1), channel_id=1, source_target_pairs={{0,8},{8,0},{64,72},{72,64},{128,136},{136,128},{192,200},{200,192... | collective-permute-start | bytes 792584 | tf_op jit(solution)/shard_map/ppermute | solution.py:151
  37.2 9.8 %collective-permute-start = (bf16[512,512]{1,0:T(8,128)(2,1)S(1)}, bf16[512,512]{1,0:T(8,128)(2,1)}, u32[]{:S(2)}, u32[]{:S(2)}) collective-permute-start(bf16[512,512]{1,0:T(8,128)(2,1)S(1)} %param.1), channel_id=1, source_target_pairs={{0,1},{1,0},{2,3},{3,2},{4,5},{5,4},{6,7},{7,6},{8,9},{9,8},{10,11... | collective-permute-start | bytes 1572872 | tf_op jit(solution)/shard_map/cond/branch_1_fun/ppermute | solution.py:139
  39.5 17.0 %collective-permute-start.2 = (bf16[512,512]{1,0:T(8,128)(2,1)S(1)}, bf16[512,512]{1,0:T(8,128)(2,1)}, u32[]{:S(2)}, u32[]{:S(2)}) collective-permute-start(bf16[512,512]{1,0:T(8,128)(2,1)S(1)} %param.1), channel_id=1, source_target_pairs={{0,4},{2,6},{4,0},{6,2},{1,5},{3,7},{5,1},{7,3},{8,12},{10,14},{12... | collective-permute-start | bytes 1572872 | tf_op jit(solution)/shard_map/cond/branch_1_fun/ppermute | solution.py:142
  44.2 23.9 %collective-permute-start.3 = (bf16[512,512]{1,0:T(8,128)(2,1)S(1)}, bf16[512,512]{1,0:T(8,128)(2,1)}, u32[]{:S(2)}, u32[]{:S(2)}) collective-permute-start(bf16[512,512]{1,0:T(8,128)(2,1)S(1)} %param.1), channel_id=1, source_target_pairs={{0,6},{2,4},{4,2},{6,0},{1,7},{3,5},{5,3},{7,1},{8,14},{10,12},{12... | collective-permute-start | bytes 1572872 | tf_op jit(solution)/shard_map/cond/branch_1_fun/ppermute | solution.py:142
  47.0 23.5 %collective-permute-start.1 = (bf16[512,512]{1,0:T(8,128)(2,1)S(1)}, bf16[512,512]{1,0:T(8,128)(2,1)}, u32[]{:S(2)}, u32[]{:S(2)}) collective-permute-start(bf16[512,512]{1,0:T(8,128)(2,1)S(1)} %param.1), channel_id=1, source_target_pairs={{0,2},{2,0},{4,6},{6,4},{1,3},{3,1},{5,7},{7,5},{8,10},{10,8},{12,... | collective-permute-start | bytes 1572872 | tf_op jit(solution)/shard_map/cond/branch_1_fun/ppermute | solution.py:142
  56.6 15.9 %collective-permute-start.5 = (bf16[512,512]{1,0:T(8,128)(2,1)}, bf16[512,512]{1,0:T(8,128)(2,1)}, u32[]{:S(2)}, u32[]{:S(2)}) collective-permute-start(bf16[512,512]{1,0:T(8,128)(2,1)} %collective-permute-done.2), channel_id=1, source_target_pairs={{0,1},{1,0},{2,3},{3,2},{4,5},{5,4},{6,7},{7,6},{8,9},{9,8},{10,11... | collective-permute-start | bytes 1572872 | tf_op jit(solution)/shard_map/cond/branch_1_fun/ppermute | solution.py:145
  68.2 4.4 %collective-permute-start.6 = (bf16[512,512]{1,0:T(8,128)(2,1)}, bf16[512,512]{1,0:T(8,128)(2,1)}, u32[]{:S(2)}, u32[]{:S(2)}) collective-permute-start(bf16[512,512]{1,0:T(8,128)(2,1)} %collective-permute-done.3), channel_id=1, source_target_pairs={{0,1},{1,0},{2,3},{3,2},{4,5},{5,4},{6,7},{7,6},{8,9},{9,8},{10,11... | collective-permute-start | bytes 1572872 | tf_op jit(solution)/shard_map/cond/branch_1_fun/ppermute | solution.py:145
  70.5 4.1 %collective-permute-start.4 = (bf16[512,512]{1,0:T(8,128)(2,1)}, bf16[512,512]{1,0:T(8,128)(2,1)}, u32[]{:S(2)}, u32[]{:S(2)}) collective-permute-start(bf16[512,512]{1,0:T(8,128)(2,1)} %collective-permute-done.1), channel_id=1, source_target_pairs={{0,1},{1,0},{2,3},{3,2},{4,5},{5,4},{6,7},{7,6},{8,9},{9,8},{10,11... | collective-permute-start | bytes 1572872 | tf_op jit(solution)/shard_map/cond/branch_1_fun/ppermute | solution.py:145
  100.1 27.1 %all-to-all-start.1 = ((f32[16,1,32]{2,1,0:T(1,128)}), f32[16,1,32]{2,1,0:T(1,128)S(1)}, u32[]{:S(2)}, u32[]{:S(2)}) async-start(f32[16,1,32]{2,1,0:T(1,128)} %broadcast_in_dim.48), calls=%async_computation.1 | async-start | bytes 16384 | tf_op jit(solution)/shard_map/all_to_all | solution.py:198
